TPU v7x, 256 devices: a whole 4x4x8 slice. The times are simulated.
256 devices in a mesh: pix: 16 (over y_lo, x, core), ion: 16 (over y_hi, z).
Axes of the slice: x: 4, y: 4 (y_hi: 2, y_lo: 2; y = y_hi * 2 + y_lo), z: 8, core: 2. Of those that a mesh axis runs over, the one named last changes fastest.
Arguments:
- images: bfloat16 [20480, 32768], P('ion', 'pix')
- stencil: float32 [5, 32768], P(None, 'pix'), may hold values from 0.05 to 0.4
- pairs: int32 [768, 2], P('ion'), may hold values from 0 to 159, as said below
- live: int32 [16], P('ion'), may hold values from 16 to 48, as said below
- rule_of_block: int32 [160], replicated, may hold values from 0 to 63
- adduct: bfloat16 [64, 128, 128], P('ion'), may hold values from -6 to 6
Outputs:
- smoothed: bfloat16 [20480, 32768], P('ion', 'pix')
- scores: bfloat16 [768, 128, 128], P('ion', 'pix')
Inputs may be any that keep to these rules, and one draw needn't show every extreme that they name: Slot s belongs to ion block range of index s // 48 of ion: a lies in that index's own 20480 // (128 * 16) blocks, and |a - b| <= 3. Entries of unused slots are valid pairs too. `live`: some index of ion uses all its slots.
All inputs are finite; a program needn't handle non-finite values.
Results may differ from a plain program's by a relative error of at most 0.0053.
Values may be sent and summed in bfloat16 or wider, within the bound.
A program may use at most 192 MiB of HBM per device.

v0:
```python
import jax
import jax.numpy as jnp
from jax import lax
from jax.sharding import PartitionSpec as P

REACH = 3


slot_group = 16


def extended_2(array, sides, width):
    for axis, dim in sides:
        size, length = (lax.axis_size(axis), array.shape[dim])
        up = [(i, (i + 1) % size) for i in range(size - 1)]
        down = [(j, i) for i, j in up]
        last = lax.slice_in_dim(array, length - width, length, axis=dim)
        first = lax.slice_in_dim(array, 0, width, axis=dim)
        before = lax.ppermute(last, axis, up)
        after = lax.ppermute(first, axis, down)
        array = jnp.concatenate([before, array, after], axis=dim)
    return array


def on_device(images, stencil, pairs, live, rule_of_block, adduct):
    local_rows, pix_local = images.shape
    block = adduct.shape[1]
    local_blocks = local_rows // block
    padded = extended_2(images, (("pix", 1),), 2)
    total = jnp.zeros((local_rows, pix_local), jnp.float32)
    for tap in range(5):
        total = total + stencil[tap][None, :] * padded[:, tap : tap + pix_local].astype(jnp.float32)
    smoothed = total.astype(jnp.bfloat16)
    extended = extended_2(smoothed, (("ion", 0),), REACH * block)
    values = extended.astype(jnp.float32)
    squares = jnp.sum(values * values, axis=1)
    pixel_count = pix_local * lax.axis_size("pix")
    energy = lax.psum(squares, "pix") / pixel_count
    inverse = 1.0 / jnp.sqrt(energy + 1e-06)
    lookup_tables = lax.all_gather(adduct, "ion", axis=0, tiled=True)
    first = lax.axis_index("ion") * local_blocks
    ext_blocks = extended.reshape(local_blocks + 2 * REACH, block, pix_local)
    inv_blocks = inverse.reshape(local_blocks + 2 * REACH, block)
    slots = pairs.shape[0]
    relative = pairs - first + REACH

    def group_gram(start):
        chosen = lax.dynamic_slice_in_dim(relative, start, slot_group, 0)
        left_operand = jnp.take(ext_blocks, chosen[:, 0], axis=0)
        right_operand = jnp.take(ext_blocks, chosen[:, 1], axis=0)
        return jnp.einsum(
            "uwf,uvf->uwv", left_operand, right_operand, preferred_element_type=jnp.float32
        )

    grams = jnp.concatenate(
        [group_gram(step * slot_group) for step in range(slots // slot_group)], axis=0
    )
    inv_left = jnp.take(inv_blocks, relative[:, 0], axis=0)
    inv_right = jnp.take(inv_blocks, relative[:, 1], axis=0)
    rules = jnp.take(rule_of_block, pairs[:, 1], axis=0)
    matrices = jnp.take(lookup_tables, rules, axis=0)
    share = block // lax.axis_size("pix")
    offset = lax.axis_index("pix") * share
    gram = lax.psum(grams, "pix")
    coloc = (gram * inv_left[:, :, None] * inv_right[:, None, :] / pixel_count).astype(jnp.bfloat16)
    complete_scores = jnp.einsum(
        "src,scd->srd", coloc, matrices, preferred_element_type=jnp.float32
    )
    scores = lax.dynamic_slice_in_dim(complete_scores, offset, share, 1)
    used = jnp.arange(slots, dtype=jnp.int32) < live[0]
    scores = jnp.where(used[:, None, None], scores, 0.0).astype(jnp.bfloat16)
    return (smoothed, scores)


def solution(mesh):
    return jax.shard_map(
        on_device,
        mesh=mesh,
        in_specs=(
            P("ion", "pix"),
            P(None, "pix"),
            P("ion", None),
            P("ion"),
            P(),
            P("ion", None, None),
        ),
        out_specs=(P("ion", "pix"), P("ion", "pix", None)),
        check_vma=False,
    )
```

profile of v0, /device:TPU:16, one launch (start us, length us, event | category | flops | bytes accessed | tf_op | source)
XLA Modules:
  0.0 306.2 jit_solution(16997683368433207593)
XLA Ops:
  8.0 0.0 copy-start
  8.0 0.0 slice-start
  8.0 0.0 copy-start.2
  8.0 0.0 all-gather.2.cloned.1.call-start
  8.1 1.3 fusion.33
  9.4 1.3 collective-permute-start.1
  10.7 0.0 slice-start.1
  10.7 3.3 %collective-permute-start = (bf16[1280,2]{1,0:T(8,128)(2,1)S(1)}, bf16[1280,2]{1,0:T(8,128)(2,1)S(1)}, u32[]{:S(2)}, u32[]{:S(2)}) collective-permute-start(bf16[1280,2]{1,0:T(8,128)(2,1)S(1)} %get-tuple-element.27), channel_id=1, source_target_pairs={{0,16},{16,32},{32,48},{48,64},{64,80},{80,96},{96,112},{112,128},... | collective-permute-start | bytes 15368 | tf_op jit(solution)/shard_map/ppermute | solution.py:19
  14.0 3.0 constant_dynamic-update-slice_fusion.1
  17.1 0.0 copy-done.2
  17.1 0.0 collective-permute-done.1
  17.1 0.1 constant_dynamic-update-slice_fusion
  17.2 0.0 collective-permute-done
  17.2 0.0 slice-done
  17.2 0.0 slice-done.1
  17.2 0.0 copy-start.3
  17.3 8.8 %add_convert_fusion = bf16[1280,2048]{1,0:T(8,128)(2,1)S(1)} fusion(bf16[1280,2048]{1,0:T(8,128)(2,1)S(1)} %bitcast.51, bf16[1280,2]{1,0:T(8,128)(2,1)S(1)} %collective-permute-done, bf16[1280,2050]{1,0:T(8,128)(2,1)S(1)} %constant_dynamic-update-slice_fusion, f32[2048]{0:T(1024)S(1)} %bitcast.55, f32[2048]{0:T(1024)S(1)} %bitcast.56, f32[2048]{0:T(1024)S(1)} %bitcast.53, ...), kind=kLoop, calls=%fused_computation.11 | loop fusion | flops 55050240 | bytes 21017600 | tf_op jit(solution)/shard_map/convert_element_type | solution.py:33
  26.1 0.0 copy-start.1
  26.1 2.3 copy-done.1
  28.5 0.4 fusion.32
  28.9 3.8 %collective-permute-start.2 = (bf16[384,2048]{1,0:T(8,128)(2,1)S(1)}, bf16[384,2048]{1,0:T(8,128)(2,1)}, u32[]{:S(2)}, u32[]{:S(2)}) collective-permute-start(bf16[384,2048]{1,0:T(8,128)(2,1)S(1)} %get-tuple-element.24), channel_id=1, source_target_pairs={{0,1},{1,2},{2,3},{3,4},{4,5},{5,6},{6,7},{7,8},{8,9},{9,10},{10,1... | collective-permute-start | bytes 4718600 | tf_op jit(solution)/shard_map/ppermute | solution.py:19
  32.7 5.6 %collective-permute-start.3 = (bf16[384,2048]{1,0:T(8,128)(2,1)S(1)}, bf16[384,2048]{1,0:T(8,128)(2,1)}, u32[]{:S(2)}, u32[]{:S(2)}) collective-permute-start(bf16[384,2048]{1,0:T(8,128)(2,1)S(1)} %get-tuple-element.25), channel_id=1, source_target_pairs={{1,0},{2,1},{3,2},{4,3},{5,4},{6,5},{7,6},{8,7},{9,8},{10,9},{11,1... | collective-permute-start | bytes 4718600 | tf_op jit(solution)/shard_map/ppermute | solution.py:20
  38.3 0.0 all-gather.2.cloned.1.call-update
  38.4 0.2 all-reduce.2.cloned.1.call-start
  38.6 0.0 copy-done.3
  38.6 0.1 compare_and_fusion.7
  38.7 32.8 %collective-permute-done.2 = bf16[384,2048]{1,0:T(8,128)(2,1)} collective-permute-done((bf16[384,2048]{1,0:T(8,128)(2,1)S(1)}, bf16[384,2048]{1,0:T(8,128)(2,1)}, u32[]{:S(2)}, u32[]{:S(2)}) %collective-permute-start.2) | collective-permute-done | bytes 1572896 | tf_op jit(solution)/shard_map/ppermute | solution.py:19
  71.6 1.9 collective-permute-done.3
  73.4 7.5 %multiply_reduce_fusion = (f32[2048]{0:T(1024)S(1)}, bf16[2048,2048]{1,0:T(8,128)(2,1)}) fusion(bf16[384,2048]{1,0:T(8,128)(2,1)} %collective-permute-done.3, bf16[1280,2048]{1,0:T(8,128)(2,1)} %copy-done.1, bf16[384,2048]{1,0:T(8,128)(2,1)} %collective-permute-done.2), kind=kLoop, calls=%fused_computation.10 | loop fusion | flops 37746688 | bytes 16785408 | tf_op jit(solution)/shard_map/reduce_sum | solution.py:36
  81.0 8.2 %gather_fusion.2 = bf16[16,128,2048]{2,1,0:T(8,128)(2,1)} fusion(bf16[16,128,2048]{2,1,0:T(8,128)(2,1)} %bitcast.44, s32[1024]{0:T(1024)S(1)} %get-tuple-element.50), kind=kCustom, calls=%fused_computation.clone | custom fusion | bytes 16777280 | tf_op jit(solution)/shard_map/jit(_take)/gather | solution.py:49
  89.1 8.1 %gather_fusion.3 = bf16[16,128,2048]{2,1,0:T(8,128)(2,1)} fusion(bf16[16,128,2048]{2,1,0:T(8,128)(2,1)} %bitcast.45, s32[1024]{0:T(1024)S(1)} %get-tuple-element.49), kind=kCustom, calls=%fused_computation.2.clone | custom fusion | bytes 16777280 | tf_op jit(solution)/shard_map/jit(_take)/gather | solution.py:50
  97.3 8.0 %gather_fusion.4 = bf16[16,128,2048]{2,1,0:T(8,128)(2,1)} fusion(bf16[16,128,2048]{2,1,0:T(8,128)(2,1)} %bitcast.46, s32[1024]{0:T(1024)S(1)} %get-tuple-element.48), kind=kCustom, calls=%fused_computation.3.clone | custom fusion | bytes 16777280 | tf_op jit(solution)/shard_map/jit(_take)/gather | solution.py:49
  105.3 8.1 %gather_fusion.5 = bf16[16,128,2048]{2,1,0:T(8,128)(2,1)} fusion(bf16[16,128,2048]{2,1,0:T(8,128)(2,1)} %bitcast.47, s32[1024]{0:T(1024)S(1)} %get-tuple-element.47), kind=kCustom, calls=%fused_computation.4.clone | custom fusion | bytes 16777280 | tf_op jit(solution)/shard_map/jit(_take)/gather | solution.py:50
  113.4 8.1 %gather_fusion.6 = bf16[16,128,2048]{2,1,0:T(8,128)(2,1)} fusion(bf16[16,128,2048]{2,1,0:T(8,128)(2,1)} %bitcast.48, s32[1024]{0:T(1024)S(1)} %get-tuple-element.46), kind=kCustom, calls=%fused_computation.5.clone | custom fusion | bytes 16777280 | tf_op jit(solution)/shard_map/jit(_take)/gather | solution.py:49
  121.5 8.2 %gather_fusion.7 = bf16[16,128,2048]{2,1,0:T(8,128)(2,1)} fusion(bf16[16,128,2048]{2,1,0:T(8,128)(2,1)} %bitcast.49, s32[1024]{0:T(1024)S(1)} %get-tuple-element.45), kind=kCustom, calls=%fused_computation.6.clone | custom fusion | bytes 16777280 | tf_op jit(solution)/shard_map/jit(_take)/gather | solution.py:50
  129.8 8.4 %fusion.6 = f32[16,128,128]{2,1,0:T(8,128)S(1)} fusion(bf16[16,128,2048]{2,1,0:T(8,128)(2,1)} %gather_fusion.3, bf16[16,128,2048]{2,1,0:T(8,128)(2,1)} %gather_fusion.2, pred[16]{0:T(512)(128)(4,1)S(1)} %get-tuple-element.43, pred[16]{0:T(512)(128)(4,1)S(1)} %get-tuple-element.12), kind=kOutput, calls=%fused_computation.19 | convolution fusion | flops 1082130432 | bytes 17825824 | tf_op jit(solution)/shard_map/uwf,uvf->uwv/dot_general | solution.py:51
  138.2 8.4 %fusion.3 = f32[16,128,128]{2,1,0:T(8,128)S(1)} fusion(bf16[16,128,2048]{2,1,0:T(8,128)(2,1)} %gather_fusion.5, bf16[16,128,2048]{2,1,0:T(8,128)(2,1)} %gather_fusion.4, pred[16]{0:T(512)(128)(4,1)S(1)} %get-tuple-element.39, pred[16]{0:T(512)(128)(4,1)S(1)} %get-tuple-element.41), kind=kOutput, calls=%fused_computation.16 | convolution fusion | flops 1082130432 | bytes 17825824 | tf_op jit(solution)/shard_map/uwf,uvf->uwv/dot_general | solution.py:51
  146.6 8.4 %fusion = f32[16,128,128]{2,1,0:T(8,128)S(1)} fusion(bf16[16,128,2048]{2,1,0:T(8,128)(2,1)} %gather_fusion.7, bf16[16,128,2048]{2,1,0:T(8,128)(2,1)} %gather_fusion.6, pred[16]{0:T(512)(128)(4,1)S(1)} %get-tuple-element.35, pred[16]{0:T(512)(128)(4,1)S(1)} %get-tuple-element.37), kind=kOutput, calls=%fused_computation.13 | convolution fusion | flops 1082130432 | bytes 17825824 | tf_op jit(solution)/shard_map/uwf,uvf->uwv/dot_general | solution.py:51
  155.0 2.0 pad_maximum_fusion.2
  157.0 0.0 all-reduce.2.cloned.1.call-update
  157.7 0.0 copy-done
  157.7 0.8 gather_fusion
  158.6 29.2 %psum.15 = f32[2048]{0:T(1024)S(1)} all-reduce(f32[2048]{0:T(1024)S(1)} %get-tuple-element.10), channel_id=1, replica_groups=mesh['pix'=16,'ion'=16] {'pix'}, use_global_device_ids=true, to_apply=%region_2.0 | all-reduce | flops 2048 | bytes 16384 | tf_op jit(solution)/shard_map/psum | solution.py:38
  187.8 0.6 gather_fusion.9
  188.4 0.6 gather_fusion.8
  189.0 0.1 broadcast_select_fusion
  189.1 0.1 broadcast_select_fusion.1
  189.1 0.0 all-gather.2.cloned.1.call-done
  189.1 2.5 gather_fusion.1
  191.6 103.4 %all-reduce.2.cloned.1.call-done = f32[48,128,128]{2,1,0:T(8,128)} async-done(((f32[48,128,128]{2,1,0:T(8,128)}), f32[48,128,128]{2,1,0:T(8,128)}) %all-reduce.2.cloned.1.call-update) | async-done | bytes 3145744 | tf_op jit(solution)/shard_map/psum | solution.py:64
  295.0 3.0 fusion.19
  298.0 0.8 select_convert_fusion
  (14 shorter events, 0.1 us)
Async XLA Ops:
  8.0 149.7 %copy-start = (s32[160]{0:T(256)S(1)}, s32[160]{0:T(256)}, u32[]{:S(2)}) copy-start(s32[160]{0:T(256)} %param.14) | copy-start | bytes 1924
  8.0 9.2 %slice-start = ((s8[5242880]{0:T(1024)(128)(4,1)}), s8[1048576]{0:T(1024)(128)(4,1)S(1)}, s32[]{:S(2)}) async-start(s8[5242880]{0:T(1024)(128)(4,1)} %bitcast.50), calls=%async_computation.2 | async-start | bytes 2097152
  8.0 9.0 %copy-start.2 = (f32[5,2048]{1,0:T(8,128)S(1)}, f32[5,2048]{1,0:T(8,128)}, u32[]{:S(2)}) copy-start(f32[5,2048]{1,0:T(8,128)} %param.11) | copy-start | bytes 122884
  8.0 181.1 %all-gather.2.cloned.1.call-start = ((), (), s32[]{:S(2)}) async-start(), calls=%async_computation.1 | async-start | bytes 2228224 | tf_op jit(solution)/shard_map/all_gather | solution.py:40
  9.4 7.7 %collective-permute-start.1 = (bf16[1280,2]{1,0:T(8,128)(2,1)S(1)}, bf16[1280,2]{1,0:T(8,128)(2,1)S(1)}, u32[]{:S(2)}, u32[]{:S(2)}) collective-permute-start(bf16[1280,2]{1,0:T(8,128)(2,1)S(1)} %get-tuple-element.26), channel_id=1, source_target_pairs={{16,0},{32,16},{48,32},{64,48},{80,64},{96,80},{112,96},{128,112},... | collective-permute-start | bytes 15368 | tf_op jit(solution)/shard_map/ppermute | solution.py:20
  10.7 6.5 %slice-start.1 = ((s8[5242880]{0:T(1024)(128)(4,1)}), s8[4194304]{0:T(1024)(128)(4,1)S(1)}, s32[]{:S(2)}) async-start(s8[5242880]{0:T(1024)(128)(4,1)} %bitcast.50), calls=%async_computation.3 | async-start | bytes 8388608
  10.7 6.5 %collective-permute-start = (bf16[1280,2]{1,0:T(8,128)(2,1)S(1)}, bf16[1280,2]{1,0:T(8,128)(2,1)S(1)}, u32[]{:S(2)}, u32[]{:S(2)}) collective-permute-start(bf16[1280,2]{1,0:T(8,128)(2,1)S(1)} %get-tuple-element.27), channel_id=1, source_target_pairs={{0,16},{16,32},{32,48},{48,64},{64,80},{80,96},{96,112},{112,128},... | collective-permute-start | bytes 15368 | tf_op jit(solution)/shard_map/ppermute | solution.py:19
  17.2 21.4 %copy-start.3 = (s32[48,2]{0,1:T(2,128)S(1)}, s32[48,2]{0,1:T(2,128)}, u32[]{:S(2)}) copy-start(s32[48,2]{0,1:T(2,128)} %param.12) | copy-start | bytes 1156
  26.1 2.4 copy-start.1
  28.9 42.7 %collective-permute-start.2 = (bf16[384,2048]{1,0:T(8,128)(2,1)S(1)}, bf16[384,2048]{1,0:T(8,128)(2,1)}, u32[]{:S(2)}, u32[]{:S(2)}) collective-permute-start(bf16[384,2048]{1,0:T(8,128)(2,1)S(1)} %get-tuple-element.24), channel_id=1, source_target_pairs={{0,1},{1,2},{2,3},{3,4},{4,5},{5,6},{6,7},{7,8},{8,9},{9,10},{10,1... | collective-permute-start | bytes 4718600 | tf_op jit(solution)/shard_map/ppermute | solution.py:19
  32.7 40.7 %collective-permute-start.3 = (bf16[384,2048]{1,0:T(8,128)(2,1)S(1)}, bf16[384,2048]{1,0:T(8,128)(2,1)}, u32[]{:S(2)}, u32[]{:S(2)}) collective-permute-start(bf16[384,2048]{1,0:T(8,128)(2,1)S(1)} %get-tuple-element.25), channel_id=1, source_target_pairs={{1,0},{2,1},{3,2},{4,3},{5,4},{6,5},{7,6},{8,7},{9,8},{10,9},{11,1... | collective-permute-start | bytes 4718600 | tf_op jit(solution)/shard_map/ppermute | solution.py:20
  38.4 256.7 %all-reduce.2.cloned.1.call-start = ((), (), s32[]{:S(2)}) async-start(), calls=%async_computation | async-start | bytes 6291456 | tf_op jit(solution)/shard_map/psum | solution.py:64
Sparse Core Ops, SparseCore 0:
  38.5 104.1 all-gather.1
Sparse Core Ops, SparseCore 1:
  157.1 137.9 all-reduce.1
where the time goes:
time: 308 us; the launch traced here: 306 us
  waiting for transfers between devices  138 us (45%)
  local copies, waits for them, and re-layouts  60.5 us (20%)
  blocking collectives  29.2 us (9%)
  matrix products  28.2 us (9%)
  other arithmetic  19.5 us (6%)
  between operations  16.4 us (5%)
  starting transfers between devices  14.3 us (5%)
    psum x1, waiting for transfers between devices, on_device(): gram = lax.psum(grams, 'pix')  103 us
    ppermute x2, waiting for transfers between devices, extended_2(): before = lax.ppermute(last, axis, up)  32.8 us
    psum x1, blocking collectives, on_device(): energy = lax.psum(squares, 'pix') / pixel_count  29.2 us
    dot_general x3, matrix products, group_gram(): jnp.einsum('uwf,uvf->uwv', left_operand, right_operand, preferred_element...  25.2 us
    gather x3, local copies, waits for them, and re-layouts, group_gram(): right_operand = jnp.take(ext_blocks, chosen[:, 1], axis=0)  24.5 us
    gather x3, local copies, waits for them, and re-layouts, group_gram(): left_operand = jnp.take(ext_blocks, chosen[:, 0], axis=0)  24.3 us
    convert_element_type x1, other arithmetic, on_device(): smoothed = total.astype(jnp.bfloat16)  8.83 us
    reduce_sum x1, other arithmetic, on_device(): squares = jnp.sum(values * values, axis=1)  7.52 us
  transfers between devices with their start and end apart: 6, of which 3 were waited for; matrix products, arithmetic and copies ran while one was open for 30% of the time, Pallas kernels for 0%

commit v1 on v0

v1 whole, which is shorter than its diff:
```python
import jax
import jax.numpy as jnp
from jax import lax
from jax.experimental import pallas as pl
from jax.experimental.pallas import tpu as pltpu
from jax.sharding import PartitionSpec as P

REACH = 3


def extended_2(array, sides, width):
    for axis, dim in sides:
        size, length = (lax.axis_size(axis), array.shape[dim])
        up = [(i, (i + 1) % size) for i in range(size - 1)]
        down = [(j, i) for i, j in up]
        last = lax.slice_in_dim(array, length - width, length, axis=dim)
        first = lax.slice_in_dim(array, 0, width, axis=dim)
        before = lax.ppermute(last, axis, up)
        after = lax.ppermute(first, axis, down)
        array = jnp.concatenate([before, array, after], axis=dim)
    return array


def gram_kernel(shares, rel_ref, ext_ref, out_ref):
    block = out_ref.shape[3]
    slots = out_ref.shape[1]
    rows = out_ref.shape[2]

    def body(s, carry):
        ra = rel_ref[2 * s]
        rb = rel_ref[2 * s + 1]
        left = ext_ref[pl.ds(pl.multiple_of(ra * block, block), block), :]
        right = ext_ref[pl.ds(pl.multiple_of(rb * block, block), block), :]
        g = lax.dot_general(
            left, right, (((1,), (1,)), ((), ())), preferred_element_type=jnp.float32
        )
        for q in range(shares):
            out_ref[q, s] = g[q * rows : (q + 1) * rows, :]
        return carry

    lax.fori_loop(0, slots, body, 0)


def pair_grams(relative, extended, shares, block):
    slots = relative.shape[0]
    rows = block // shares
    pix_local = extended.shape[1]
    flat = relative.reshape(-1).astype(jnp.int32)
    return pl.pallas_call(
        lambda *refs: gram_kernel(shares, *refs),
        out_shape=jax.ShapeDtypeStruct((shares, slots, rows, block), jnp.float32),
        in_specs=[
            pl.BlockSpec(memory_space=pltpu.SMEM),
            pl.BlockSpec(memory_space=pltpu.VMEM),
        ],
        out_specs=pl.BlockSpec(memory_space=pltpu.VMEM),
        compiler_params=pltpu.CompilerParams(vmem_limit_bytes=48 * 1024 * 1024),
        cost_estimate=pl.CostEstimate(
            flops=2 * slots * block * block * pix_local,
            transcendentals=0,
            bytes_accessed=extended.size * 2 + slots * block * block * 4,
        ),
    )(flat, extended)


def on_device(images, stencil, pairs, live, rule_of_block, adduct):
    local_rows, pix_local = images.shape
    block = adduct.shape[1]
    local_blocks = local_rows // block
    shares = lax.axis_size("pix")
    rows = block // shares
    padded = extended_2(images, (("pix", 1),), 2)
    total = jnp.zeros((local_rows, pix_local), jnp.float32)
    for tap in range(5):
        total = total + stencil[tap][None, :] * padded[:, tap : tap + pix_local].astype(jnp.float32)
    smoothed = total.astype(jnp.bfloat16)
    extended = extended_2(smoothed, (("ion", 0),), REACH * block)
    values = extended.astype(jnp.float32)
    squares = jnp.sum(values * values, axis=1)
    pixel_count = pix_local * shares
    energy = lax.psum(squares, "pix") / pixel_count
    inverse = 1.0 / jnp.sqrt(energy + 1e-06)
    lookup_tables = lax.all_gather(adduct, "ion", axis=0, tiled=True)
    first = lax.axis_index("ion") * local_blocks
    inv_blocks = inverse.reshape(local_blocks + 2 * REACH, block)
    slots = pairs.shape[0]
    relative = pairs - first + REACH

    grams = pair_grams(relative, extended, shares, block)
    gram = lax.psum_scatter(grams, "pix", scatter_dimension=0, tiled=True)[0]

    offset = lax.axis_index("pix") * rows
    inv_left = lax.dynamic_slice_in_dim(
        jnp.take(inv_blocks, relative[:, 0], axis=0), offset, rows, 1
    )
    inv_right = jnp.take(inv_blocks, relative[:, 1], axis=0)
    rules = jnp.take(rule_of_block, pairs[:, 1], axis=0)
    matrices = jnp.take(lookup_tables, rules, axis=0)
    coloc = (gram * inv_left[:, :, None] * inv_right[:, None, :] / pixel_count).astype(jnp.bfloat16)
    scores = jnp.einsum("src,scd->srd", coloc, matrices, preferred_element_type=jnp.float32)
    used = jnp.arange(slots, dtype=jnp.int32) < live[0]
    scores = jnp.where(used[:, None, None], scores, 0.0).astype(jnp.bfloat16)
    return (smoothed, scores)


def solution(mesh):
    return jax.shard_map(
        on_device,
        mesh=mesh,
        in_specs=(
            P("ion", "pix"),
            P(None, "pix"),
            P("ion", None),
            P("ion"),
            P(),
            P("ion", None, None),
        ),
        out_specs=(P("ion", "pix"), P("ion", "pix", None)),
        check_vma=False,
    )
```

time: 308 us -> 194 us (0.63)
  waiting for transfers between devices: 138 us -> 78.1 us
  local copies, waits for them, and re-layouts: 60.5 us -> 11.8 us
  matrix products: 28.2 us -> 2.17 us
  Pallas kernels: 0 us -> 19.7 us
  other arithmetic: 19.5 us -> 22.9 us
    psum x1 -> x0, waiting for transfers between devices: 103 us -> none  [on_device(): gram = lax.psum(grams, 'pix')]
    gather x7 -> x1, local copies, waits for them, and re-layouts: 49.4 us -> 0.59 us  [on_device(): jnp.take(inv_blocks, relative[:, 0], axis=0)]
    reduce_scatter x0 -> x1, waiting for transfers between devices: none -> 40 us  [on_device(): gram = lax.psum_scatter(grams, 'pix', scatter_dimension=0, tiled=True)[0]]
    dot_general x3 -> x0, matrix products: 25.2 us -> none  [group_gram(): jnp.einsum('uwf,uvf->uwv', left_operand, right_operand, preferred_element...]
    pallas_call x0 -> x1, Pallas kernels: none -> 19.7 us  [pair_grams(): pl.pallas_call(lambda *refs: gram_kernel(shares, *refs), out_shape=jax.Sh...]
    convert_element_type x1, other arithmetic: 8.83 us -> 15.2 us  [on_device(): smoothed = total.astype(jnp.bfloat16)]
    ppermute x2, waiting for transfers between devices: 32.8 us -> 37.2 us  [extended_2(): before = lax.ppermute(last, axis, up)]
  transfers between devices with their start and end apart: 6 -> 6, of which waited for: 3 -> 3; matrix products, arithmetic and copies ran while one was open for 30% -> 16% of each run, Pallas kernels for 0% -> 10%
where the time goes in v1:
time: 194 us
  waiting for transfers between devices  78.1 us (40%)
  blocking collectives  28.6 us (15%)
  other arithmetic  22.9 us (12%)
  Pallas kernels  19.7 us (10%)
  between operations  16.3 us (8%)
  starting transfers between devices  14 us (7%)
  local copies, waits for them, and re-layouts  11.8 us (6%)
  matrix products  2.17 us (1%)
    reduce_scatter x1, waiting for transfers between devices, on_device(): gram = lax.psum_scatter(grams, 'pix', scatter_dimension=0, tiled=True)[0]  40 us
    ppermute x2, waiting for transfers between devices, extended_2(): before = lax.ppermute(last, axis, up)  37.2 us
    psum x1, blocking collectives, on_device(): energy = lax.psum(squares, 'pix') / pixel_count  28.6 us
    pallas_call x1, Pallas kernels, pair_grams(): pl.pallas_call(lambda *refs: gram_kernel(shares, *refs), out_shape=jax.Sh...  19.7 us
    convert_element_type x1, other arithmetic, on_device(): smoothed = total.astype(jnp.bfloat16)  15.2 us
    reduce_sum x1, other arithmetic, on_device(): squares = jnp.sum(values * values, axis=1)  7.47 us
    ppermute x2, starting transfers between devices, extended_2(): after = lax.ppermute(first, axis, down)  7.06 us
    ppermute x2, starting transfers between devices, extended_2(): before = lax.ppermute(last, axis, up)  6.88 us
  transfers between devices with their start and end apart: 6, of which 3 were waited for; matrix products, arithmetic and copies ran while one was open for 16% of the time, Pallas kernels for 10%

profile of v1, /device:TPU:16, one launch (start us, length us, event | category | flops | bytes accessed | tf_op | source)
XLA Modules:
  0.0 193.6 jit_solution(18164482910688863519)
XLA Ops:
  8.0 0.0 copy-start
  8.0 0.0 all-gather.2.cloned.1.call-start
  8.1 1.2 fusion.22
  9.3 0.0 copy-start.2
  9.3 1.4 collective-permute-start.1
  10.7 3.1 %collective-permute-start = (bf16[1280,2]{1,0:T(8,128)(2,1)S(1)}, bf16[1280,2]{1,0:T(8,128)(2,1)S(1)}, u32[]{:S(2)}, u32[]{:S(2)}) collective-permute-start(bf16[1280,2]{1,0:T(8,128)(2,1)S(1)} %get-tuple-element.14), channel_id=1, source_target_pairs={{0,16},{16,32},{32,48},{48,64},{64,80},{80,96},{96,112},{112,128},... | collective-permute-start | bytes 15368 | tf_op jit(solution)/shard_map/ppermute | solution.py:18
  13.8 0.0 all-gather.2.cloned.1.call-update
  13.8 0.0 reduce-scatter.2.cloned.1.call-start
  13.9 3.0 %constant_dynamic-update-slice_fusion.1 = bf16[1280,2050]{1,0:T(8,128)(2,1)S(1)} fusion(bf16[1280,2048]{1,0:T(8,128)(2,1)} %param.8), kind=kLoop, calls=%fused_computation.32 | loop fusion | bytes 10485760
  16.9 0.0 copy-done.2
  16.9 0.0 collective-permute-done.1
  17.0 0.1 constant_dynamic-update-slice_fusion
  17.0 0.0 collective-permute-done
  17.1 15.2 %add_convert_fusion = bf16[1280,2048]{1,0:T(8,128)(2,1)S(1)} fusion(bf16[1280,2048]{1,0:T(8,128)(2,1)} %param.8, bf16[1280,2]{1,0:T(8,128)(2,1)S(1)} %collective-permute-done, bf16[1280,2050]{1,0:T(8,128)(2,1)S(1)} %constant_dynamic-update-slice_fusion, f32[2048]{0:T(1024)S(1)} %bitcast.37, f32[2048]{0:T(1024)S(1)} %bitcast.38, f32[2048]{0:T(1024)S(1)} %bitcast.35, ...), kind=kLoop, calls=%fused_computation.5 | loop fusion | flops 55050240 | bytes 21017600 | tf_op jit(solution)/shard_map/convert_element_type | solution.py:76
  32.3 0.0 copy-start.1
  32.3 2.3 %copy-done.1 = bf16[1280,2048]{1,0:T(8,128)(2,1)} copy-done((bf16[1280,2048]{1,0:T(8,128)(2,1)}, bf16[1280,2048]{1,0:T(8,128)(2,1)S(1)}, u32[]{:S(2)}) %copy-start.1) | copy-done | bytes 5242904
  34.6 0.0 copy-start.3
  34.6 0.4 fusion.21
  35.0 3.8 %collective-permute-start.2 = (bf16[384,2048]{1,0:T(8,128)(2,1)S(1)}, bf16[384,2048]{1,0:T(8,128)(2,1)}, u32[]{:S(2)}, u32[]{:S(2)}) collective-permute-start(bf16[384,2048]{1,0:T(8,128)(2,1)S(1)} %get-tuple-element.11), channel_id=1, source_target_pairs={{0,1},{1,2},{2,3},{3,4},{4,5},{5,6},{6,7},{7,8},{8,9},{9,10},{10,1... | collective-permute-start | bytes 4718600 | tf_op jit(solution)/shard_map/ppermute | solution.py:18
  38.9 5.6 %collective-permute-start.3 = (bf16[384,2048]{1,0:T(8,128)(2,1)S(1)}, bf16[384,2048]{1,0:T(8,128)(2,1)}, u32[]{:S(2)}, u32[]{:S(2)}) collective-permute-start(bf16[384,2048]{1,0:T(8,128)(2,1)S(1)} %get-tuple-element.12), channel_id=1, source_target_pairs={{1,0},{2,1},{3,2},{4,3},{5,4},{6,5},{7,6},{8,7},{9,8},{10,9},{11,1... | collective-permute-start | bytes 4718600 | tf_op jit(solution)/shard_map/ppermute | solution.py:19
  44.5 0.0 copy-done.3
  44.5 0.1 copy.10
  44.6 0.1 reshape.31.refs_0_
  44.7 37.2 %collective-permute-done.2 = bf16[384,2048]{1,0:T(8,128)(2,1)} collective-permute-done((bf16[384,2048]{1,0:T(8,128)(2,1)S(1)}, bf16[384,2048]{1,0:T(8,128)(2,1)}, u32[]{:S(2)}, u32[]{:S(2)}) %collective-permute-start.2) | collective-permute-done | bytes 1572896 | tf_op jit(solution)/shard_map/ppermute | solution.py:18
  82.0 0.9 collective-permute-done.3
  82.8 7.5 %multiply_reduce_fusion = (f32[2048]{0:T(1024)S(1)}, bf16[2048,2048]{1,0:T(8,128)(2,1)}) fusion(bf16[384,2048]{1,0:T(8,128)(2,1)} %collective-permute-done.3, bf16[1280,2048]{1,0:T(8,128)(2,1)} %copy-done.1, bf16[384,2048]{1,0:T(8,128)(2,1)} %collective-permute-done.2), kind=kLoop, calls=%fused_computation.4 | loop fusion | flops 37746688 | bytes 16785408 | tf_op jit(solution)/shard_map/reduce_sum | solution.py:79
  90.3 19.7 %shard_map.77 = f32[16,48,8,128]{3,2,1,0:T(8,128)} custom-call(s32[96]{0:T(128)S(1)} %reshape.31.refs_0_, bf16[2048,2048]{1,0:T(8,128)(2,1)} %get-tuple-element.8.refs_1_), custom_call_target="tpu_custom_call" | custom-call | flops 3221225472 | bytes 11534336 | tf_op jit(solution)/shard_map/pallas_call | solution.py:49
  110.0 0.0 reduce-scatter.2.cloned.1.call-update
  110.7 0.0 copy-done
  110.7 0.8 gather_fusion
  111.5 28.6 %psum.7 = f32[2048]{0:T(1024)S(1)} all-reduce(f32[2048]{0:T(1024)S(1)} %get-tuple-element.7), channel_id=1, replica_groups=mesh['pix'=16,'ion'=16] {'pix'}, use_global_device_ids=true, to_apply=%region_2.0 | all-reduce | flops 2048 | bytes 16384 | tf_op jit(solution)/shard_map/psum | solution.py:81
  140.1 0.6 gather_fusion.2
  140.7 0.6 gather_fusion.3
  141.3 0.1 dynamic-slice_select_fusion
  141.4 0.1 broadcast_select_fusion
  141.5 0.0 all-gather.2.cloned.1.call-done
  141.5 2.5 %gather_fusion.1 = bf16[48,128,128]{2,1,0:T(8,128)(2,1)S(1)} fusion(bf16[64,128,128]{2,1,0:T(8,128)(2,1)} %all-gather.2.cloned.1.call-done, s32[1024]{0:T(1024)S(1)} %pad_clamp_fusion), kind=kCustom, calls=%fused_computation.3 | custom fusion | bytes 3145920 | tf_op jit(solution)/shard_map/jit(_take)/gather | solution.py:98
  143.9 40.0 %reduce-scatter.2.cloned.1.call-done = f32[1,48,8,128]{3,2,1,0:T(8,128)} async-done(((f32[16,48,8,128]{3,2,1,0:T(8,128)}), f32[1,48,8,128]{3,2,1,0:T(8,128)}) %reduce-scatter.2.cloned.1.call-update) | async-done | bytes 196624 | tf_op jit(solution)/shard_map/reduce_scatter | solution.py:90
  183.9 2.2 %fusion.7 = bf16[48,8,128]{2,1,0:T(8,128)(2,1)} fusion(bf16[48,128,128]{2,1,0:T(8,128)(2,1)S(1)} %gather_fusion.1, pred[48]{0:T(512)(128)(4,1)S(1)} %get-tuple-element.9, f32[1,48,8,128]{3,2,1,0:T(8,128)} %reduce-scatter.2.cloned.1.call-done, f32[48,128]{1,0:T(8,128)S(1)} %broadcast_select_fusion, f32[48,8]{1,0:T(8,128)S(1)} %dynamic-slice_select_fusion, ...), kind=kOutput, calls=%fused_computation.15 | convolution fusion | flops 13664256 | bytes 1893984 | tf_op jit(solution)/shard_map/src,scd->srd/dot_general | solution.py:100
  (10 shorter events, 0.1 us)
Async XLA Ops:
  8.0 102.7 %copy-start = (s32[160]{0:T(256)S(1)}, s32[160]{0:T(256)}, u32[]{:S(2)}) copy-start(s32[160]{0:T(256)} %param.12) | copy-start | bytes 1924
  8.0 133.5 %all-gather.2.cloned.1.call-start = ((), (), s32[]{:S(2)}) async-start(), calls=%async_computation.2 | async-start | bytes 2228224 | tf_op jit(solution)/shard_map/all_gather | solution.py:83
  9.3 7.6 %copy-start.2 = (f32[5,2048]{1,0:T(8,128)S(1)}, f32[5,2048]{1,0:T(8,128)}, u32[]{:S(2)}) copy-start(f32[5,2048]{1,0:T(8,128)} %param.9) | copy-start | bytes 122884
  9.3 7.6 %collective-permute-start.1 = (bf16[1280,2]{1,0:T(8,128)(2,1)S(1)}, bf16[1280,2]{1,0:T(8,128)(2,1)S(1)}, u32[]{:S(2)}, u32[]{:S(2)}) collective-permute-start(bf16[1280,2]{1,0:T(8,128)(2,1)S(1)} %get-tuple-element.13), channel_id=1, source_target_pairs={{16,0},{32,16},{48,32},{64,48},{80,64},{96,80},{112,96},{128,112},... | collective-permute-start | bytes 15368 | tf_op jit(solution)/shard_map/ppermute | solution.py:19
  10.7 6.3 %collective-permute-start = (bf16[1280,2]{1,0:T(8,128)(2,1)S(1)}, bf16[1280,2]{1,0:T(8,128)(2,1)S(1)}, u32[]{:S(2)}, u32[]{:S(2)}) collective-permute-start(bf16[1280,2]{1,0:T(8,128)(2,1)S(1)} %get-tuple-element.14), channel_id=1, source_target_pairs={{0,16},{16,32},{32,48},{48,64},{64,80},{80,96},{96,112},{112,128},... | collective-permute-start | bytes 15368 | tf_op jit(solution)/shard_map/ppermute | solution.py:18
  13.8 170.1 %reduce-scatter.2.cloned.1.call-start = ((), (), s32[]{:S(2)}) async-start(), calls=%async_computation.1 | async-start | bytes 3342336 | tf_op jit(solution)/shard_map/reduce_scatter | solution.py:90
  32.3 2.4 %copy-start.1 = (bf16[1280,2048]{1,0:T(8,128)(2,1)}, bf16[1280,2048]{1,0:T(8,128)(2,1)S(1)}, u32[]{:S(2)}) copy-start(bf16[1280,2048]{1,0:T(8,128)(2,1)S(1)} %add_convert_fusion) | copy-start | bytes 15728644
  34.6 9.9 %copy-start.3 = (s32[48,2]{0,1:T(2,128)S(1)}, s32[48,2]{0,1:T(2,128)}, u32[]{:S(2)}) copy-start(s32[48,2]{0,1:T(2,128)} %param.10) | copy-start | bytes 1156
  35.0 47.0 %collective-permute-start.2 = (bf16[384,2048]{1,0:T(8,128)(2,1)S(1)}, bf16[384,2048]{1,0:T(8,128)(2,1)}, u32[]{:S(2)}, u32[]{:S(2)}) collective-permute-start(bf16[384,2048]{1,0:T(8,128)(2,1)S(1)} %get-tuple-element.11), channel_id=1, source_target_pairs={{0,1},{1,2},{2,3},{3,4},{4,5},{5,6},{6,7},{7,8},{8,9},{9,10},{10,1... | collective-permute-start | bytes 4718600 | tf_op jit(solution)/shard_map/ppermute | solution.py:18
  38.9 44.0 %collective-permute-start.3 = (bf16[384,2048]{1,0:T(8,128)(2,1)S(1)}, bf16[384,2048]{1,0:T(8,128)(2,1)}, u32[]{:S(2)}, u32[]{:S(2)}) collective-permute-start(bf16[384,2048]{1,0:T(8,128)(2,1)S(1)} %get-tuple-element.12), channel_id=1, source_target_pairs={{1,0},{2,1},{3,2},{4,3},{5,4},{6,5},{7,6},{8,7},{9,8},{10,9},{11,1... | collective-permute-start | bytes 4718600 | tf_op jit(solution)/shard_map/ppermute | solution.py:19
Sparse Core Ops, SparseCore 0:
  13.9 95.6 all-gather.1
Sparse Core Ops, SparseCore 1:
  110.1 73.8 reduce-scatter.1

commit v2 on v1

--- a/solution.py
+++ b/solution.py
@@ -22,9 +22,9 @@
 
 
 def gram_kernel(shares, rel_ref, ext_ref, out_ref):
-    block = out_ref.shape[3]
-    slots = out_ref.shape[1]
-    rows = out_ref.shape[2]
+    block = out_ref.shape[-1]
+    slots = out_ref.shape[-3]
+    rows = out_ref.shape[-2]
 
     def body(s, carry):
         ra = rel_ref[2 * s]
@@ -35,7 +35,7 @@
             left, right, (((1,), (1,)), ((), ())), preferred_element_type=jnp.float32
         )
         for q in range(shares):
-            out_ref[q, s] = g[q * rows : (q + 1) * rows, :]
+            out_ref[q % 2, (q // 2) % 4, q // 8, s] = g[q * rows : (q + 1) * rows, :]
         return carry
 
     lax.fori_loop(0, slots, body, 0)
@@ -48,7 +48,7 @@
     flat = relative.reshape(-1).astype(jnp.int32)
     return pl.pallas_call(
         lambda *refs: gram_kernel(shares, *refs),
-        out_shape=jax.ShapeDtypeStruct((shares, slots, rows, block), jnp.float32),
+        out_shape=jax.ShapeDtypeStruct((2, 4, 2, slots, rows, block), jnp.float32),
         in_specs=[
             pl.BlockSpec(memory_space=pltpu.SMEM),
             pl.BlockSpec(memory_space=pltpu.VMEM),
@@ -61,6 +61,120 @@
             bytes_accessed=extended.size * 2 + slots * block * block * 4,
         ),
     )(flat, extended)
+
+
+MESH = pl.DeviceIdType.MESH
+
+
+def scatter_kernel(g_ref, e_ref, out_ref, eout_ref, r1, s1, recv_r, recv_l, acc_r, acc_l, tbuf, r3, ebuf, send_sem, recv_sem):
+    p = lax.axis_index("pix")
+    c = p % 2
+    x = (p // 2) % 4
+    yl = p // 8
+    partner = p + 1 - 2 * c
+    right = (yl * 4 + (x + 1) % 4) * 2 + c
+    left = (yl * 4 + (x + 3) % 4) * 2 + c
+    ypart = ((1 - yl) * 4 + x) * 2 + c
+
+    barrier = pltpu.get_barrier_semaphore()
+    for peer in (partner, right, left, ypart):
+        pl.semaphore_signal(barrier, 1, device_id={"pix": peer}, device_id_type=MESH)
+    pl.semaphore_wait(barrier, 4)
+
+    def remote(src, dst, k, peer):
+        return pltpu.make_async_remote_copy(
+            src_ref=src, dst_ref=dst, send_sem=send_sem.at[k], recv_sem=recv_sem.at[k],
+            device_id={"pix": peer}, device_id_type=MESH,
+        )
+
+    c1 = remote(g_ref.at[1 - c], r1, 0, partner)
+    c1.start()
+    ce1 = remote(e_ref, ebuf.at[0], 1, partner)
+    ce1.start()
+    c1.wait()
+    ce1.wait()
+    for j in range(4):
+        s1[j] = g_ref[c, j] + r1[j]
+    ebuf[1] = e_ref[...] + ebuf[0]
+
+    done = []
+    cr = cl = None
+    for k in range(3):
+        jr = (x + 3 - k) % 4
+        jl = (x + k + 1) % 4
+        if k == 0:
+            src_r, src_l = s1.at[jr, 0], s1.at[jl, 1]
+        else:
+            cr.wait_recv()
+            cl.wait_recv()
+            acc_r[k] = s1[jr, 0] + recv_r[k - 1]
+            acc_l[k] = s1[jl, 1] + recv_l[k - 1]
+            src_r, src_l = acc_r.at[k], acc_l.at[k]
+        cr = remote(src_r, recv_r.at[k], 2 + k, right)
+        cr.start()
+        cl = remote(src_l, recv_l.at[k], 5 + k, left)
+        cl.start()
+        done += [cr, cl]
+        if k == 0:
+            er = remote(ebuf.at[1], ebuf.at[2], 8, right)
+            er.start()
+            el = remote(ebuf.at[1], ebuf.at[3], 9, left)
+            el.start()
+            done += [er, el]
+        if k == 1:
+            er.wait_recv()
+            ef = remote(ebuf.at[2], ebuf.at[4], 10, right)
+            ef.start()
+            done.append(ef)
+    cr.wait_recv()
+    cl.wait_recv()
+    tbuf[0] = s1[x, 0] + recv_r[2]
+    tbuf[1] = s1[x, 1] + recv_l[2]
+    el.wait_recv()
+    ef.wait_recv()
+    ebuf[5] = ebuf[1] + ebuf[2] + ebuf[3] + ebuf[4]
+
+    c3 = remote(tbuf.at[1 - yl], r3, 11, ypart)
+    c3.start()
+    ce3 = remote(ebuf.at[5], ebuf.at[6], 12, ypart)
+    ce3.start()
+    c3.wait()
+    ce3.wait()
+    out_ref[...] = tbuf[yl] + r3[...]
+    eout_ref[...] = ebuf[5] + ebuf[6]
+    for d in done:
+        d.wait_send()
+
+
+def scatter_grams(grams, energy_part):
+    slots, rows, block = grams.shape[-3:]
+    part = (slots, rows, block)
+    f32 = jnp.float32
+    return pl.pallas_call(
+        scatter_kernel,
+        out_shape=(
+            jax.ShapeDtypeStruct(part, f32),
+            jax.ShapeDtypeStruct(energy_part.shape, f32),
+        ),
+        in_specs=[pl.BlockSpec(memory_space=pltpu.VMEM)] * 2,
+        out_specs=(pl.BlockSpec(memory_space=pltpu.VMEM),) * 2,
+        scratch_shapes=[
+            pltpu.VMEM((4, 2) + part, f32),
+            pltpu.VMEM((4, 2) + part, f32),
+            pltpu.VMEM((3,) + part, f32),
+            pltpu.VMEM((3,) + part, f32),
+            pltpu.VMEM((3,) + part, f32),
+            pltpu.VMEM((3,) + part, f32),
+            pltpu.VMEM((2,) + part, f32),
+            pltpu.VMEM(part, f32),
+            pltpu.VMEM((7,) + energy_part.shape, f32),
+            pltpu.SemaphoreType.DMA((13,)),
+            pltpu.SemaphoreType.DMA((13,)),
+        ],
+        compiler_params=pltpu.CompilerParams(
+            collective_id=0, has_side_effects=True, vmem_limit_bytes=48 * 1024 * 1024
+        ),
+    )(grams, energy_part)
 
 
 def on_device(images, stencil, pairs, live, rule_of_block, adduct):
@@ -78,16 +192,15 @@
     values = extended.astype(jnp.float32)
     squares = jnp.sum(values * values, axis=1)
     pixel_count = pix_local * shares
-    energy = lax.psum(squares, "pix") / pixel_count
-    inverse = 1.0 / jnp.sqrt(energy + 1e-06)
     lookup_tables = lax.all_gather(adduct, "ion", axis=0, tiled=True)
     first = lax.axis_index("ion") * local_blocks
-    inv_blocks = inverse.reshape(local_blocks + 2 * REACH, block)
     slots = pairs.shape[0]
     relative = pairs - first + REACH
 
     grams = pair_grams(relative, extended, shares, block)
-    gram = lax.psum_scatter(grams, "pix", scatter_dimension=0, tiled=True)[0]
+    gram, energy_sum = scatter_grams(grams, squares.reshape(-1, block))
+    inverse = 1.0 / jnp.sqrt(energy_sum.reshape(-1) / pixel_count + 1e-06)
+    inv_blocks = inverse.reshape(local_blocks + 2 * REACH, block)
 
     offset = lax.axis_index("pix") * rows
     inv_left = lax.dynamic_slice_in_dim(

time: 194 us -> 149 us (0.77)
  waiting for transfers between devices: 78.1 us -> 38.2 us
  Pallas kernels: 19.7 us -> 49.6 us
  blocking collectives: 28.6 us -> 0 us
  other arithmetic: 22.9 us -> 16.5 us
    reduce_scatter x1 -> x0, waiting for transfers between devices: 40 us -> none  [on_device(): gram = lax.psum_scatter(grams, 'pix', scatter_dimension=0, tiled=True)[0]]
    pallas_call x0 -> x1, Pallas kernels: none -> 31.6 us  [scatter_grams(): pl.pallas_call(scatter_kernel, out_shape=(jax.ShapeDtypeStruct(part, f32)...]
    psum x1 -> x0, blocking collectives: 28.6 us -> none  [on_device(): energy = lax.psum(squares, 'pix') / pixel_count]
    convert_element_type x1, other arithmetic: 15.2 us -> 8.81 us  [on_device(): smoothed = total.astype(jnp.bfloat16)]
    unnamed x9 -> x13, local copies, waits for them, and re-layouts: 5.39 us -> 6.24 us
  transfers between devices with their start and end apart: 6 -> 5, of which waited for: 3 -> 2; matrix products, arithmetic and copies ran while one was open for 16% -> 15% of each run, Pallas kernels for 10% -> 34%
where the time goes in v2:
time: 149 us; the launch traced here: 147 us
  Pallas kernels  49.6 us (33%)
  waiting for transfers between devices  38.2 us (26%)
  other arithmetic  16.5 us (11%)
  between operations  14.9 us (10%)
  starting transfers between devices  14 us (9%)
  local copies, waits for them, and re-layouts  12.6 us (8%)
    ppermute x2, waiting for transfers between devices, extended_2(): before = lax.ppermute(last, axis, up)  37.1 us
    pallas_call x1, Pallas kernels, scatter_grams(): pl.pallas_call(scatter_kernel, out_shape=(jax.ShapeDtypeStruct(part, f32)...  31.6 us
    pallas_call x1, Pallas kernels, pair_grams(): pl.pallas_call(lambda *refs: gram_kernel(shares, *refs), out_shape=jax.Sh...  18 us
    convert_element_type x1, other arithmetic, on_device(): smoothed = total.astype(jnp.bfloat16)  8.81 us
    reduce_sum x1, other arithmetic, on_device(): squares = jnp.sum(values * values, axis=1)  7.48 us
    ppermute x2, starting transfers between devices, extended_2(): after = lax.ppermute(first, axis, down)  7.06 us
    ppermute x2, starting transfers between devices, extended_2(): before = lax.ppermute(last, axis, up)  6.88 us
    unnamed x13, local copies, waits for them, and re-layouts  6.24 us
  transfers between devices with their start and end apart: 5, of which 2 were waited for; matrix products, arithmetic and copies ran while one was open for 15% of the time, Pallas kernels for 34%

profile of v2, /device:TPU:16, one launch (start us, length us, event | category | flops | bytes accessed | tf_op | source)
XLA Modules:
  0.0 147.1 jit_solution(13910223856760289724)
XLA Ops:
  7.2 0.0 copy-start
  7.2 0.0 all-gather.2.cloned.1.call-start
  7.2 1.2 fusion.18
  8.5 0.0 copy-start.2
  8.5 1.4 collective-permute-start.1
  9.9 3.1 %collective-permute-start = (bf16[1280,2]{1,0:T(8,128)(2,1)S(1)}, bf16[1280,2]{1,0:T(8,128)(2,1)S(1)}, u32[]{:S(2)}, u32[]{:S(2)}) collective-permute-start(bf16[1280,2]{1,0:T(8,128)(2,1)S(1)} %get-tuple-element.18), channel_id=1, source_target_pairs={{0,16},{16,32},{32,48},{48,64},{64,80},{80,96},{96,112},{112,128},... | collective-permute-start | bytes 15368 | tf_op jit(solution)/shard_map/ppermute | solution.py:18
  13.0 0.0 slice-start
  13.0 0.0 all-gather.2.cloned.1.call-update
  13.0 0.0 slice-start.1
  13.0 3.2 %constant_dynamic-update-slice_fusion.1 = bf16[1280,2050]{1,0:T(8,128)(2,1)S(1)} fusion(bf16[1280,2048]{1,0:T(8,128)(2,1)} %param.8), kind=kLoop, calls=%fused_computation.29 | loop fusion | bytes 10485760
  16.2 0.0 copy-done.2
  16.2 0.0 collective-permute-done.1
  16.3 0.1 constant_dynamic-update-slice_fusion
  16.3 0.0 collective-permute-done
  16.4 0.0 slice-done
  16.4 0.7 slice-done.1
  17.0 8.8 %add_convert_fusion = bf16[1280,2048]{1,0:T(8,128)(2,1)S(1)} fusion(bf16[1280,2048]{1,0:T(8,128)(2,1)S(1)} %bitcast.26, bf16[1280,2]{1,0:T(8,128)(2,1)S(1)} %collective-permute-done, bf16[1280,2050]{1,0:T(8,128)(2,1)S(1)} %constant_dynamic-update-slice_fusion, f32[2048]{0:T(1024)S(1)} %bitcast.30, f32[2048]{0:T(1024)S(1)} %bitcast.31, f32[2048]{0:T(1024)S(1)} %bitcast.28, ...), kind=kLoop, calls=%fused_computation.5 | loop fusion | flops 55050240 | bytes 21017600 | tf_op jit(solution)/shard_map/convert_element_type | solution.py:190
  25.9 0.0 copy-start.1
  25.9 2.3 %copy-done.1 = bf16[1280,2048]{1,0:T(8,128)(2,1)} copy-done((bf16[1280,2048]{1,0:T(8,128)(2,1)}, bf16[1280,2048]{1,0:T(8,128)(2,1)S(1)}, u32[]{:S(2)}) %copy-start.1) | copy-done | bytes 5242904
  28.2 0.0 copy-start.3
  28.2 0.4 fusion.17
  28.6 3.8 %collective-permute-start.2 = (bf16[384,2048]{1,0:T(8,128)(2,1)S(1)}, bf16[384,2048]{1,0:T(8,128)(2,1)}, u32[]{:S(2)}, u32[]{:S(2)}) collective-permute-start(bf16[384,2048]{1,0:T(8,128)(2,1)S(1)} %get-tuple-element.15), channel_id=1, source_target_pairs={{0,1},{1,2},{2,3},{3,4},{4,5},{5,6},{6,7},{7,8},{8,9},{9,10},{10,1... | collective-permute-start | bytes 4718600 | tf_op jit(solution)/shard_map/ppermute | solution.py:18
  32.5 5.6 %collective-permute-start.3 = (bf16[384,2048]{1,0:T(8,128)(2,1)S(1)}, bf16[384,2048]{1,0:T(8,128)(2,1)}, u32[]{:S(2)}, u32[]{:S(2)}) collective-permute-start(bf16[384,2048]{1,0:T(8,128)(2,1)S(1)} %get-tuple-element.16), channel_id=1, source_target_pairs={{1,0},{2,1},{3,2},{4,3},{5,4},{6,5},{7,6},{8,7},{9,8},{10,9},{11,1... | collective-permute-start | bytes 4718600 | tf_op jit(solution)/shard_map/ppermute | solution.py:19
  38.1 0.0 copy-done.3
  38.1 0.1 copy.10
  38.2 0.1 reshape.33.refs_0_
  39.1 0.0 copy-done
  39.1 0.8 gather_fusion
  39.9 37.1 %collective-permute-done.2 = bf16[384,2048]{1,0:T(8,128)(2,1)} collective-permute-done((bf16[384,2048]{1,0:T(8,128)(2,1)S(1)}, bf16[384,2048]{1,0:T(8,128)(2,1)}, u32[]{:S(2)}, u32[]{:S(2)}) %collective-permute-start.2) | collective-permute-done | bytes 1572896 | tf_op jit(solution)/shard_map/ppermute | solution.py:18
  77.0 1.1 collective-permute-done.3
  78.1 7.5 %multiply_reduce_fusion = (f32[2048]{0:T(1024)S(1)}, bf16[2048,2048]{1,0:T(8,128)(2,1)}) fusion(bf16[384,2048]{1,0:T(8,128)(2,1)} %collective-permute-done.3, bf16[1280,2048]{1,0:T(8,128)(2,1)} %copy-done.1, bf16[384,2048]{1,0:T(8,128)(2,1)} %collective-permute-done.2), kind=kLoop, calls=%fused_computation.4 | loop fusion | flops 37746688 | bytes 16785408 | tf_op jit(solution)/shard_map/reduce_sum | solution.py:193
  85.6 18.0 %shard_map.77.g_ref = f32[2,4,2,48,8,128]{5,4,3,2,1,0:T(8,128)S(1)} custom-call(s32[96]{0:T(128)S(1)} %reshape.33.refs_0_, bf16[2048,2048]{1,0:T(8,128)(2,1)} %get-tuple-element.12.refs_1_), custom_call_target="tpu_custom_call" | custom-call | flops 3221225472 | bytes 11534336 | tf_op jit(solution)/shard_map/pallas_call | solution.py:49
  103.6 31.6 %shard_map.78 = (f32[48,8,128]{2,1,0:T(8,128)S(1)}, f32[16,128]{1,0:T(8,128)S(1)}) custom-call(f32[2,4,2,48,8,128]{5,4,3,2,1,0:T(8,128)S(1)} %shard_map.77.g_ref, f32[16,128]{1,0:T(8,128)S(1)} %bitcast.24), custom_call_target="tpu_custom_call" | custom-call | tf_op jit(solution)/shard_map/pallas_call | solution.py:153
  135.2 0.6 gather_fusion.2
  135.8 0.6 gather_fusion.3
  136.4 0.1 dynamic-slice_select_fusion
  136.5 0.1 broadcast_select_fusion
  136.6 0.0 all-gather.2.cloned.1.call-done
  136.6 2.4 %gather_fusion.1 = bf16[48,128,128]{2,1,0:T(8,128)(2,1)S(1)} fusion(bf16[64,128,128]{2,1,0:T(8,128)(2,1)} %all-gather.2.cloned.1.call-done, s32[1024]{0:T(1024)S(1)} %pad_clamp_fusion), kind=kCustom, calls=%fused_computation.3 | custom fusion | bytes 3145920 | tf_op jit(solution)/shard_map/jit(_take)/gather | solution.py:211
  139.0 1.2 fusion.7
  (11 shorter events, 0.1 us)
Async XLA Ops:
  7.2 31.9 %copy-start = (s32[160]{0:T(256)S(1)}, s32[160]{0:T(256)}, u32[]{:S(2)}) copy-start(s32[160]{0:T(256)} %param.12) | copy-start | bytes 1924
  7.2 129.4 %all-gather.2.cloned.1.call-start = ((), (), s32[]{:S(2)}) async-start(), calls=%async_computation | async-start | bytes 2228224 | tf_op jit(solution)/shard_map/all_gather | solution.py:195
  8.5 7.7 %copy-start.2 = (f32[5,2048]{1,0:T(8,128)S(1)}, f32[5,2048]{1,0:T(8,128)}, u32[]{:S(2)}) copy-start(f32[5,2048]{1,0:T(8,128)} %param.9) | copy-start | bytes 122884
  8.5 7.8 %collective-permute-start.1 = (bf16[1280,2]{1,0:T(8,128)(2,1)S(1)}, bf16[1280,2]{1,0:T(8,128)(2,1)S(1)}, u32[]{:S(2)}, u32[]{:S(2)}) collective-permute-start(bf16[1280,2]{1,0:T(8,128)(2,1)S(1)} %get-tuple-element.17), channel_id=1, source_target_pairs={{16,0},{32,16},{48,32},{64,48},{80,64},{96,80},{112,96},{128,112},... | collective-permute-start | bytes 15368 | tf_op jit(solution)/shard_map/ppermute | solution.py:19
  9.9 6.4 %collective-permute-start = (bf16[1280,2]{1,0:T(8,128)(2,1)S(1)}, bf16[1280,2]{1,0:T(8,128)(2,1)S(1)}, u32[]{:S(2)}, u32[]{:S(2)}) collective-permute-start(bf16[1280,2]{1,0:T(8,128)(2,1)S(1)} %get-tuple-element.18), channel_id=1, source_target_pairs={{0,16},{16,32},{32,48},{48,64},{64,80},{80,96},{96,112},{112,128},... | collective-permute-start | bytes 15368 | tf_op jit(solution)/shard_map/ppermute | solution.py:18
  13.0 3.4 %slice-start = ((s8[5242880]{0:T(1024)(128)(4,1)}), s8[1048576]{0:T(1024)(128)(4,1)S(1)}, s32[]{:S(2)}) async-start(s8[5242880]{0:T(1024)(128)(4,1)} %bitcast.25), calls=%async_computation.1 | async-start | bytes 2097152
  13.0 4.0 %slice-start.1 = ((s8[5242880]{0:T(1024)(128)(4,1)}), s8[4194304]{0:T(1024)(128)(4,1)S(1)}, s32[]{:S(2)}) async-start(s8[5242880]{0:T(1024)(128)(4,1)} %bitcast.25), calls=%async_computation.2 | async-start | bytes 8388608
  25.9 2.4 %copy-start.1 = (bf16[1280,2048]{1,0:T(8,128)(2,1)}, bf16[1280,2048]{1,0:T(8,128)(2,1)S(1)}, u32[]{:S(2)}) copy-start(bf16[1280,2048]{1,0:T(8,128)(2,1)S(1)} %add_convert_fusion) | copy-start | bytes 15728644
  28.2 9.9 %copy-start.3 = (s32[48,2]{0,1:T(2,128)S(1)}, s32[48,2]{0,1:T(2,128)}, u32[]{:S(2)}) copy-start(s32[48,2]{0,1:T(2,128)} %param.10) | copy-start | bytes 1156
  28.6 48.3 %collective-permute-start.2 = (bf16[384,2048]{1,0:T(8,128)(2,1)S(1)}, bf16[384,2048]{1,0:T(8,128)(2,1)}, u32[]{:S(2)}, u32[]{:S(2)}) collective-permute-start(bf16[384,2048]{1,0:T(8,128)(2,1)S(1)} %get-tuple-element.15), channel_id=1, source_target_pairs={{0,1},{1,2},{2,3},{3,4},{4,5},{5,6},{6,7},{7,8},{8,9},{9,10},{10,1... | collective-permute-start | bytes 4718600 | tf_op jit(solution)/shard_map/ppermute | solution.py:18
  32.5 45.6 %collective-permute-start.3 = (bf16[384,2048]{1,0:T(8,128)(2,1)S(1)}, bf16[384,2048]{1,0:T(8,128)(2,1)}, u32[]{:S(2)}, u32[]{:S(2)}) collective-permute-start(bf16[384,2048]{1,0:T(8,128)(2,1)S(1)} %get-tuple-element.16), channel_id=1, source_target_pairs={{1,0},{2,1},{3,2},{4,3},{5,4},{6,5},{7,6},{8,7},{9,8},{10,9},{11,1... | collective-permute-start | bytes 4718600 | tf_op jit(solution)/shard_map/ppermute | solution.py:19
Sparse Core Ops, SparseCore 0:
  13.1 91.1 all-gather.1

commit v3 on v2

--- a/solution.py
+++ b/solution.py
@@ -177,22 +177,51 @@
     )(grams, energy_part)
 
 
+def smooth_rows(padded, stencil):
+    pix_local = stencil.shape[1]
+    total = jnp.zeros((padded.shape[0], pix_local), jnp.float32)
+    for tap in range(5):
+        total = total + stencil[tap][None, :] * padded[:, tap : tap + pix_local].astype(jnp.float32)
+    return total.astype(jnp.bfloat16)
+
+
+def row_squares(rows):
+    values = rows.astype(jnp.float32)
+    return jnp.sum(values * values, axis=1)
+
+
 def on_device(images, stencil, pairs, live, rule_of_block, adduct):
     local_rows, pix_local = images.shape
     block = adduct.shape[1]
     local_blocks = local_rows // block
     shares = lax.axis_size("pix")
     rows = block // shares
+    width = REACH * block
+    ions = lax.axis_size("ion")
+    up = [(i, i + 1) for i in range(ions - 1)]
+    down = [(j, i) for i, j in up]
+    raw_before = lax.ppermute(images[local_rows - width :], "ion", up)
+    raw_after = lax.ppermute(images[:width], "ion", down)
+    offset = lax.axis_index("pix") * rows
+    piece = lax.dynamic_slice_in_dim(adduct, offset, rows, 1)
+    lookup_tables = lax.all_gather(
+        lax.all_gather(piece, "ion", axis=0, tiled=True), "pix", axis=1, tiled=True
+    )
     padded = extended_2(images, (("pix", 1),), 2)
-    total = jnp.zeros((local_rows, pix_local), jnp.float32)
-    for tap in range(5):
-        total = total + stencil[tap][None, :] * padded[:, tap : tap + pix_local].astype(jnp.float32)
-    smoothed = total.astype(jnp.bfloat16)
-    extended = extended_2(smoothed, (("ion", 0),), REACH * block)
-    values = extended.astype(jnp.float32)
-    squares = jnp.sum(values * values, axis=1)
+    smoothed = smooth_rows(padded, stencil)
+    local_squares = row_squares(smoothed)
+    edges = jnp.concatenate([padded[:, :2], padded[:, pix_local + 2 :]], axis=1)
+    edge_before = lax.ppermute(edges[local_rows - width :], "ion", up)
+    edge_after = lax.ppermute(edges[:width], "ion", down)
+    before = smooth_rows(
+        jnp.concatenate([edge_before[:, :2], raw_before, edge_before[:, 2:]], axis=1), stencil
+    )
+    after = smooth_rows(
+        jnp.concatenate([edge_after[:, :2], raw_after, edge_after[:, 2:]], axis=1), stencil
+    )
+    extended = jnp.concatenate([before, smoothed, after], axis=0)
+    squares = jnp.concatenate([row_squares(before), local_squares, row_squares(after)])
     pixel_count = pix_local * shares
-    lookup_tables = lax.all_gather(adduct, "ion", axis=0, tiled=True)
     first = lax.axis_index("ion") * local_blocks
     slots = pairs.shape[0]
     relative = pairs - first + REACH
@@ -202,7 +231,6 @@
     inverse = 1.0 / jnp.sqrt(energy_sum.reshape(-1) / pixel_count + 1e-06)
     inv_blocks = inverse.reshape(local_blocks + 2 * REACH, block)
 
-    offset = lax.axis_index("pix") * rows
     inv_left = lax.dynamic_slice_in_dim(
         jnp.take(inv_blocks, relative[:, 0], axis=0), offset, rows, 1
     )

time: 149 us -> 217 us (1.46)
  blocking collectives: 0 us -> 71.2 us
  waiting for transfers between devices: 38.2 us -> 0.03 us
  other arithmetic: 16.5 us -> 35 us
  local copies, waits for them, and re-layouts: 12.6 us -> 21.7 us
  starting transfers between devices: 14 us -> 22.7 us
    all_gather x0 -> x1, blocking collectives: none -> 71.2 us  [on_device(): lax.all_gather(piece, 'ion', axis=0, tiled=True)]
    ppermute x2 -> x1, waiting for transfers between devices: 37.1 us -> 0.01 us  [extended_2(): before = lax.ppermute(last, axis, up)]
    reduce_sum x1 -> x3, other arithmetic: 7.48 us -> 30.7 us  [row_squares(): return jnp.sum(values * values, axis=1)]
    ppermute x0 -> x4, starting transfers between devices: none -> 18.9 us  [the longest x1 7.53 us: on_device(): edge_after = lax.ppermute(edges[:width], 'ion', down)]
    convert_element_type x1 -> x0, other arithmetic: 8.81 us -> none  [on_device(): smoothed = total.astype(jnp.bfloat16)]
    ppermute x2 -> x1, starting transfers between devices: 7.06 us -> 1.28 us  [extended_2(): after = lax.ppermute(first, axis, down)]
    ppermute x2 -> x1, starting transfers between devices: 6.88 us -> 2.48 us  [extended_2(): before = lax.ppermute(last, axis, up)]
    concatenate x0 -> x1, other arithmetic: none -> 4.05 us  [on_device(): extended = jnp.concatenate([before, smoothed, after], axis=0)]
  transfers between devices with their start and end apart: 5 -> 7, of which waited for: 2 -> 0; matrix products, arithmetic and copies ran while one was open for 15% -> 24% of each run, Pallas kernels for 34% -> 23%
where the time goes in v3:
time: 217 us
  blocking collectives  71.2 us (33%)
  Pallas kernels  50.1 us (23%)
  other arithmetic  35 us (16%)
  starting transfers between devices  22.7 us (10%)
  local copies, waits for them, and re-layouts  21.7 us (10%)
  between operations  15 us (7%)
    all_gather x1, blocking collectives, on_device(): lax.all_gather(piece, 'ion', axis=0, tiled=True)  71.2 us
    pallas_call x1, Pallas kernels, scatter_grams(): pl.pallas_call(scatter_kernel, out_shape=(jax.ShapeDtypeStruct(part, f32)...  32.1 us
    reduce_sum x3, other arithmetic, row_squares(): return jnp.sum(values * values, axis=1)  30.7 us
    pallas_call x1, Pallas kernels, pair_grams(): pl.pallas_call(lambda *refs: gram_kernel(shares, *refs), out_shape=jax.Sh...  18 us
    ppermute x1, starting transfers between devices, on_device(): edge_after = lax.ppermute(edges[:width], 'ion', down)  7.53 us
    unnamed x11, local copies, waits for them, and re-layouts  5.75 us
    ppermute x1, starting transfers between devices, on_device(): raw_after = lax.ppermute(images[:width], 'ion', down)  5.63 us
  transfers between devices with their start and end apart: 7, of which 0 were waited for; matrix products, arithmetic and copies ran while one was open for 24% of the time, Pallas kernels for 23%

profile of v3, /device:TPU:16, one launch (start us, length us, event | category | flops | bytes accessed | tf_op | source)
XLA Modules:
  0.0 216.9 jit_solution(984702564490187597)
XLA Ops:
  7.2 0.0 copy-start
  7.2 0.0 all-gather.2.cloned.1.call-start
  7.2 2.1 fusion.22
  9.3 2.5 %collective-permute-start = (bf16[1280,2]{1,0:T(8,128)(2,1)}, bf16[1280,2]{1,0:T(8,128)(2,1)}, u32[]{:S(2)}, u32[]{:S(2)}) collective-permute-start(bf16[1280,2]{1,0:T(8,128)(2,1)} %get-tuple-element.21), channel_id=1, source_target_pairs={{0,16},{16,32},{32,48},{48,64},{64,80},{80,96},{96,112},{112,128},... | collective-permute-start | bytes 15368 | tf_op jit(solution)/shard_map/ppermute | solution.py:18
  11.8 1.3 collective-permute-start.1
  13.0 4.0 %fusion.21 = (bf16[384,2048]{1,0:T(8,128)(2,1)}, bf16[384,2048]{1,0:T(8,128)(2,1)}) fusion(bf16[1280,2048]{1,0:T(8,128)(2,1)} %param.8), kind=kLoop, calls=%fused_computation.67 | loop fusion | bytes 6291456 | tf_op jit(solution)/shard_map/slice | solution.py:203
  17.1 3.8 %collective-permute-start.3 = (bf16[384,2048]{1,0:T(8,128)(2,1)}, bf16[384,2048]{1,0:T(8,128)(2,1)S(1)}, u32[]{:S(2)}, u32[]{:S(2)}) collective-permute-start(bf16[384,2048]{1,0:T(8,128)(2,1)} %get-tuple-element.19), channel_id=1, source_target_pairs={{0,1},{1,2},{2,3},{3,4},{4,5},{5,6},{6,7},{7,8},{8,9},{9,10},{10,1... | collective-permute-start | bytes 4718600 | tf_op jit(solution)/shard_map/ppermute | solution.py:203
  20.9 5.6 %collective-permute-start.5 = (bf16[384,2048]{1,0:T(8,128)(2,1)}, bf16[384,2048]{1,0:T(8,128)(2,1)S(1)}, u32[]{:S(2)}, u32[]{:S(2)}) collective-permute-start(bf16[384,2048]{1,0:T(8,128)(2,1)} %get-tuple-element.20), channel_id=1, source_target_pairs={{1,0},{2,1},{3,2},{4,3},{5,4},{6,5},{7,6},{8,7},{9,8},{10,9},{11,1... | collective-permute-start | bytes 4718600 | tf_op jit(solution)/shard_map/ppermute | solution.py:204
  26.5 0.0 copy-done
  26.6 71.2 %all_gather.6 = bf16[64,8,128]{2,1,0:T(8,128)(2,1)} all-gather(bf16[4,8,128]{2,1,0:T(8,128)(2,1)S(1)} %constant_dynamic-slice_fusion), channel_id=1, replica_groups=mesh['pix'=16,'ion'=16] {'ion'}, dimensions={0}, use_global_device_ids=true | all-gather | bytes 139264 | tf_op jit(solution)/shard_map/all_gather | solution.py:208
  97.8 0.0 all-gather.2.cloned.1.call-update
  97.8 0.0 copy-start.3
  97.8 0.0 copy-start.4
  97.9 0.0 copy-start.1
  97.9 5.7 %constant_dynamic-update-slice_fusion.1 = bf16[1280,2050]{1,0:T(8,128)(2,1)} fusion(bf16[1280,2048]{1,0:T(8,128)(2,1)} %param.8), kind=kLoop, calls=%fused_computation.50 | loop fusion | bytes 10485760
  103.6 0.0 copy-done.3
  103.6 0.0 copy-done.4
  103.7 0.0 copy-done.1
  103.7 0.8 gather_fusion
  105.2 0.1 copy.10
  105.3 0.1 reshape.33.refs_0_
  105.4 0.0 collective-permute-done
  105.4 1.1 copy.11
  106.6 0.0 collective-permute-done.1
  106.6 1.1 copy.12
  107.7 0.8 copy.13
  108.5 1.9 collective-permute-start.2
  110.5 0.2 copy.14
  110.6 7.5 %collective-permute-start.4 = (bf16[384,4]{1,0:T(8,128)(2,1)S(1)}, bf16[384,4]{1,0:T(8,128)(2,1)S(1)}, u32[]{:S(2)}, u32[]{:S(2)}) collective-permute-start(bf16[384,4]{1,0:T(8,128)(2,1)S(1)} %copy.14), channel_id=1, source_target_pairs={{1,0},{2,1},{3,2},{4,3},{5,4},{6,5},{7,6},{8,7},{9,8},{10,9},{11,1... | collective-permute-start | bytes 9224 | tf_op jit(solution)/shard_map/ppermute | solution.py:215
  118.2 1.8 constant_dynamic-update-slice_fusion
  120.0 23.4 %multiply_reduce_fusion = (f32[1280]{0:T(1024)S(1)}, bf16[1280,2048]{1,0:T(8,128)(2,1)S(1)}) fusion(bf16[1280,2050]{1,0:T(8,128)(2,1)} %constant_dynamic-update-slice_fusion, f32[2048]{0:T(1024)S(1)} %bitcast.34, f32[2048]{0:T(1024)S(1)} %bitcast.37, bf16[1280,2048]{1,0:T(8,128)(2,1)} %param.8, f32[2048]{0:T(1024)S(1)} %bitcast.28, ...), kind=kLoop, calls=%fused_computation.4 | loop fusion | flops 62913280 | bytes 21022720 | tf_op jit(solution)/shard_map/reduce_sum | solution.py:190
  143.3 0.0 copy-start.2
  143.4 0.0 collective-permute-done.2
  143.4 0.1 fusion.23
  143.5 0.0 collective-permute-done.4
  143.5 0.1 fusion.24
  143.6 0.0 collective-permute-done.3
  143.6 3.7 %multiply_reduce_fusion.2 = (f32[384]{0:T(512)S(1)}, bf16[384,2048]{1,0:T(8,128)(2,1)S(1)}) fusion(bf16[384,2]{1,0:T(8,128)(2,1)S(1)} %get-tuple-element.24, bf16[384,2048]{1,0:T(8,128)(2,1)S(1)} %collective-permute-done.3, f32[2048]{0:T(1024)S(1)} %bitcast.35, f32[2048]{0:T(1024)S(1)} %bitcast.38, f32[2048]{0:T(1024)S(1)} %bitcast.29, ...), kind=kLoop, calls=%fused_computation.12 | loop fusion | flops 23592576 | bytes 3191296 | tf_op jit(solution)/shard_map/reduce_sum | solution.py:190
  147.2 0.0 collective-permute-done.5
  147.3 3.7 %multiply_reduce_fusion.1 = (f32[384]{0:T(512)S(1)}, bf16[384,2048]{1,0:T(8,128)(2,1)S(1)}) fusion(bf16[384,2]{1,0:T(8,128)(2,1)S(1)} %get-tuple-element.26, bf16[384,2048]{1,0:T(8,128)(2,1)S(1)} %collective-permute-done.5, f32[2048]{0:T(1024)S(1)} %bitcast.36, f32[2048]{0:T(1024)S(1)} %bitcast.39, f32[2048]{0:T(1024)S(1)} %bitcast.30, ...), kind=kLoop, calls=%fused_computation.11 | loop fusion | flops 23592576 | bytes 3191296 | tf_op jit(solution)/shard_map/reduce_sum | solution.py:190
  150.9 0.0 copy-done.2
  150.9 4.0 %pad_maximum_fusion.refs_1_ = bf16[2048,2048]{1,0:T(8,128)(2,1)} fusion(bf16[384,2048]{1,0:T(8,128)(2,1)S(1)} %get-tuple-element.16, bf16[1280,2048]{1,0:T(8,128)(2,1)S(1)} %get-tuple-element.14, bf16[384,2048]{1,0:T(8,128)(2,1)S(1)} %get-tuple-element.12), kind=kLoop, calls=%fused_computation.6 | loop fusion | flops 25165824 | bytes 16777216 | tf_op jit(solution)/shard_map/concatenate | solution.py:222
  155.0 18.0 %shard_map.77.g_ref = f32[2,4,2,48,8,128]{5,4,3,2,1,0:T(8,128)S(1)} custom-call(s32[96]{0:T(128)S(1)} %reshape.33.refs_0_, bf16[2048,2048]{1,0:T(8,128)(2,1)} %pad_maximum_fusion.refs_1_), custom_call_target="tpu_custom_call" | custom-call | flops 3221225472 | bytes 11534336 | tf_op jit(solution)/shard_map/pallas_call | solution.py:49
  173.0 32.1 %shard_map.78 = (f32[48,8,128]{2,1,0:T(8,128)S(1)}, f32[16,128]{1,0:T(8,128)S(1)}) custom-call(f32[2,4,2,48,8,128]{5,4,3,2,1,0:T(8,128)S(1)} %shard_map.77.g_ref, f32[16,128]{1,0:T(8,128)S(1)} %maximum_bitcast_fusion.e_ref), custom_call_target="tpu_custom_call" | custom-call | tf_op jit(solution)/shard_map/pallas_call | solution.py:153
  205.1 0.6 gather_fusion.2
  205.7 0.6 gather_fusion.3
  206.3 0.1 dynamic-slice_select_fusion
  206.3 0.1 broadcast_select_fusion
  206.4 0.0 all-gather.2.cloned.1.call-done
  206.4 2.4 %gather_fusion.1 = bf16[48,128,128]{2,1,0:T(8,128)(2,1)S(1)} fusion(bf16[64,128,128]{2,1,0:T(8,128)(2,1)} %all-gather.2.cloned.1.call-done, s32[1024]{0:T(1024)S(1)} %pad_clamp_fusion), kind=kCustom, calls=%fused_computation.3 | custom fusion | bytes 3145920 | tf_op jit(solution)/shard_map/jit(_take)/gather | solution.py:239
  208.9 1.2 fusion.11
  (13 shorter events, 0.1 us)
Async XLA Ops:
  7.2 19.4 %copy-start = (bf16[4,128,128]{2,1,0:T(8,128)(2,1)S(1)}, bf16[4,128,128]{2,1,0:T(8,128)(2,1)}, u32[]{:S(2)}) copy-start(bf16[4,128,128]{2,1,0:T(8,128)(2,1)} %param.13) | copy-start | bytes 393220
  7.2 199.2 %all-gather.2.cloned.1.call-start = ((), (), s32[]{:S(2)}) async-start(), calls=%async_computation | async-start | bytes 2228224 | tf_op jit(solution)/shard_map/all_gather | solution.py:207
  9.3 96.1 %collective-permute-start = (bf16[1280,2]{1,0:T(8,128)(2,1)}, bf16[1280,2]{1,0:T(8,128)(2,1)}, u32[]{:S(2)}, u32[]{:S(2)}) collective-permute-start(bf16[1280,2]{1,0:T(8,128)(2,1)} %get-tuple-element.21), channel_id=1, source_target_pairs={{0,16},{16,32},{32,48},{48,64},{64,80},{80,96},{96,112},{112,128},... | collective-permute-start | bytes 15368 | tf_op jit(solution)/shard_map/ppermute | solution.py:18
  11.8 94.8 %collective-permute-start.1 = (bf16[1280,2]{1,0:T(8,128)(2,1)}, bf16[1280,2]{1,0:T(8,128)(2,1)}, u32[]{:S(2)}, u32[]{:S(2)}) collective-permute-start(bf16[1280,2]{1,0:T(8,128)(2,1)} %get-tuple-element.22), channel_id=1, source_target_pairs={{16,0},{32,16},{48,32},{64,48},{80,64},{96,80},{112,96},{128,112},... | collective-permute-start | bytes 15368 | tf_op jit(solution)/shard_map/ppermute | solution.py:19
  17.1 126.5 %collective-permute-start.3 = (bf16[384,2048]{1,0:T(8,128)(2,1)}, bf16[384,2048]{1,0:T(8,128)(2,1)S(1)}, u32[]{:S(2)}, u32[]{:S(2)}) collective-permute-start(bf16[384,2048]{1,0:T(8,128)(2,1)} %get-tuple-element.19), channel_id=1, source_target_pairs={{0,1},{1,2},{2,3},{3,4},{4,5},{5,6},{6,7},{7,8},{8,9},{9,10},{10,1... | collective-permute-start | bytes 4718600 | tf_op jit(solution)/shard_map/ppermute | solution.py:203
  20.9 126.4 %collective-permute-start.5 = (bf16[384,2048]{1,0:T(8,128)(2,1)}, bf16[384,2048]{1,0:T(8,128)(2,1)S(1)}, u32[]{:S(2)}, u32[]{:S(2)}) collective-permute-start(bf16[384,2048]{1,0:T(8,128)(2,1)} %get-tuple-element.20), channel_id=1, source_target_pairs={{1,0},{2,1},{3,2},{4,3},{5,4},{6,5},{7,6},{8,7},{9,8},{10,9},{11,1... | collective-permute-start | bytes 4718600 | tf_op jit(solution)/shard_map/ppermute | solution.py:204
  97.8 5.8 %copy-start.3 = (f32[5,2048]{1,0:T(8,128)S(1)}, f32[5,2048]{1,0:T(8,128)}, u32[]{:S(2)}) copy-start(f32[5,2048]{1,0:T(8,128)} %param.9) | copy-start | bytes 122884
  97.8 5.8 %copy-start.4 = (s32[48,2]{0,1:T(2,128)S(1)}, s32[48,2]{0,1:T(2,128)}, u32[]{:S(2)}) copy-start(s32[48,2]{0,1:T(2,128)} %param.10) | copy-start | bytes 1156
  97.9 5.8 %copy-start.1 = (s32[160]{0:T(256)S(1)}, s32[160]{0:T(256)}, u32[]{:S(2)}) copy-start(s32[160]{0:T(256)} %param.12) | copy-start | bytes 1924
  108.5 34.8 %collective-permute-start.2 = (bf16[384,4]{1,0:T(8,128)(2,1)}, bf16[384,4]{1,0:T(8,128)(2,1)S(1)}, u32[]{:S(2)}, u32[]{:S(2)}) collective-permute-start(bf16[384,4]{1,0:T(8,128)(2,1)} %copy.13), channel_id=1, source_target_pairs={{0,1},{1,2},{2,3},{3,4},{4,5},{5,6},{6,7},{7,8},{8,9},{9,10},{10,1... | collective-permute-start | bytes 9224 | tf_op jit(solution)/shard_map/ppermute | solution.py:214
  110.6 32.8 %collective-permute-start.4 = (bf16[384,4]{1,0:T(8,128)(2,1)S(1)}, bf16[384,4]{1,0:T(8,128)(2,1)S(1)}, u32[]{:S(2)}, u32[]{:S(2)}) collective-permute-start(bf16[384,4]{1,0:T(8,128)(2,1)S(1)} %copy.14), channel_id=1, source_target_pairs={{1,0},{2,1},{3,2},{4,3},{5,4},{6,5},{7,6},{8,7},{9,8},{10,9},{11,1... | collective-permute-start | bytes 9224 | tf_op jit(solution)/shard_map/ppermute | solution.py:215
  143.3 7.6 %copy-start.2 = (bf16[1280,2048]{1,0:T(8,128)(2,1)}, bf16[1280,2048]{1,0:T(8,128)(2,1)S(1)}, u32[]{:S(2)}) copy-start(bf16[1280,2048]{1,0:T(8,128)(2,1)S(1)} %get-tuple-element.14) | copy-start | bytes 15728644
Sparse Core Ops, SparseCore 0:
  98.0 37.6 all-gather.1

commit v4 on v3

--- a/solution.py
+++ b/solution.py
@@ -202,11 +202,17 @@
     down = [(j, i) for i, j in up]
     raw_before = lax.ppermute(images[local_rows - width :], "ion", up)
     raw_after = lax.ppermute(images[:width], "ion", down)
-    offset = lax.axis_index("pix") * rows
-    piece = lax.dynamic_slice_in_dim(adduct, offset, rows, 1)
-    lookup_tables = lax.all_gather(
-        lax.all_gather(piece, "ion", axis=0, tiled=True), "pix", axis=1, tiled=True
-    )
+    me_pix = lax.axis_index("pix")
+    me_ion = lax.axis_index("ion")
+    offset = me_pix * rows
+    turn = [
+        (p * ions + j, p * ions + (j - p) % ions)
+        for j in range(ions)
+        for p in range(1, shares)
+    ]
+    fetched = lax.ppermute(adduct, ("pix", "ion"), turn)
+    own_turn = jnp.where(me_pix == 0, adduct, fetched)
+    lookup_tables = lax.all_gather(own_turn, "pix", axis=0, tiled=True)
     padded = extended_2(images, (("pix", 1),), 2)
     smoothed = smooth_rows(padded, stencil)
     local_squares = row_squares(smoothed)
@@ -236,6 +242,8 @@
     )
     inv_right = jnp.take(inv_blocks, relative[:, 1], axis=0)
     rules = jnp.take(rule_of_block, pairs[:, 1], axis=0)
+    per_index = adduct.shape[0]
+    rules = ((rules // per_index - me_ion) % ions) * per_index + rules % per_index
     matrices = jnp.take(lookup_tables, rules, axis=0)
     coloc = (gram * inv_left[:, :, None] * inv_right[:, None, :] / pixel_count).astype(jnp.bfloat16)
     scores = jnp.einsum("src,scd->srd", coloc, matrices, preferred_element_type=jnp.float32)

time: 217 us -> 173 us (0.80)
  the two profiles are of different devices: /device:TPU:16 before, /device:TPU:66 now
where the time goes in v4:
time: 173 us
  Pallas kernels  48.5 us (28%)
  other arithmetic  38.8 us (22%)
  starting transfers between devices  25.8 us (15%)
  waiting for transfers between devices  23.4 us (14%)
  local copies, waits for them, and re-layouts  19.8 us (11%)
  between operations  15 us (9%)
    pallas_call x1, Pallas kernels, scatter_grams(): pl.pallas_call(scatter_kernel, out_shape=(jax.ShapeDtypeStruct(part, f32)...  30.6 us
    reduce_sum x3, other arithmetic, row_squares(): return jnp.sum(values * values, axis=1)  30.6 us
    ppermute x1, waiting for transfers between devices, on_device(): fetched = lax.ppermute(adduct, ('pix', 'ion'), turn)  23.4 us
    pallas_call x1, Pallas kernels, pair_grams(): pl.pallas_call(lambda *refs: gram_kernel(shares, *refs), out_shape=jax.Sh...  17.9 us
    ppermute x1, starting transfers between devices, on_device(): edge_after = lax.ppermute(edges[:width], 'ion', down)  7.1 us
    ppermute x1, starting transfers between devices, on_device(): edge_before = lax.ppermute(edges[local_rows - width:], 'ion', up)  4.93 us
    concatenate x1, other arithmetic, on_device(): extended = jnp.concatenate([before, smoothed, after], axis=0)  4.06 us
    slice x1, local copies, waits for them, and re-layouts, on_device(): raw_before = lax.ppermute(images[local_rows - width:], 'ion', up)  3.99 us
  transfers between devices with their start and end apart: 8, of which 1 were waited for; matrix products, arithmetic and copies ran while one was open for 31% of the time, Pallas kernels for 28%

profile of v4, /device:TPU:66, one launch (start us, length us, event | category | flops | bytes accessed | tf_op | source)
XLA Modules:
  0.0 172.6 jit_solution(10925485238754589578)
XLA Ops:
  7.2 0.0 copy-start
  7.2 0.0 all-gather.2.cloned.1.call-start
  7.2 2.0 %fusion.25 = (bf16[1280,2]{1,0:T(8,128)(2,1)}, bf16[1280,2]{1,0:T(8,128)(2,1)}) fusion(bf16[1280,2048]{1,0:T(8,128)(2,1)} %param.8), kind=kLoop, calls=%fused_computation.79 | loop fusion | bytes 20480 | tf_op jit(solution)/shard_map/slice | solution.py:16
  9.3 1.9 %collective-permute-start = (bf16[1280,2]{1,0:T(8,128)(2,1)}, bf16[1280,2]{1,0:T(8,128)(2,1)}, u32[]{:S(2)}, u32[]{:S(2)}) collective-permute-start(bf16[1280,2]{1,0:T(8,128)(2,1)} %get-tuple-element.21), channel_id=1, source_target_pairs={{0,16},{16,32},{32,48},{48,64},{64,80},{80,96},{96,112},{112,128},... | collective-permute-start | bytes 15368 | tf_op jit(solution)/shard_map/ppermute | solution.py:18
  11.2 0.0 copy-start.1
  11.2 3.9 %collective-permute-start.1 = (bf16[1280,2]{1,0:T(8,128)(2,1)}, bf16[1280,2]{1,0:T(8,128)(2,1)S(1)}, u32[]{:S(2)}, u32[]{:S(2)}) collective-permute-start(bf16[1280,2]{1,0:T(8,128)(2,1)} %get-tuple-element.22), channel_id=1, source_target_pairs={{16,0},{32,16},{48,32},{64,48},{80,64},{96,80},{112,96},{128,112},... | collective-permute-start | bytes 15368 | tf_op jit(solution)/shard_map/ppermute | solution.py:19
  15.1 4.0 %fusion.24 = (bf16[384,2048]{1,0:T(8,128)(2,1)}, bf16[384,2048]{1,0:T(8,128)(2,1)}) fusion(bf16[1280,2048]{1,0:T(8,128)(2,1)} %param.8), kind=kLoop, calls=%fused_computation.78 | loop fusion | bytes 6291456 | tf_op jit(solution)/shard_map/slice | solution.py:203
  19.1 3.8 %collective-permute-start.3 = (bf16[384,2048]{1,0:T(8,128)(2,1)}, bf16[384,2048]{1,0:T(8,128)(2,1)S(1)}, u32[]{:S(2)}, u32[]{:S(2)}) collective-permute-start(bf16[384,2048]{1,0:T(8,128)(2,1)} %get-tuple-element.19), channel_id=1, source_target_pairs={{0,1},{1,2},{2,3},{3,4},{4,5},{5,6},{6,7},{7,8},{8,9},{9,10},{10,1... | collective-permute-start | bytes 4718600 | tf_op jit(solution)/shard_map/ppermute | solution.py:203
  22.9 0.0 copy-start.3
  22.9 0.0 copy-start.4
  22.9 2.1 %collective-permute-start.5 = (bf16[384,2048]{1,0:T(8,128)(2,1)}, bf16[384,2048]{1,0:T(8,128)(2,1)S(1)}, u32[]{:S(2)}, u32[]{:S(2)}) collective-permute-start(bf16[384,2048]{1,0:T(8,128)(2,1)} %get-tuple-element.20), channel_id=1, source_target_pairs={{1,0},{2,1},{3,2},{4,3},{5,4},{6,5},{7,6},{8,7},{9,8},{10,9},{11,1... | collective-permute-start | bytes 4718600 | tf_op jit(solution)/shard_map/ppermute | solution.py:204
  25.1 1.9 %collective-permute-start.6 = (bf16[4,128,128]{2,1,0:T(8,128)(2,1)}, bf16[4,128,128]{2,1,0:T(8,128)(2,1)}, u32[]{:S(2)}, u32[]{:S(2)}) collective-permute-start(bf16[4,128,128]{2,1,0:T(8,128)(2,1)} %param.13), channel_id=1, source_target_pairs={{16,31},{32,46},{48,61},{64,76},{80,91},{96,106},{112,121},{128,13... | collective-permute-start | bytes 393224 | tf_op jit(solution)/shard_map/ppermute | solution.py:213
  27.0 0.0 copy-done.1
  27.0 2.8 %constant_dynamic-update-slice_fusion.1 = bf16[1280,2050]{1,0:T(8,128)(2,1)} fusion(bf16[1280,2048]{1,0:T(8,128)(2,1)S(1)} %copy-done.1), kind=kLoop, calls=%fused_computation.51 | loop fusion | bytes 10485760
  29.8 0.0 copy-done.3
  29.8 0.0 copy-done.4
  29.9 0.6 compare_and_fusion.1
  30.5 0.0 copy-done
  30.5 0.8 gather_fusion
  31.3 0.6 and_bitcast_fusion
  31.9 0.6 pad_clamp_fusion
  33.1 0.6 iota_compare_fusion
  33.7 0.1 copy.10
  33.8 0.1 reshape.33.refs_0_
  33.9 0.0 collective-permute-done
  34.0 1.1 copy.11
  35.1 0.0 collective-permute-done.1
  35.1 0.2 copy.12
  35.3 0.8 copy.13
  36.1 4.9 %collective-permute-start.2 = (bf16[384,4]{1,0:T(8,128)(2,1)}, bf16[384,4]{1,0:T(8,128)(2,1)}, u32[]{:S(2)}, u32[]{:S(2)}) collective-permute-start(bf16[384,4]{1,0:T(8,128)(2,1)} %copy.13), channel_id=1, source_target_pairs={{0,1},{1,2},{2,3},{3,4},{4,5},{5,6},{6,7},{7,8},{8,9},{9,10},{10,1... | collective-permute-start | bytes 9224 | tf_op jit(solution)/shard_map/ppermute | solution.py:220
  41.0 0.8 copy.14
  41.8 7.1 %collective-permute-start.4 = (bf16[384,4]{1,0:T(8,128)(2,1)}, bf16[384,4]{1,0:T(8,128)(2,1)}, u32[]{:S(2)}, u32[]{:S(2)}) collective-permute-start(bf16[384,4]{1,0:T(8,128)(2,1)} %copy.14), channel_id=1, source_target_pairs={{1,0},{2,1},{3,2},{4,3},{5,4},{6,5},{7,6},{8,7},{9,8},{10,9},{11,1... | collective-permute-start | bytes 9224 | tf_op jit(solution)/shard_map/ppermute | solution.py:221
  48.9 0.8 constant_dynamic-update-slice_fusion
  49.7 23.4 %collective-permute-done.6 = bf16[4,128,128]{2,1,0:T(8,128)(2,1)} collective-permute-done((bf16[4,128,128]{2,1,0:T(8,128)(2,1)}, bf16[4,128,128]{2,1,0:T(8,128)(2,1)}, u32[]{:S(2)}, u32[]{:S(2)}) %collective-permute-start.6) | collective-permute-done | bytes 131104 | tf_op jit(solution)/shard_map/ppermute | solution.py:213
  73.1 1.6 broadcast_select_fusion
  74.7 0.0 all-gather.2.cloned.1.call-update
  74.8 23.2 %multiply_reduce_fusion = (f32[1280]{0:T(1024)S(1)}, bf16[1280,2048]{1,0:T(8,128)(2,1)S(1)}) fusion(bf16[1280,2050]{1,0:T(8,128)(2,1)} %constant_dynamic-update-slice_fusion, f32[2048]{0:T(1024)S(1)} %bitcast.34, f32[2048]{0:T(1024)S(1)} %bitcast.37, bf16[1280,2048]{1,0:T(8,128)(2,1)} %param.8, f32[2048]{0:T(1024)S(1)} %bitcast.28, ...), kind=kLoop, calls=%fused_computation.4 | loop fusion | flops 62913280 | bytes 21022720 | tf_op jit(solution)/shard_map/reduce_sum | solution.py:190
  98.0 0.0 copy-start.2
  98.0 0.0 collective-permute-done.2
  98.0 1.3 fusion.26
  99.3 0.0 collective-permute-done.4
  99.3 1.3 fusion.27
  100.5 0.0 collective-permute-done.3
  100.6 3.7 %multiply_reduce_fusion.2 = (f32[384]{0:T(512)S(1)}, bf16[384,2048]{1,0:T(8,128)(2,1)S(1)}) fusion(bf16[384,2]{1,0:T(8,128)(2,1)S(1)} %get-tuple-element.24, bf16[384,2048]{1,0:T(8,128)(2,1)S(1)} %collective-permute-done.3, f32[2048]{0:T(1024)S(1)} %bitcast.35, f32[2048]{0:T(1024)S(1)} %bitcast.38, f32[2048]{0:T(1024)S(1)} %bitcast.29, ...), kind=kLoop, calls=%fused_computation.12 | loop fusion | flops 23592576 | bytes 3191296 | tf_op jit(solution)/shard_map/reduce_sum | solution.py:190
  104.2 0.0 collective-permute-done.5
  104.3 3.7 %multiply_reduce_fusion.1 = (f32[384]{0:T(512)S(1)}, bf16[384,2048]{1,0:T(8,128)(2,1)S(1)}) fusion(bf16[384,2]{1,0:T(8,128)(2,1)S(1)} %get-tuple-element.26, bf16[384,2048]{1,0:T(8,128)(2,1)S(1)} %collective-permute-done.5, f32[2048]{0:T(1024)S(1)} %bitcast.36, f32[2048]{0:T(1024)S(1)} %bitcast.39, f32[2048]{0:T(1024)S(1)} %bitcast.30, ...), kind=kLoop, calls=%fused_computation.11 | loop fusion | flops 23592576 | bytes 3191296 | tf_op jit(solution)/shard_map/reduce_sum | solution.py:190
  108.0 0.0 copy-done.2
  108.0 4.1 %pad_maximum_fusion.refs_1_ = bf16[2048,2048]{1,0:T(8,128)(2,1)} fusion(bf16[384,2048]{1,0:T(8,128)(2,1)S(1)} %get-tuple-element.16, bf16[1280,2048]{1,0:T(8,128)(2,1)S(1)} %get-tuple-element.14, bf16[384,2048]{1,0:T(8,128)(2,1)S(1)} %get-tuple-element.12), kind=kLoop, calls=%fused_computation.6 | loop fusion | flops 25165824 | bytes 16777216 | tf_op jit(solution)/shard_map/concatenate | solution.py:228
  112.0 17.9 %shard_map.77.g_ref = f32[2,4,2,48,8,128]{5,4,3,2,1,0:T(8,128)S(1)} custom-call(s32[96]{0:T(128)S(1)} %reshape.33.refs_0_, bf16[2048,2048]{1,0:T(8,128)(2,1)} %pad_maximum_fusion.refs_1_), custom_call_target="tpu_custom_call" | custom-call | flops 3221225472 | bytes 11534336 | tf_op jit(solution)/shard_map/pallas_call | solution.py:49
  130.0 0.0 copy-start.6
  130.0 0.0 copy-start.5
  130.0 0.0 copy-start.7
  130.0 0.0 copy-start.8
  130.0 30.6 %shard_map.78 = (f32[48,8,128]{2,1,0:T(8,128)S(1)}, f32[16,128]{1,0:T(8,128)S(1)}) custom-call(f32[2,4,2,48,8,128]{5,4,3,2,1,0:T(8,128)S(1)} %shard_map.77.g_ref, f32[16,128]{1,0:T(8,128)S(1)} %maximum_bitcast_fusion.e_ref), custom_call_target="tpu_custom_call" | custom-call | tf_op jit(solution)/shard_map/pallas_call | solution.py:153
  160.6 0.6 gather_fusion.2
  161.2 0.6 gather_fusion.3
  161.8 0.0 copy-done.6
  161.8 0.1 dynamic-slice_select_fusion
  161.9 0.0 copy-done.5
  161.9 0.1 broadcast_select_fusion.1
  162.0 2.6 %gather_fusion.1 = bf16[48,128,128]{2,1,0:T(8,128)(2,1)S(1)} fusion(bf16[64,128,128]{2,1,0:T(8,128)(2,1)} %all-gather.2.cloned.1.call-done, s32[1024]{0:T(1024)} %pad_clamp_fusion), kind=kCustom, calls=%fused_computation.3 | custom fusion | bytes 3145920 | tf_op jit(solution)/shard_map/jit(_take)/gather | solution.py:247
  164.5 0.0 copy-done.7
  164.5 0.0 copy-done.8
  164.6 1.2 fusion.11
  (9 shorter events, 0.1 us)
Async XLA Ops:
  7.2 23.3 %copy-start = (s32[160]{0:T(256)S(1)}, s32[160]{0:T(256)}, u32[]{:S(2)}) copy-start(s32[160]{0:T(256)} %param.12) | copy-start | bytes 1924
  7.2 154.8 %all-gather.2.cloned.1.call-start = ((), (), s32[]{:S(2)}) async-start(), calls=%async_computation | async-start | bytes 2228224 | tf_op jit(solution)/shard_map/all_gather | solution.py:215
  9.3 24.7 %collective-permute-start = (bf16[1280,2]{1,0:T(8,128)(2,1)}, bf16[1280,2]{1,0:T(8,128)(2,1)}, u32[]{:S(2)}, u32[]{:S(2)}) collective-permute-start(bf16[1280,2]{1,0:T(8,128)(2,1)} %get-tuple-element.21), channel_id=1, source_target_pairs={{0,16},{16,32},{32,48},{48,64},{64,80},{80,96},{96,112},{112,128},... | collective-permute-start | bytes 15368 | tf_op jit(solution)/shard_map/ppermute | solution.py:18
  11.2 15.9 %copy-start.1 = (bf16[1280,2048]{1,0:T(8,128)(2,1)S(1)}, bf16[1280,2048]{1,0:T(8,128)(2,1)}, u32[]{:S(2)}) copy-start(bf16[1280,2048]{1,0:T(8,128)(2,1)} %param.8) | copy-start | bytes 15728644
  11.2 23.9 %collective-permute-start.1 = (bf16[1280,2]{1,0:T(8,128)(2,1)}, bf16[1280,2]{1,0:T(8,128)(2,1)S(1)}, u32[]{:S(2)}, u32[]{:S(2)}) collective-permute-start(bf16[1280,2]{1,0:T(8,128)(2,1)} %get-tuple-element.22), channel_id=1, source_target_pairs={{16,0},{32,16},{48,32},{64,48},{80,64},{96,80},{112,96},{128,112},... | collective-permute-start | bytes 15368 | tf_op jit(solution)/shard_map/ppermute | solution.py:19
  19.1 81.5 %collective-permute-start.3 = (bf16[384,2048]{1,0:T(8,128)(2,1)}, bf16[384,2048]{1,0:T(8,128)(2,1)S(1)}, u32[]{:S(2)}, u32[]{:S(2)}) collective-permute-start(bf16[384,2048]{1,0:T(8,128)(2,1)} %get-tuple-element.19), channel_id=1, source_target_pairs={{0,1},{1,2},{2,3},{3,4},{4,5},{5,6},{6,7},{7,8},{8,9},{9,10},{10,1... | collective-permute-start | bytes 4718600 | tf_op jit(solution)/shard_map/ppermute | solution.py:203
  22.9 6.9 %copy-start.3 = (f32[5,2048]{1,0:T(8,128)S(1)}, f32[5,2048]{1,0:T(8,128)}, u32[]{:S(2)}) copy-start(f32[5,2048]{1,0:T(8,128)} %param.9) | copy-start | bytes 122884
  22.9 6.9 %copy-start.4 = (s32[48,2]{0,1:T(2,128)S(1)}, s32[48,2]{0,1:T(2,128)}, u32[]{:S(2)}) copy-start(s32[48,2]{0,1:T(2,128)} %param.10) | copy-start | bytes 1156
  22.9 81.3 %collective-permute-start.5 = (bf16[384,2048]{1,0:T(8,128)(2,1)}, bf16[384,2048]{1,0:T(8,128)(2,1)S(1)}, u32[]{:S(2)}, u32[]{:S(2)}) collective-permute-start(bf16[384,2048]{1,0:T(8,128)(2,1)} %get-tuple-element.20), channel_id=1, source_target_pairs={{1,0},{2,1},{3,2},{4,3},{5,4},{6,5},{7,6},{8,7},{9,8},{10,9},{11,1... | collective-permute-start | bytes 4718600 | tf_op jit(solution)/shard_map/ppermute | solution.py:204
  25.1 48.1 %collective-permute-start.6 = (bf16[4,128,128]{2,1,0:T(8,128)(2,1)}, bf16[4,128,128]{2,1,0:T(8,128)(2,1)}, u32[]{:S(2)}, u32[]{:S(2)}) collective-permute-start(bf16[4,128,128]{2,1,0:T(8,128)(2,1)} %param.13), channel_id=1, source_target_pairs={{16,31},{32,46},{48,61},{64,76},{80,91},{96,106},{112,121},{128,13... | collective-permute-start | bytes 393224 | tf_op jit(solution)/shard_map/ppermute | solution.py:213
  36.1 61.9 %collective-permute-start.2 = (bf16[384,4]{1,0:T(8,128)(2,1)}, bf16[384,4]{1,0:T(8,128)(2,1)}, u32[]{:S(2)}, u32[]{:S(2)}) collective-permute-start(bf16[384,4]{1,0:T(8,128)(2,1)} %copy.13), channel_id=1, source_target_pairs={{0,1},{1,2},{2,3},{3,4},{4,5},{5,6},{6,7},{7,8},{8,9},{9,10},{10,1... | collective-permute-start | bytes 9224 | tf_op jit(solution)/shard_map/ppermute | solution.py:220
  41.8 57.4 %collective-permute-start.4 = (bf16[384,4]{1,0:T(8,128)(2,1)}, bf16[384,4]{1,0:T(8,128)(2,1)}, u32[]{:S(2)}, u32[]{:S(2)}) collective-permute-start(bf16[384,4]{1,0:T(8,128)(2,1)} %copy.14), channel_id=1, source_target_pairs={{1,0},{2,1},{3,2},{4,3},{5,4},{6,5},{7,6},{8,7},{9,8},{10,9},{11,1... | collective-permute-start | bytes 9224 | tf_op jit(solution)/shard_map/ppermute | solution.py:221
  98.0 10.0 %copy-start.2 = (bf16[1280,2048]{1,0:T(8,128)(2,1)}, bf16[1280,2048]{1,0:T(8,128)(2,1)S(1)}, u32[]{:S(2)}) copy-start(bf16[1280,2048]{1,0:T(8,128)(2,1)S(1)} %get-tuple-element.14) | copy-start | bytes 15728644
  130.0 31.8 %copy-start.6 = (pred[48]{0:T(512)(128)(4,1)S(1)}, pred[48]{0:T(512)(128)(4,1)}, u32[]{:S(2)}) copy-start(pred[48]{0:T(512)(128)(4,1)} %get-tuple-element.7) | copy-start | bytes 148
  130.0 31.9 %copy-start.5 = (pred[48]{0:T(512)(128)(4,1)S(1)}, pred[48]{0:T(512)(128)(4,1)}, u32[]{:S(2)}) copy-start(pred[48]{0:T(512)(128)(4,1)} %get-tuple-element.34) | copy-start | bytes 148
  130.0 34.5 %copy-start.7 = (pred[48]{0:T(512)(128)(4,1)S(1)}, pred[48]{0:T(512)(128)(4,1)}, u32[]{:S(2)}) copy-start(pred[48]{0:T(512)(128)(4,1)} %get-tuple-element.17) | copy-start | bytes 148
  130.0 34.5 %copy-start.8 = (pred[48]{0:T(512)(128)(4,1)S(1)}, pred[48]{0:T(512)(128)(4,1)}, u32[]{:S(2)}) copy-start(pred[48]{0:T(512)(128)(4,1)} %iota_compare_fusion) | copy-start | bytes 148
Sparse Core Ops, SparseCore 0:
  74.9 33.3 all-gather.1

commit v5 on v3

--- a/solution.py
+++ b/solution.py
@@ -21,10 +21,21 @@
     return array
 
 
-def gram_kernel(shares, rel_ref, ext_ref, out_ref):
+def gram_kernel(shares, rel_ref, before_ref, local_ref, after_ref, out_ref, ext_ref, sems):
     block = out_ref.shape[-1]
     slots = out_ref.shape[-3]
     rows = out_ref.shape[-2]
+    width = before_ref.shape[0]
+    middle = local_ref.shape[0]
+    copies = [
+        pltpu.make_async_copy(local_ref, ext_ref.at[pl.ds(width, middle)], sems.at[0]),
+        pltpu.make_async_copy(before_ref, ext_ref.at[pl.ds(0, width)], sems.at[1]),
+        pltpu.make_async_copy(after_ref, ext_ref.at[pl.ds(width + middle, width)], sems.at[2]),
+    ]
+    for cp in copies:
+        cp.start()
+    for cp in copies:
+        cp.wait()
 
     def body(s, carry):
         ra = rel_ref[2 * s]
@@ -41,27 +52,29 @@
     lax.fori_loop(0, slots, body, 0)
 
 
-def pair_grams(relative, extended, shares, block):
+def pair_grams(relative, before, local, after, shares, block):
     slots = relative.shape[0]
     rows = block // shares
-    pix_local = extended.shape[1]
+    pix_local = local.shape[1]
+    ext_rows = before.shape[0] + local.shape[0] + after.shape[0]
     flat = relative.reshape(-1).astype(jnp.int32)
     return pl.pallas_call(
         lambda *refs: gram_kernel(shares, *refs),
         out_shape=jax.ShapeDtypeStruct((2, 4, 2, slots, rows, block), jnp.float32),
-        in_specs=[
-            pl.BlockSpec(memory_space=pltpu.SMEM),
-            pl.BlockSpec(memory_space=pltpu.VMEM),
+        in_specs=[pl.BlockSpec(memory_space=pltpu.SMEM)]
+        + [pl.BlockSpec(memory_space=pl.ANY)] * 3,
+        out_specs=pl.BlockSpec(memory_space=pltpu.VMEM),
+        scratch_shapes=[
+            pltpu.VMEM((ext_rows, pix_local), local.dtype),
+            pltpu.SemaphoreType.DMA((3,)),
         ],
-        out_specs=pl.BlockSpec(memory_space=pltpu.VMEM),
         compiler_params=pltpu.CompilerParams(vmem_limit_bytes=48 * 1024 * 1024),
         cost_estimate=pl.CostEstimate(
             flops=2 * slots * block * block * pix_local,
             transcendentals=0,
-            bytes_accessed=extended.size * 2 + slots * block * block * 4,
-        ),
-    )(flat, extended)
-
+            bytes_accessed=ext_rows * pix_local * 2 + slots * block * block * 4,
+        ),
+    )(flat, before, local, after)
 
 MESH = pl.DeviceIdType.MESH
 
@@ -202,11 +215,9 @@
     down = [(j, i) for i, j in up]
     raw_before = lax.ppermute(images[local_rows - width :], "ion", up)
     raw_after = lax.ppermute(images[:width], "ion", down)
-    offset = lax.axis_index("pix") * rows
-    piece = lax.dynamic_slice_in_dim(adduct, offset, rows, 1)
-    lookup_tables = lax.all_gather(
-        lax.all_gather(piece, "ion", axis=0, tiled=True), "pix", axis=1, tiled=True
-    )
+    me_pix = lax.axis_index("pix")
+    offset = me_pix * rows
+    lookup_tables = lax.all_gather(adduct, "ion", axis=0, tiled=True)
     padded = extended_2(images, (("pix", 1),), 2)
     smoothed = smooth_rows(padded, stencil)
     local_squares = row_squares(smoothed)
@@ -219,14 +230,13 @@
     after = smooth_rows(
         jnp.concatenate([edge_after[:, :2], raw_after, edge_after[:, 2:]], axis=1), stencil
     )
-    extended = jnp.concatenate([before, smoothed, after], axis=0)
     squares = jnp.concatenate([row_squares(before), local_squares, row_squares(after)])
     pixel_count = pix_local * shares
     first = lax.axis_index("ion") * local_blocks
     slots = pairs.shape[0]
     relative = pairs - first + REACH
 
-    grams = pair_grams(relative, extended, shares, block)
+    grams = pair_grams(relative, before, smoothed, after, shares, block)
     gram, energy_sum = scatter_grams(grams, squares.reshape(-1, block))
     inverse = 1.0 / jnp.sqrt(energy_sum.reshape(-1) / pixel_count + 1e-06)
     inv_blocks = inverse.reshape(local_blocks + 2 * REACH, block)

time: 217 us -> 147 us (0.68)
  blocking collectives: 71.2 us -> 0 us
    all_gather x1 -> x0, blocking collectives: 71.2 us -> none  [on_device(): lax.all_gather(piece, 'ion', axis=0, tiled=True)]
    concatenate x1, other arithmetic: 4.05 us -> 0.03 us  [on_device(): edges = jnp.concatenate([padded[:, :2], padded[:, pix_local + 2:]], axis=1)]
    unnamed x11 -> x19, local copies, waits for them, and re-layouts: 5.75 us -> 4.67 us
  transfers between devices with their start and end apart: 7 -> 7, of which waited for: 0 -> 0; matrix products, arithmetic and copies ran while one was open for 24% -> 33% of each run, Pallas kernels for 23% -> 35%
where the time goes in v5:
time: 147 us; the launch traced here: 146 us
  Pallas kernels  51.3 us (35%)
  other arithmetic  34.1 us (23%)
  starting transfers between devices  24.1 us (16%)
  local copies, waits for them, and re-layouts  20.6 us (14%)
  between operations  14.9 us (10%)
    pallas_call x1, Pallas kernels, scatter_grams(): pl.pallas_call(scatter_kernel, out_shape=(jax.ShapeDtypeStruct(part, f32)...  32 us
    reduce_sum x3, other arithmetic, row_squares(): return jnp.sum(values * values, axis=1)  31.7 us
    pallas_call x1, Pallas kernels, pair_grams(): pl.pallas_call(lambda *refs: gram_kernel(shares, *refs), out_shape=jax.Sh...  19.3 us
    ppermute x1, starting transfers between devices, on_device(): edge_after = lax.ppermute(edges[:width], 'ion', down)  7.52 us
    ppermute x1, starting transfers between devices, on_device(): raw_after = lax.ppermute(images[:width], 'ion', down)  5.78 us
    unnamed x19, local copies, waits for them, and re-layouts  4.67 us
    slice x1, local copies, waits for them, and re-layouts, on_device(): raw_after = lax.ppermute(images[:width], 'ion', down)  4.21 us
    ppermute x1, starting transfers between devices, on_device(): raw_before = lax.ppermute(images[local_rows - width:], 'ion', up)  3.83 us
  transfers between devices with their start and end apart: 7, of which 0 were waited for; matrix products, arithmetic and copies ran while one was open for 33% of the time, Pallas kernels for 35%

profile of v5, /device:TPU:16, one launch (start us, length us, event | category | flops | bytes accessed | tf_op | source)
XLA Modules:
  0.0 146.3 jit_solution(16013207442569608738)
XLA Ops:
  7.2 0.0 copy-start
  7.2 0.0 all-gather.2.cloned.1.call-start
  7.2 2.0 %fusion.22 = (bf16[1280,2]{1,0:T(8,128)(2,1)}, bf16[1280,2]{1,0:T(8,128)(2,1)}) fusion(bf16[1280,2048]{1,0:T(8,128)(2,1)} %param.8), kind=kLoop, calls=%fused_computation.66 | loop fusion | bytes 20480 | tf_op jit(solution)/shard_map/slice | solution.py:16
  9.3 1.3 collective-permute-start.1
  10.5 3.8 %collective-permute-start = (bf16[1280,2]{1,0:T(8,128)(2,1)}, bf16[1280,2]{1,0:T(8,128)(2,1)}, u32[]{:S(2)}, u32[]{:S(2)}) collective-permute-start(bf16[1280,2]{1,0:T(8,128)(2,1)} %get-tuple-element.21), channel_id=1, source_target_pairs={{0,16},{16,32},{32,48},{48,64},{64,80},{80,96},{96,112},{112,128},... | collective-permute-start | bytes 15368 | tf_op jit(solution)/shard_map/ppermute | solution.py:18
  14.3 0.0 all-gather.2.cloned.1.call-update
  14.3 0.0 copy-start.2
  14.4 4.2 %fusion.21 = (bf16[384,2048]{1,0:T(8,128)(2,1)}, bf16[384,2048]{1,0:T(8,128)(2,1)}) fusion(bf16[1280,2048]{1,0:T(8,128)(2,1)} %param.8), kind=kLoop, calls=%fused_computation.65 | loop fusion | bytes 6291456 | tf_op jit(solution)/shard_map/slice | solution.py:217
  18.6 3.8 %collective-permute-start.3 = (bf16[384,2048]{1,0:T(8,128)(2,1)}, bf16[384,2048]{1,0:T(8,128)(2,1)S(1)}, u32[]{:S(2)}, u32[]{:S(2)}) collective-permute-start(bf16[384,2048]{1,0:T(8,128)(2,1)} %get-tuple-element.20), channel_id=1, source_target_pairs={{0,1},{1,2},{2,3},{3,4},{4,5},{5,6},{6,7},{7,8},{8,9},{9,10},{10,1... | collective-permute-start | bytes 4718600 | tf_op jit(solution)/shard_map/ppermute | solution.py:216
  22.4 0.0 copy-start.3
  22.4 0.0 copy-start.4
  22.4 5.8 %collective-permute-start.5 = (bf16[384,2048]{1,0:T(8,128)(2,1)}, bf16[384,2048]{1,0:T(8,128)(2,1)S(1)}, u32[]{:S(2)}, u32[]{:S(2)}) collective-permute-start(bf16[384,2048]{1,0:T(8,128)(2,1)} %get-tuple-element.19), channel_id=1, source_target_pairs={{1,0},{2,1},{3,2},{4,3},{5,4},{6,5},{7,6},{8,7},{9,8},{10,9},{11,1... | collective-permute-start | bytes 4718600 | tf_op jit(solution)/shard_map/ppermute | solution.py:217
  28.2 0.0 copy-done.2
  28.2 2.7 %constant_dynamic-update-slice_fusion.1 = bf16[1280,2050]{1,0:T(8,128)(2,1)} fusion(bf16[1280,2048]{1,0:T(8,128)(2,1)S(1)} %copy-done.2), kind=kLoop, calls=%fused_computation.49 | loop fusion | bytes 10485760
  31.0 0.0 copy-done.3
  31.0 0.0 copy-done.4
  31.0 0.5 compare_and_fusion.1
  31.6 0.0 copy-done
  31.6 0.8 gather_fusion
  32.4 0.5 and_bitcast_fusion
  32.9 0.6 pad_clamp_fusion
  34.2 0.5 iota_compare_fusion
  34.7 0.1 copy.10
  34.8 0.1 reshape.33.refs_0_
  34.9 0.0 collective-permute-done.1
  34.9 0.2 copy.12
  35.1 0.0 collective-permute-done
  35.1 1.1 copy.11
  36.3 0.8 copy.13
  37.1 1.9 %collective-permute-start.2 = (bf16[384,4]{1,0:T(8,128)(2,1)}, bf16[384,4]{1,0:T(8,128)(2,1)}, u32[]{:S(2)}, u32[]{:S(2)}) collective-permute-start(bf16[384,4]{1,0:T(8,128)(2,1)} %copy.13), channel_id=1, source_target_pairs={{0,1},{1,2},{2,3},{3,4},{4,5},{5,6},{6,7},{7,8},{8,9},{9,10},{10,1... | collective-permute-start | bytes 9224 | tf_op jit(solution)/shard_map/ppermute | solution.py:225
  39.0 0.8 copy.14
  39.8 7.5 %collective-permute-start.4 = (bf16[384,4]{1,0:T(8,128)(2,1)}, bf16[384,4]{1,0:T(8,128)(2,1)S(1)}, u32[]{:S(2)}, u32[]{:S(2)}) collective-permute-start(bf16[384,4]{1,0:T(8,128)(2,1)} %copy.14), channel_id=1, source_target_pairs={{1,0},{2,1},{3,2},{4,3},{5,4},{6,5},{7,6},{8,7},{9,8},{10,9},{11,1... | collective-permute-start | bytes 9224 | tf_op jit(solution)/shard_map/ppermute | solution.py:226
  47.3 0.8 constant_dynamic-update-slice_fusion
  48.1 24.3 %multiply_reduce_fusion = (f32[1280]{0:T(1024)S(1)}, bf16[1280,2048]{1,0:T(8,128)(2,1)}) fusion(bf16[1280,2050]{1,0:T(8,128)(2,1)} %constant_dynamic-update-slice_fusion, f32[2048]{0:T(1024)S(1)} %bitcast.34, f32[2048]{0:T(1024)S(1)} %bitcast.37, bf16[1280,2048]{1,0:T(8,128)(2,1)} %param.8, f32[2048]{0:T(1024)S(1)} %bitcast.28, ...), kind=kLoop, calls=%fused_computation.4 | loop fusion | flops 62913280 | bytes 21022720 | tf_op jit(solution)/shard_map/reduce_sum | solution.py:203
  72.4 0.0 collective-permute-done.2
  72.4 1.1 fusion.24
  73.5 0.0 collective-permute-done.4
  73.5 0.1 fusion.23
  73.6 0.0 collective-permute-done.3
  73.6 3.7 %multiply_reduce_fusion.2 = (f32[384]{0:T(512)S(1)}, bf16[384,2048]{1,0:T(8,128)(2,1)S(1)}) fusion(bf16[384,2]{1,0:T(8,128)(2,1)S(1)} %get-tuple-element.26, bf16[384,2048]{1,0:T(8,128)(2,1)S(1)} %collective-permute-done.3, f32[2048]{0:T(1024)S(1)} %bitcast.35, f32[2048]{0:T(1024)S(1)} %bitcast.38, f32[2048]{0:T(1024)S(1)} %bitcast.29, ...), kind=kLoop, calls=%fused_computation.11 | loop fusion | flops 23592576 | bytes 3191296 | tf_op jit(solution)/shard_map/reduce_sum | solution.py:203
  77.3 0.0 collective-permute-done.5
  77.3 3.7 %multiply_reduce_fusion.1 = (f32[384]{0:T(512)S(1)}, bf16[384,2048]{1,0:T(8,128)(2,1)S(1)}) fusion(bf16[384,2]{1,0:T(8,128)(2,1)S(1)} %get-tuple-element.24, bf16[384,2048]{1,0:T(8,128)(2,1)S(1)} %collective-permute-done.5, f32[2048]{0:T(1024)S(1)} %bitcast.36, f32[2048]{0:T(1024)S(1)} %bitcast.39, f32[2048]{0:T(1024)S(1)} %bitcast.30, ...), kind=kLoop, calls=%fused_computation.10 | loop fusion | flops 23592576 | bytes 3191296 | tf_op jit(solution)/shard_map/reduce_sum | solution.py:203
  81.1 19.3 %shard_map.77.g_ref = f32[2,4,2,48,8,128]{5,4,3,2,1,0:T(8,128)} custom-call(s32[96]{0:T(128)S(1)} %reshape.33.refs_0_, bf16[384,2048]{1,0:T(8,128)(2,1)S(1)} %get-tuple-element.12.refs_1_, bf16[1280,2048]{1,0:T(8,128)(2,1)} %get-tuple-element.14.refs_2_, bf16[384,2048]{1,0:T(8,128)(2,1)S(1)} %get-tuple-element.16.refs_3_), custom_call_target="tpu_custom_call" | custom-call | flops 3221225472 | bytes 11534336 | tf_op jit(solution)/shard_map/pallas_call | solution.py:61
  100.3 0.0 copy-start.1
  100.3 1.9 %copy-done.1 = f32[2,4,2,48,8,128]{5,4,3,2,1,0:T(8,128)S(1)} copy-done((f32[2,4,2,48,8,128]{5,4,3,2,1,0:T(8,128)S(1)}, f32[2,4,2,48,8,128]{5,4,3,2,1,0:T(8,128)}, u32[]{:S(2)}) %copy-start.1) | copy-done | bytes 3145752
  102.2 0.0 copy-start.6
  102.2 0.0 copy-start.5
  102.2 0.0 copy-start.7
  102.2 0.0 copy-start.8
  102.2 32.0 %shard_map.78 = (f32[48,8,128]{2,1,0:T(8,128)S(1)}, f32[16,128]{1,0:T(8,128)S(1)}) custom-call(f32[2,4,2,48,8,128]{5,4,3,2,1,0:T(8,128)S(1)} %copy-done.1, f32[16,128]{1,0:T(8,128)S(1)} %maximum_bitcast_fusion.e_ref), custom_call_target="tpu_custom_call" | custom-call | tf_op jit(solution)/shard_map/pallas_call | solution.py:166
  134.3 0.6 gather_fusion.3
  134.9 0.6 gather_fusion.2
  135.4 0.0 copy-done.6
  135.4 0.1 dynamic-slice_select_fusion
  135.5 0.0 copy-done.5
  135.5 0.1 broadcast_select_fusion
  135.6 0.0 all-gather.2.cloned.1.call-done
  135.6 2.6 %gather_fusion.1 = bf16[48,128,128]{2,1,0:T(8,128)(2,1)S(1)} fusion(bf16[64,128,128]{2,1,0:T(8,128)(2,1)} %all-gather.2.cloned.1.call-done, s32[1024]{0:T(1024)} %pad_clamp_fusion), kind=kCustom, calls=%fused_computation.3 | custom fusion | bytes 3145920 | tf_op jit(solution)/shard_map/jit(_take)/gather | solution.py:249
  138.2 0.0 copy-done.7
  138.2 0.0 copy-done.8
  138.2 1.2 fusion.11
  (8 shorter events, 0.1 us)
Async XLA Ops:
  7.2 24.4 %copy-start = (s32[160]{0:T(256)S(1)}, s32[160]{0:T(256)}, u32[]{:S(2)}) copy-start(s32[160]{0:T(256)} %param.12) | copy-start | bytes 1924
  7.2 128.4 %all-gather.2.cloned.1.call-start = ((), (), s32[]{:S(2)}) async-start(), calls=%async_computation | async-start | bytes 2228224 | tf_op jit(solution)/shard_map/all_gather | solution.py:220
  9.3 25.7 %collective-permute-start.1 = (bf16[1280,2]{1,0:T(8,128)(2,1)}, bf16[1280,2]{1,0:T(8,128)(2,1)S(1)}, u32[]{:S(2)}, u32[]{:S(2)}) collective-permute-start(bf16[1280,2]{1,0:T(8,128)(2,1)} %get-tuple-element.22), channel_id=1, source_target_pairs={{16,0},{32,16},{48,32},{64,48},{80,64},{96,80},{112,96},{128,112},... | collective-permute-start | bytes 15368 | tf_op jit(solution)/shard_map/ppermute | solution.py:19
  10.5 24.6 %collective-permute-start = (bf16[1280,2]{1,0:T(8,128)(2,1)}, bf16[1280,2]{1,0:T(8,128)(2,1)}, u32[]{:S(2)}, u32[]{:S(2)}) collective-permute-start(bf16[1280,2]{1,0:T(8,128)(2,1)} %get-tuple-element.21), channel_id=1, source_target_pairs={{0,16},{16,32},{32,48},{48,64},{64,80},{80,96},{96,112},{112,128},... | collective-permute-start | bytes 15368 | tf_op jit(solution)/shard_map/ppermute | solution.py:18
  14.3 13.9 %copy-start.2 = (bf16[1280,2048]{1,0:T(8,128)(2,1)S(1)}, bf16[1280,2048]{1,0:T(8,128)(2,1)}, u32[]{:S(2)}) copy-start(bf16[1280,2048]{1,0:T(8,128)(2,1)} %param.8) | copy-start | bytes 15728644
  18.6 55.0 %collective-permute-start.3 = (bf16[384,2048]{1,0:T(8,128)(2,1)}, bf16[384,2048]{1,0:T(8,128)(2,1)S(1)}, u32[]{:S(2)}, u32[]{:S(2)}) collective-permute-start(bf16[384,2048]{1,0:T(8,128)(2,1)} %get-tuple-element.20), channel_id=1, source_target_pairs={{0,1},{1,2},{2,3},{3,4},{4,5},{5,6},{6,7},{7,8},{8,9},{9,10},{10,1... | collective-permute-start | bytes 4718600 | tf_op jit(solution)/shard_map/ppermute | solution.py:216
  22.4 8.6 %copy-start.3 = (f32[5,2048]{1,0:T(8,128)S(1)}, f32[5,2048]{1,0:T(8,128)}, u32[]{:S(2)}) copy-start(f32[5,2048]{1,0:T(8,128)} %param.9) | copy-start | bytes 122884
  22.4 8.6 %copy-start.4 = (s32[48,2]{0,1:T(2,128)S(1)}, s32[48,2]{0,1:T(2,128)}, u32[]{:S(2)}) copy-start(s32[48,2]{0,1:T(2,128)} %param.10) | copy-start | bytes 1156
  22.4 54.9 %collective-permute-start.5 = (bf16[384,2048]{1,0:T(8,128)(2,1)}, bf16[384,2048]{1,0:T(8,128)(2,1)S(1)}, u32[]{:S(2)}, u32[]{:S(2)}) collective-permute-start(bf16[384,2048]{1,0:T(8,128)(2,1)} %get-tuple-element.19), channel_id=1, source_target_pairs={{1,0},{2,1},{3,2},{4,3},{5,4},{6,5},{7,6},{8,7},{9,8},{10,9},{11,1... | collective-permute-start | bytes 4718600 | tf_op jit(solution)/shard_map/ppermute | solution.py:217
  37.1 35.4 %collective-permute-start.2 = (bf16[384,4]{1,0:T(8,128)(2,1)}, bf16[384,4]{1,0:T(8,128)(2,1)}, u32[]{:S(2)}, u32[]{:S(2)}) collective-permute-start(bf16[384,4]{1,0:T(8,128)(2,1)} %copy.13), channel_id=1, source_target_pairs={{0,1},{1,2},{2,3},{3,4},{4,5},{5,6},{6,7},{7,8},{8,9},{9,10},{10,1... | collective-permute-start | bytes 9224 | tf_op jit(solution)/shard_map/ppermute | solution.py:225
  39.8 33.7 %collective-permute-start.4 = (bf16[384,4]{1,0:T(8,128)(2,1)}, bf16[384,4]{1,0:T(8,128)(2,1)S(1)}, u32[]{:S(2)}, u32[]{:S(2)}) collective-permute-start(bf16[384,4]{1,0:T(8,128)(2,1)} %copy.14), channel_id=1, source_target_pairs={{1,0},{2,1},{3,2},{4,3},{5,4},{6,5},{7,6},{8,7},{9,8},{10,9},{11,1... | collective-permute-start | bytes 9224 | tf_op jit(solution)/shard_map/ppermute | solution.py:226
  100.3 1.9 %copy-start.1 = (f32[2,4,2,48,8,128]{5,4,3,2,1,0:T(8,128)S(1)}, f32[2,4,2,48,8,128]{5,4,3,2,1,0:T(8,128)}, u32[]{:S(2)}) copy-start(f32[2,4,2,48,8,128]{5,4,3,2,1,0:T(8,128)} %shard_map.77.g_ref) | copy-start | bytes 9437188
  102.2 33.2 %copy-start.6 = (pred[48]{0:T(512)(128)(4,1)S(1)}, pred[48]{0:T(512)(128)(4,1)}, u32[]{:S(2)}) copy-start(pred[48]{0:T(512)(128)(4,1)} %get-tuple-element.7) | copy-start | bytes 148
  102.2 33.3 %copy-start.5 = (pred[48]{0:T(512)(128)(4,1)S(1)}, pred[48]{0:T(512)(128)(4,1)}, u32[]{:S(2)}) copy-start(pred[48]{0:T(512)(128)(4,1)} %get-tuple-element.34) | copy-start | bytes 148
  102.2 36.0 %copy-start.7 = (pred[48]{0:T(512)(128)(4,1)S(1)}, pred[48]{0:T(512)(128)(4,1)}, u32[]{:S(2)}) copy-start(pred[48]{0:T(512)(128)(4,1)} %get-tuple-element.17) | copy-start | bytes 148
  102.2 36.0 %copy-start.8 = (pred[48]{0:T(512)(128)(4,1)S(1)}, pred[48]{0:T(512)(128)(4,1)}, u32[]{:S(2)}) copy-start(pred[48]{0:T(512)(128)(4,1)} %iota_compare_fusion) | copy-start | bytes 148
Sparse Core Ops, SparseCore 0:
  14.5 117.4 all-gather.1

commit v6 on v5

--- a/solution.py
+++ b/solution.py
@@ -217,7 +217,19 @@
     raw_after = lax.ppermute(images[:width], "ion", down)
     me_pix = lax.axis_index("pix")
     offset = me_pix * rows
-    lookup_tables = lax.all_gather(adduct, "ion", axis=0, tiled=True)
+    me_pix = lax.axis_index("pix")
+    me_ion = lax.axis_index("ion")
+    per_index = adduct.shape[0]
+    half = per_index // 2
+    by_ion = lax.all_gather(adduct[:half], "ion", axis=0, tiled=True)
+    turn = [
+        (p * ions + j, p * ions + (j - p) % ions)
+        for j in range(ions)
+        for p in range(1, shares)
+    ]
+    fetched = lax.ppermute(adduct[half:], ("pix", "ion"), turn)
+    by_pix = lax.all_gather(jnp.where(me_pix == 0, adduct[half:], fetched), "pix", axis=0, tiled=True)
+    lookup_tables = jnp.concatenate([by_ion, by_pix], axis=0)
     padded = extended_2(images, (("pix", 1),), 2)
     smoothed = smooth_rows(padded, stencil)
     local_squares = row_squares(smoothed)
@@ -246,6 +258,12 @@
     )
     inv_right = jnp.take(inv_blocks, relative[:, 1], axis=0)
     rules = jnp.take(rule_of_block, pairs[:, 1], axis=0)
+    group, within = rules // per_index, rules % per_index
+    rules = jnp.where(
+        within < half,
+        group * half + within,
+        ions * half + ((group - me_ion) % ions) * half + within - half,
+    )
     matrices = jnp.take(lookup_tables, rules, axis=0)
     coloc = (gram * inv_left[:, :, None] * inv_right[:, None, :] / pixel_count).astype(jnp.bfloat16)
     scores = jnp.einsum("src,scd->srd", coloc, matrices, preferred_element_type=jnp.float32)

time: 147 us -> 188 us (1.28); the launches traced: 146 us -> 185 us
  waiting for transfers between devices: 0.03 us -> 18.1 us
  Pallas kernels: 51.3 us -> 60.3 us
  other arithmetic: 34.1 us -> 40.1 us
  local copies, waits for them, and re-layouts: 20.6 us -> 22.8 us
    all_gather x1 -> x2, waiting for transfers between devices: 0.01 us -> 18.1 us  [the longest x1 18.1 us: on_device(): by_ion = lax.all_gather(adduct[:half], 'ion', axis=0, tiled=True)]
    pallas_call x1, Pallas kernels: 32 us -> 41.1 us  [scatter_grams(): pl.pallas_call(scatter_kernel, out_shape=(jax.ShapeDtypeStruct(part, f32)...]
    unnamed x19 -> x37, local copies, waits for them, and re-layouts: 4.67 us -> 4.75 us
  transfers between devices with their start and end apart: 7 -> 9, of which waited for: 0 -> 1; matrix products, arithmetic and copies ran while one was open for 33% -> 30% of each run, Pallas kernels for 35% -> 33%
where the time goes in v6:
time: 188 us; the launch traced here: 185 us
  Pallas kernels  60.3 us (32%)
  other arithmetic  40.1 us (21%)
  starting transfers between devices  25.6 us (14%)
  local copies, waits for them, and re-layouts  22.8 us (12%)
  waiting for transfers between devices  18.1 us (10%)
  between operations  15.1 us (8%)
  matrix products  2.65 us (1%)
    pallas_call x1, Pallas kernels, scatter_grams(): pl.pallas_call(scatter_kernel, out_shape=(jax.ShapeDtypeStruct(part, f32)...  41.1 us
    reduce_sum x3, other arithmetic, row_squares(): return jnp.sum(values * values, axis=1)  33.1 us
    pallas_call x1, Pallas kernels, pair_grams(): pl.pallas_call(lambda *refs: gram_kernel(shares, *refs), out_shape=jax.Sh...  19.3 us
    all_gather x1, waiting for transfers between devices, on_device(): by_ion = lax.all_gather(adduct[:half], 'ion', axis=0, tiled=True)  18.1 us
    ppermute x1, starting transfers between devices, on_device(): edge_after = lax.ppermute(edges[:width], 'ion', down)  7.52 us
    ppermute x1, starting transfers between devices, on_device(): raw_after = lax.ppermute(images[:width], 'ion', down)  5.76 us
    unnamed x37, local copies, waits for them, and re-layouts  4.75 us
    slice x1, local copies, waits for them, and re-layouts, on_device(): raw_after = lax.ppermute(images[:width], 'ion', down)  4.16 us
  transfers between devices with their start and end apart: 9, of which 1 were waited for; matrix products, arithmetic and copies ran while one was open for 30% of the time, Pallas kernels for 33%

profile of v6, /device:TPU:16, one launch (start us, length us, event | category | flops | bytes accessed | tf_op | source)
XLA Modules:
  0.0 184.6 jit_solution(10027665097930326646)
XLA Ops:
  7.2 0.0 copy-start
  7.2 0.0 all-gather.5.cloned.1.call-start
  7.2 2.0 %fusion.26 = (bf16[1280,2]{1,0:T(8,128)(2,1)}, bf16[1280,2]{1,0:T(8,128)(2,1)}) fusion(bf16[1280,2048]{1,0:T(8,128)(2,1)} %param.8), kind=kLoop, calls=%fused_computation.81 | loop fusion | bytes 20480 | tf_op jit(solution)/shard_map/slice | solution.py:16
  9.3 1.3 collective-permute-start.1
  10.5 3.8 %collective-permute-start = (bf16[1280,2]{1,0:T(8,128)(2,1)}, bf16[1280,2]{1,0:T(8,128)(2,1)}, u32[]{:S(2)}, u32[]{:S(2)}) collective-permute-start(bf16[1280,2]{1,0:T(8,128)(2,1)} %get-tuple-element.21), channel_id=1, source_target_pairs={{0,16},{16,32},{32,48},{48,64},{64,80},{80,96},{96,112},{112,128},... | collective-permute-start | bytes 15368 | tf_op jit(solution)/shard_map/ppermute | solution.py:18
  14.3 1.5 slice.150
  15.8 1.4 collective-permute-start.6
  17.2 4.2 %fusion.25 = (bf16[384,2048]{1,0:T(8,128)(2,1)}, bf16[384,2048]{1,0:T(8,128)(2,1)}) fusion(bf16[1280,2048]{1,0:T(8,128)(2,1)} %param.8), kind=kLoop, calls=%fused_computation.80 | loop fusion | bytes 6291456 | tf_op jit(solution)/shard_map/slice | solution.py:217
  21.4 3.8 %collective-permute-start.3 = (bf16[384,2048]{1,0:T(8,128)(2,1)}, bf16[384,2048]{1,0:T(8,128)(2,1)S(1)}, u32[]{:S(2)}, u32[]{:S(2)}) collective-permute-start(bf16[384,2048]{1,0:T(8,128)(2,1)} %get-tuple-element.20), channel_id=1, source_target_pairs={{0,1},{1,2},{2,3},{3,4},{4,5},{5,6},{6,7},{7,8},{8,9},{9,10},{10,1... | collective-permute-start | bytes 4718600 | tf_op jit(solution)/shard_map/ppermute | solution.py:216
  25.2 0.0 copy-start.12
  25.2 0.0 copy-start.13
  25.2 5.8 %collective-permute-start.5 = (bf16[384,2048]{1,0:T(8,128)(2,1)}, bf16[384,2048]{1,0:T(8,128)(2,1)S(1)}, u32[]{:S(2)}, u32[]{:S(2)}) collective-permute-start(bf16[384,2048]{1,0:T(8,128)(2,1)} %get-tuple-element.19), channel_id=1, source_target_pairs={{1,0},{2,1},{3,2},{4,3},{5,4},{6,5},{7,6},{8,7},{9,8},{10,9},{11,1... | collective-permute-start | bytes 4718600 | tf_op jit(solution)/shard_map/ppermute | solution.py:217
  31.0 2.8 %constant_dynamic-update-slice_fusion.1 = bf16[1280,2050]{1,0:T(8,128)(2,1)} fusion(bf16[1280,2048]{1,0:T(8,128)(2,1)S(1)} %copy-done.2), kind=kLoop, calls=%fused_computation.51 | loop fusion | bytes 10485760
  33.9 0.6 compare_and_fusion.1
  34.5 0.6 pad_clamp_fusion.1
  35.1 0.0 copy-done
  35.1 0.8 gather_fusion
  35.9 0.6 and_bitcast_fusion
  36.5 0.6 pad_clamp_fusion
  37.1 0.6 pad_clamp_fusion.3
  38.3 0.5 iota_compare_fusion
  38.9 0.1 copy.10
  39.0 0.1 reshape.33.refs_0_
  39.1 0.0 collective-permute-done.1
  39.1 0.2 copy.12
  39.3 0.0 collective-permute-done
  39.3 1.1 copy.11
  40.5 0.8 copy.13
  41.3 1.9 %collective-permute-start.2 = (bf16[384,4]{1,0:T(8,128)(2,1)}, bf16[384,4]{1,0:T(8,128)(2,1)}, u32[]{:S(2)}, u32[]{:S(2)}) collective-permute-start(bf16[384,4]{1,0:T(8,128)(2,1)} %copy.13), channel_id=1, source_target_pairs={{0,1},{1,2},{2,3},{3,4},{4,5},{5,6},{6,7},{7,8},{8,9},{9,10},{10,1... | collective-permute-start | bytes 9224 | tf_op jit(solution)/shard_map/ppermute | solution.py:237
  43.2 0.8 copy.14
  44.0 7.5 %collective-permute-start.4 = (bf16[384,4]{1,0:T(8,128)(2,1)}, bf16[384,4]{1,0:T(8,128)(2,1)}, u32[]{:S(2)}, u32[]{:S(2)}) collective-permute-start(bf16[384,4]{1,0:T(8,128)(2,1)} %copy.14), channel_id=1, source_target_pairs={{1,0},{2,1},{3,2},{4,3},{5,4},{6,5},{7,6},{8,7},{9,8},{10,9},{11,1... | collective-permute-start | bytes 9224 | tf_op jit(solution)/shard_map/ppermute | solution.py:238
  51.5 0.8 constant_dynamic-update-slice_fusion
  52.3 0.0 collective-permute-done.6
  52.3 1.5 fusion.27
  53.8 0.0 all-gather.5.cloned.1.call-update
  53.9 0.0 all-gather.3.cloned.1.call-start
  53.9 25.0 %multiply_reduce_fusion = (f32[1280]{0:T(1024)}, bf16[1280,2048]{1,0:T(8,128)(2,1)}) fusion(bf16[1280,2050]{1,0:T(8,128)(2,1)} %constant_dynamic-update-slice_fusion, f32[2048]{0:T(1024)S(1)} %bitcast.34, f32[2048]{0:T(1024)S(1)} %bitcast.37, bf16[1280,2048]{1,0:T(8,128)(2,1)} %param.8, f32[2048]{0:T(1024)S(1)} %bitcast.28, ...), kind=kLoop, calls=%fused_computation.4 | loop fusion | flops 62913280 | bytes 21022720 | tf_op jit(solution)/shard_map/reduce_sum | solution.py:203
  78.9 0.0 collective-permute-done.2
  78.9 1.1 fusion.29
  80.0 0.0 collective-permute-done.4
  80.0 1.1 fusion.28
  81.1 0.0 all-gather.3.cloned.1.call-update
  81.1 0.0 copy-start.4
  81.1 0.0 copy-start.6
  81.1 0.0 copy-start.8
  81.1 0.0 copy-start.10
  81.1 0.0 collective-permute-done.3
  81.1 4.5 %multiply_reduce_fusion.2 = (f32[384]{0:T(512)S(1)}, bf16[384,2048]{1,0:T(8,128)(2,1)S(1)}) fusion(bf16[384,2]{1,0:T(8,128)(2,1)S(1)} %get-tuple-element.28, bf16[384,2048]{1,0:T(8,128)(2,1)S(1)} %collective-permute-done.3, f32[2048]{0:T(1024)} %bitcast.35, f32[2048]{0:T(1024)} %bitcast.38, f32[2048]{0:T(1024)} %bitcast.29, ...), kind=kLoop, calls=%fused_computation.11 | loop fusion | flops 23592576 | bytes 3191296 | tf_op jit(solution)/shard_map/reduce_sum | solution.py:203
  85.6 0.0 collective-permute-done.5
  85.6 0.0 copy-done.4
  85.6 0.0 copy-done.6
  85.7 3.7 %multiply_reduce_fusion.1 = (f32[384]{0:T(512)S(1)}, bf16[384,2048]{1,0:T(8,128)(2,1)S(1)}) fusion(bf16[384,2]{1,0:T(8,128)(2,1)S(1)} %get-tuple-element.26, bf16[384,2048]{1,0:T(8,128)(2,1)S(1)} %collective-permute-done.5, f32[2048]{0:T(1024)S(1)} %bitcast.36, f32[2048]{0:T(1024)S(1)} %bitcast.39, f32[2048]{0:T(1024)S(1)} %bitcast.30, ...), kind=kLoop, calls=%fused_computation.10 | loop fusion | flops 23592576 | bytes 3191296 | tf_op jit(solution)/shard_map/reduce_sum | solution.py:203
  89.4 19.3 %shard_map.77.g_ref = f32[2,4,2,48,8,128]{5,4,3,2,1,0:T(8,128)} custom-call(s32[96]{0:T(128)S(1)} %reshape.33.refs_0_, bf16[384,2048]{1,0:T(8,128)(2,1)S(1)} %get-tuple-element.12.refs_1_, bf16[1280,2048]{1,0:T(8,128)(2,1)} %get-tuple-element.14.refs_2_, bf16[384,2048]{1,0:T(8,128)(2,1)S(1)} %get-tuple-element.16.refs_3_), custom_call_target="tpu_custom_call" | custom-call | flops 3221225472 | bytes 11534336 | tf_op jit(solution)/shard_map/pallas_call | solution.py:61
  108.7 1.9 %copy-done.1 = f32[2,4,2,48,8,128]{5,4,3,2,1,0:T(8,128)S(1)} copy-done((f32[2,4,2,48,8,128]{5,4,3,2,1,0:T(8,128)S(1)}, f32[2,4,2,48,8,128]{5,4,3,2,1,0:T(8,128)}, u32[]{:S(2)}) %copy-start.1) | copy-done | bytes 3145752
  110.5 41.1 %shard_map.78 = (f32[48,8,128]{2,1,0:T(8,128)S(1)}, f32[16,128]{1,0:T(8,128)S(1)}) custom-call(f32[2,4,2,48,8,128]{5,4,3,2,1,0:T(8,128)S(1)} %copy-done.1, f32[16,128]{1,0:T(8,128)S(1)} %maximum_bitcast_fusion.e_ref), custom_call_target="tpu_custom_call" | custom-call | tf_op jit(solution)/shard_map/pallas_call | solution.py:166
  151.6 0.7 gather_fusion.3
  152.3 0.7 gather_fusion.2
  153.0 0.1 dynamic-slice_select_fusion
  153.1 0.1 broadcast_select_fusion.1
  153.2 0.0 all-gather.5.cloned.1.call-done
  153.2 18.1 %all-gather.3.cloned.1.call-done = bf16[32,128,128]{2,1,0:T(8,128)(2,1)} async-done(((bf16[2,128,128]{2,1,0:T(8,128)(2,1)}), bf16[32,128,128]{2,1,0:T(8,128)(2,1)}) %all-gather.3.cloned.1.call-update) | async-done | bytes 1048592 | tf_op jit(solution)/shard_map/all_gather | solution.py:224
  171.3 1.7 pad_maximum_fusion.1
  173.0 2.1 %gather_fusion.1 = bf16[48,128,128]{2,1,0:T(8,128)(2,1)} fusion(bf16[64,128,128]{2,1,0:T(8,128)(2,1)S(1)} %pad_maximum_fusion.1, s32[1024]{0:T(1024)} %pad_clamp_fusion), kind=kCustom, calls=%fused_computation.3 | custom fusion | bytes 3145920 | tf_op jit(solution)/shard_map/jit(_take)/gather | solution.py:267
  175.1 2.7 %fusion.11 = bf16[48,8,128]{2,1,0:T(8,128)(2,1)} fusion(bf16[48,128,128]{2,1,0:T(8,128)(2,1)} %gather_fusion.1, pred[48]{0:T(512)(128)(4,1)S(1)} %copy-done.16, f32[48,8,128]{2,1,0:T(8,128)S(1)} %get-tuple-element.5, f32[48,128]{1,0:T(8,128)S(1)} %broadcast_select_fusion.1, f32[48,8]{1,0:T(8,128)S(1)} %dynamic-slice_select_fusion, ...), kind=kOutput, calls=%fused_computation.35 | convolution fusion | flops 13664256 | bytes 1893984 | tf_op jit(solution)/shard_map/src,scd->srd/dot_general | solution.py:269
  (31 shorter events, 0.1 us)
Async XLA Ops:
  7.2 27.9 %copy-start = (s32[160]{0:T(256)S(1)}, s32[160]{0:T(256)}, u32[]{:S(2)}) copy-start(s32[160]{0:T(256)} %param.12) | copy-start | bytes 1924
  7.2 146.0 %all-gather.5.cloned.1.call-start = ((), (), s32[]{:S(2)}) async-start(), calls=%async_computation.1 | async-start | bytes 1114112 | tf_op jit(solution)/shard_map/all_gather | solution.py:231
  9.3 29.8 %collective-permute-start.1 = (bf16[1280,2]{1,0:T(8,128)(2,1)}, bf16[1280,2]{1,0:T(8,128)(2,1)S(1)}, u32[]{:S(2)}, u32[]{:S(2)}) collective-permute-start(bf16[1280,2]{1,0:T(8,128)(2,1)} %get-tuple-element.22), channel_id=1, source_target_pairs={{16,0},{32,16},{48,32},{64,48},{80,64},{96,80},{112,96},{128,112},... | collective-permute-start | bytes 15368 | tf_op jit(solution)/shard_map/ppermute | solution.py:19
  10.5 28.7 %collective-permute-start = (bf16[1280,2]{1,0:T(8,128)(2,1)}, bf16[1280,2]{1,0:T(8,128)(2,1)}, u32[]{:S(2)}, u32[]{:S(2)}) collective-permute-start(bf16[1280,2]{1,0:T(8,128)(2,1)} %get-tuple-element.21), channel_id=1, source_target_pairs={{0,16},{16,32},{32,48},{48,64},{64,80},{80,96},{96,112},{112,128},... | collective-permute-start | bytes 15368 | tf_op jit(solution)/shard_map/ppermute | solution.py:18
  15.8 15.2 %copy-start.2 = (bf16[1280,2048]{1,0:T(8,128)(2,1)S(1)}, bf16[1280,2048]{1,0:T(8,128)(2,1)}, u32[]{:S(2)}) copy-start(bf16[1280,2048]{1,0:T(8,128)(2,1)} %param.8) | copy-start | bytes 15728644
  15.8 36.5 %collective-permute-start.6 = (bf16[2,128,128]{2,1,0:T(8,128)(2,1)}, bf16[2,128,128]{2,1,0:T(8,128)(2,1)}, u32[]{:S(2)}, u32[]{:S(2)}) collective-permute-start(bf16[2,128,128]{2,1,0:T(8,128)(2,1)} %slice.150), channel_id=1, source_target_pairs={{16,31},{32,46},{48,61},{64,76},{80,91},{96,106},{112,121},{128,13... | collective-permute-start | bytes 196616 | tf_op jit(solution)/shard_map/ppermute | solution.py:230
  21.4 59.8 %collective-permute-start.3 = (bf16[384,2048]{1,0:T(8,128)(2,1)}, bf16[384,2048]{1,0:T(8,128)(2,1)S(1)}, u32[]{:S(2)}, u32[]{:S(2)}) collective-permute-start(bf16[384,2048]{1,0:T(8,128)(2,1)} %get-tuple-element.20), channel_id=1, source_target_pairs={{0,1},{1,2},{2,3},{3,4},{4,5},{5,6},{6,7},{7,8},{8,9},{9,10},{10,1... | collective-permute-start | bytes 4718600 | tf_op jit(solution)/shard_map/ppermute | solution.py:216
  25.2 8.6 %copy-start.12 = (f32[5,2048]{1,0:T(8,128)S(1)}, f32[5,2048]{1,0:T(8,128)}, u32[]{:S(2)}) copy-start(f32[5,2048]{1,0:T(8,128)} %param.9) | copy-start | bytes 122884
  25.2 8.7 %copy-start.13 = (s32[48,2]{0,1:T(2,128)S(1)}, s32[48,2]{0,1:T(2,128)}, u32[]{:S(2)}) copy-start(s32[48,2]{0,1:T(2,128)} %param.10) | copy-start | bytes 1156
  25.2 60.4 %collective-permute-start.5 = (bf16[384,2048]{1,0:T(8,128)(2,1)}, bf16[384,2048]{1,0:T(8,128)(2,1)S(1)}, u32[]{:S(2)}, u32[]{:S(2)}) collective-permute-start(bf16[384,2048]{1,0:T(8,128)(2,1)} %get-tuple-element.19), channel_id=1, source_target_pairs={{1,0},{2,1},{3,2},{4,3},{5,4},{6,5},{7,6},{8,7},{9,8},{10,9},{11,1... | collective-permute-start | bytes 4718600 | tf_op jit(solution)/shard_map/ppermute | solution.py:217
  33.8 45.1 %copy-start.3 = (f32[1,2048]{1,0:T(1,128)}, f32[1,2048]{1,0:T(1,128)S(1)}, u32[]{:S(2)}) copy-start(f32[1,2048]{1,0:T(1,128)S(1)} %get-tuple-element.30) | copy-start | bytes 24580
  33.8 45.1 %copy-start.5 = (f32[1,2048]{1,0:T(1,128)}, f32[1,2048]{1,0:T(1,128)S(1)}, u32[]{:S(2)}) copy-start(f32[1,2048]{1,0:T(1,128)S(1)} %get-tuple-element.31) | copy-start | bytes 24580
  33.8 45.1 %copy-start.7 = (f32[1,2048]{1,0:T(1,128)}, f32[1,2048]{1,0:T(1,128)S(1)}, u32[]{:S(2)}) copy-start(f32[1,2048]{1,0:T(1,128)S(1)} %get-tuple-element.32) | copy-start | bytes 24580
  33.9 45.1 %copy-start.9 = (f32[1,2048]{1,0:T(1,128)}, f32[1,2048]{1,0:T(1,128)S(1)}, u32[]{:S(2)}) copy-start(f32[1,2048]{1,0:T(1,128)S(1)} %get-tuple-element.33) | copy-start | bytes 24580
  41.3 37.6 %collective-permute-start.2 = (bf16[384,4]{1,0:T(8,128)(2,1)}, bf16[384,4]{1,0:T(8,128)(2,1)}, u32[]{:S(2)}, u32[]{:S(2)}) collective-permute-start(bf16[384,4]{1,0:T(8,128)(2,1)} %copy.13), channel_id=1, source_target_pairs={{0,1},{1,2},{2,3},{3,4},{4,5},{5,6},{6,7},{7,8},{8,9},{9,10},{10,1... | collective-permute-start | bytes 9224 | tf_op jit(solution)/shard_map/ppermute | solution.py:237
  44.0 36.0 %collective-permute-start.4 = (bf16[384,4]{1,0:T(8,128)(2,1)}, bf16[384,4]{1,0:T(8,128)(2,1)}, u32[]{:S(2)}, u32[]{:S(2)}) collective-permute-start(bf16[384,4]{1,0:T(8,128)(2,1)} %copy.14), channel_id=1, source_target_pairs={{1,0},{2,1},{3,2},{4,3},{5,4},{6,5},{7,6},{8,7},{9,8},{10,9},{11,1... | collective-permute-start | bytes 9224 | tf_op jit(solution)/shard_map/ppermute | solution.py:238
  53.9 117.4 %all-gather.3.cloned.1.call-start = ((), (), s32[]{:S(2)}) async-start(), calls=%async_computation | async-start | bytes 1114112 | tf_op jit(solution)/shard_map/all_gather | solution.py:224
  81.1 4.5 %copy-start.4 = (f32[1,2048]{1,0:T(1,128)S(1)}, f32[1,2048]{1,0:T(1,128)}, u32[]{:S(2)}) copy-start(f32[1,2048]{1,0:T(1,128)} %copy-done.3) | copy-start | bytes 24580
  81.1 4.5 %copy-start.6 = (f32[1,2048]{1,0:T(1,128)S(1)}, f32[1,2048]{1,0:T(1,128)}, u32[]{:S(2)}) copy-start(f32[1,2048]{1,0:T(1,128)} %copy-done.5) | copy-start | bytes 24580
  81.1 4.5 %copy-start.8 = (f32[1,2048]{1,0:T(1,128)S(1)}, f32[1,2048]{1,0:T(1,128)}, u32[]{:S(2)}) copy-start(f32[1,2048]{1,0:T(1,128)} %copy-done.7) | copy-start | bytes 24580
  81.1 4.5 %copy-start.10 = (f32[1,2048]{1,0:T(1,128)S(1)}, f32[1,2048]{1,0:T(1,128)}, u32[]{:S(2)}) copy-start(f32[1,2048]{1,0:T(1,128)} %copy-done.9) | copy-start | bytes 24580
  81.1 8.2 %copy-start.11 = (f32[1280]{0:T(1024)S(1)}, f32[1280]{0:T(1024)}, u32[]{:S(2)}) copy-start(f32[1280]{0:T(1024)} %get-tuple-element.13) | copy-start | bytes 15364
  108.6 1.9 %copy-start.1 = (f32[2,4,2,48,8,128]{5,4,3,2,1,0:T(8,128)S(1)}, f32[2,4,2,48,8,128]{5,4,3,2,1,0:T(8,128)}, u32[]{:S(2)}) copy-start(f32[2,4,2,48,8,128]{5,4,3,2,1,0:T(8,128)} %shard_map.77.g_ref) | copy-start | bytes 9437188
  110.5 42.5 %copy-start.15 = (pred[48]{0:T(512)(128)(4,1)S(1)}, pred[48]{0:T(512)(128)(4,1)}, u32[]{:S(2)}) copy-start(pred[48]{0:T(512)(128)(4,1)} %get-tuple-element.7) | copy-start | bytes 148
  110.5 42.6 %copy-start.14 = (pred[48]{0:T(512)(128)(4,1)S(1)}, pred[48]{0:T(512)(128)(4,1)}, u32[]{:S(2)}) copy-start(pred[48]{0:T(512)(128)(4,1)} %get-tuple-element.36) | copy-start | bytes 148
  153.2 21.9 %copy-start.16 = (pred[48]{0:T(512)(128)(4,1)S(1)}, pred[48]{0:T(512)(128)(4,1)}, u32[]{:S(2)}) copy-start(pred[48]{0:T(512)(128)(4,1)} %get-tuple-element.17) | copy-start | bytes 148
  153.2 21.9 %copy-start.17 = (pred[48]{0:T(512)(128)(4,1)S(1)}, pred[48]{0:T(512)(128)(4,1)}, u32[]{:S(2)}) copy-start(pred[48]{0:T(512)(128)(4,1)} %iota_compare_fusion) | copy-start | bytes 148
Sparse Core Ops, SparseCore 0:
  54.0 37.7 all-gather.4
  94.4 76.8 all-gather.2

commit v7 on v5

--- a/solution.py
+++ b/solution.py
@@ -21,12 +21,29 @@
     return array
 
 
-def gram_kernel(shares, rel_ref, before_ref, local_ref, after_ref, out_ref, ext_ref, sems):
+def gram_kernel(shares, rel_ref, before_ref, local_ref, after_ref, chunk_ref, out_ref, table_out,
+                ext_ref, table, sems, send_sems, recv_sems):
     block = out_ref.shape[-1]
     slots = out_ref.shape[-3]
     rows = out_ref.shape[-2]
     width = before_ref.shape[0]
     middle = local_ref.shape[0]
+    p = lax.axis_index("pix")
+
+    barrier = pltpu.get_barrier_semaphore()
+    for k in range(1, shares):
+        pl.semaphore_signal(barrier, 1, device_id={"pix": (p + k) % shares}, device_id_type=MESH)
+    pl.semaphore_wait(barrier, shares - 1)
+    sends = []
+    for k in range(1, shares):
+        dest = (p + k) % shares
+        cp = pltpu.make_async_remote_copy(
+            src_ref=chunk_ref, dst_ref=table.at[p], send_sem=send_sems.at[dest],
+            recv_sem=recv_sems.at[p], device_id={"pix": dest}, device_id_type=MESH,
+        )
+        cp.start()
+        sends.append(cp)
+
     copies = [
         pltpu.make_async_copy(local_ref, ext_ref.at[pl.ds(width, middle)], sems.at[0]),
         pltpu.make_async_copy(before_ref, ext_ref.at[pl.ds(0, width)], sems.at[1]),
@@ -38,10 +55,8 @@
         cp.wait()
 
     def body(s, carry):
-        ra = rel_ref[2 * s]
-        rb = rel_ref[2 * s + 1]
-        left = ext_ref[pl.ds(pl.multiple_of(ra * block, block), block), :]
-        right = ext_ref[pl.ds(pl.multiple_of(rb * block, block), block), :]
+        left = ext_ref[rel_ref[2 * s]]
+        right = ext_ref[rel_ref[2 * s + 1]]
         g = lax.dot_general(
             left, right, (((1,), (1,)), ((), ())), preferred_element_type=jnp.float32
         )
@@ -51,30 +66,55 @@
 
     lax.fori_loop(0, slots, body, 0)
 
-
-def pair_grams(relative, before, local, after, shares, block):
+    for cp in sends:
+        cp.wait_send()
+    for k in range(1, shares):
+        src = (p + shares - k) % shares
+        pltpu.make_async_remote_copy(
+            src_ref=chunk_ref, dst_ref=table.at[src], send_sem=send_sems.at[src],
+            recv_sem=recv_sems.at[src], device_id={"pix": src}, device_id_type=MESH,
+        ).wait_recv()
+    table_out[p] = chunk_ref[...]
+    for k in range(1, shares):
+        src = (p + shares - k) % shares
+        table_out[src] = table[src]
+
+
+def pair_grams(relative, before, local, after, chunk, shares, block):
     slots = relative.shape[0]
     rows = block // shares
     pix_local = local.shape[1]
-    ext_rows = before.shape[0] + local.shape[0] + after.shape[0]
+    ext_blocks = (before.shape[0] + local.shape[0] + after.shape[0]) // block
+    ext_rows = ext_blocks * block
     flat = relative.reshape(-1).astype(jnp.int32)
+    table_shape = (shares,) + chunk.shape
+    before, local, after = (a.reshape(-1, block, pix_local) for a in (before, local, after))
     return pl.pallas_call(
         lambda *refs: gram_kernel(shares, *refs),
-        out_shape=jax.ShapeDtypeStruct((2, 4, 2, slots, rows, block), jnp.float32),
+        out_shape=(
+            jax.ShapeDtypeStruct((2, 4, 2, slots, rows, block), jnp.float32),
+            jax.ShapeDtypeStruct(table_shape, chunk.dtype),
+        ),
         in_specs=[pl.BlockSpec(memory_space=pltpu.SMEM)]
-        + [pl.BlockSpec(memory_space=pl.ANY)] * 3,
-        out_specs=pl.BlockSpec(memory_space=pltpu.VMEM),
+        + [pl.BlockSpec(memory_space=pl.ANY)] * 3
+        + [pl.BlockSpec(memory_space=pltpu.VMEM)],
+        out_specs=(pl.BlockSpec(memory_space=pltpu.VMEM),) * 2,
         scratch_shapes=[
-            pltpu.VMEM((ext_rows, pix_local), local.dtype),
+            pltpu.VMEM((ext_blocks, block, pix_local), local.dtype),
+            pltpu.VMEM(table_shape, chunk.dtype),
             pltpu.SemaphoreType.DMA((3,)),
+            pltpu.SemaphoreType.DMA((shares,)),
+            pltpu.SemaphoreType.DMA((shares,)),
         ],
-        compiler_params=pltpu.CompilerParams(vmem_limit_bytes=48 * 1024 * 1024),
+        compiler_params=pltpu.CompilerParams(
+            collective_id=1, has_side_effects=True, vmem_limit_bytes=56 * 1024 * 1024
+        ),
         cost_estimate=pl.CostEstimate(
             flops=2 * slots * block * block * pix_local,
             transcendentals=0,
             bytes_accessed=ext_rows * pix_local * 2 + slots * block * block * 4,
         ),
-    )(flat, before, local, after)
+    )(flat, before, local, after, chunk)
 
 MESH = pl.DeviceIdType.MESH
 
@@ -217,7 +257,16 @@
     raw_after = lax.ppermute(images[:width], "ion", down)
     me_pix = lax.axis_index("pix")
     offset = me_pix * rows
-    lookup_tables = lax.all_gather(adduct, "ion", axis=0, tiled=True)
+    me_pix = lax.axis_index("pix")
+    me_ion = lax.axis_index("ion")
+    per_index = adduct.shape[0]
+    turn = [
+        (p * ions + j, p * ions + (j - p) % ions)
+        for j in range(ions)
+        for p in range(1, shares)
+    ]
+    fetched = lax.ppermute(adduct, ("pix", "ion"), turn)
+    own_turn = jnp.where(me_pix == 0, adduct, fetched)
     padded = extended_2(images, (("pix", 1),), 2)
     smoothed = smooth_rows(padded, stencil)
     local_squares = row_squares(smoothed)
@@ -236,7 +285,8 @@
     slots = pairs.shape[0]
     relative = pairs - first + REACH
 
-    grams = pair_grams(relative, before, smoothed, after, shares, block)
+    grams, lookup_tables = pair_grams(relative, before, smoothed, after, own_turn, shares, block)
+    lookup_tables = lookup_tables.reshape((-1,) + adduct.shape[1:])
     gram, energy_sum = scatter_grams(grams, squares.reshape(-1, block))
     inverse = 1.0 / jnp.sqrt(energy_sum.reshape(-1) / pixel_count + 1e-06)
     inv_blocks = inverse.reshape(local_blocks + 2 * REACH, block)
@@ -246,6 +296,7 @@
     )
     inv_right = jnp.take(inv_blocks, relative[:, 1], axis=0)
     rules = jnp.take(rule_of_block, pairs[:, 1], axis=0)
+    rules = ((rules // per_index - me_ion) % ions) * per_index + rules % per_index
     matrices = jnp.take(lookup_tables, rules, axis=0)
     coloc = (gram * inv_left[:, :, None] * inv_right[:, None, :] / pixel_count).astype(jnp.bfloat16)
     scores = jnp.einsum("src,scd->srd", coloc, matrices, preferred_element_type=jnp.float32)

time: 147 us -> 155 us (1.054)
  Pallas kernels: 51.3 us -> 75.4 us
  between operations: 14.9 us -> 1.61 us
  local copies, waits for them, and re-layouts: 20.6 us -> 14.9 us
  other arithmetic: 34.1 us -> 37.6 us
    pallas_call x1, Pallas kernels: 19.3 us -> 45.3 us  [pair_grams(): pl.pallas_call(lambda *refs: gram_kernel(shares, *refs), out_shape=(jax.S...]
    unnamed x19 -> x36, local copies, waits for them, and re-layouts: 4.67 us -> 2.29 us
    ppermute x1, starting transfers between devices: 3.78 us -> 1.74 us  [extended_2(): before = lax.ppermute(last, axis, up)]
    pallas_call x1, Pallas kernels: 32 us -> 30.2 us  [scatter_grams(): pl.pallas_call(scatter_kernel, out_shape=(jax.ShapeDtypeStruct(part, f32)...]
    select_n x0 -> x1, other arithmetic: none -> 1.59 us  [on_device(): own_turn = jnp.where(me_pix == 0, adduct, fetched)]
  transfers between devices with their start and end apart: 7 -> 7, of which waited for: 0 -> 0; matrix products, arithmetic and copies ran while one was open for 33% -> 26% of each run, Pallas kernels for 35% -> 0%
where the time goes in v7:
time: 155 us; the launch traced here: 154 us
  Pallas kernels  75.4 us (49%)
  other arithmetic  37.6 us (24%)
  starting transfers between devices  23.4 us (15%)
  local copies, waits for them, and re-layouts  14.9 us (10%)
  between operations  1.61 us (1%)
    pallas_call x1, Pallas kernels, pair_grams(): pl.pallas_call(lambda *refs: gram_kernel(shares, *refs), out_shape=(jax.S...  45.3 us
    reduce_sum x3, other arithmetic, row_squares(): return jnp.sum(values * values, axis=1)  32.9 us
    pallas_call x1, Pallas kernels, scatter_grams(): pl.pallas_call(scatter_kernel, out_shape=(jax.ShapeDtypeStruct(part, f32)...  30.2 us
    ppermute x1, starting transfers between devices, on_device(): edge_after = lax.ppermute(edges[:width], 'ion', down)  7.54 us
    ppermute x1, starting transfers between devices, on_device(): raw_after = lax.ppermute(images[:width], 'ion', down)  5.63 us
    slice x1, local copies, waits for them, and re-layouts, on_device(): raw_after = lax.ppermute(images[:width], 'ion', down)  3.93 us
    ppermute x1, starting transfers between devices, on_device(): raw_before = lax.ppermute(images[local_rows - width:], 'ion', up)  3.81 us
  transfers between devices with their start and end apart: 7, of which 0 were waited for; matrix products, arithmetic and copies ran while one was open for 26% of the time, Pallas kernels for 0%

profile of v7, /device:TPU:16, one launch (start us, length us, event | category | flops | bytes accessed | tf_op | source)
XLA Modules:
  0.0 154.2 jit_solution(10380935517459481477)
XLA Ops:
  0.6 0.0 copy-start
  0.6 1.2 fusion.26
  1.9 0.2 copy.19
  2.1 1.7 %collective-permute-start = (bf16[1280,2]{0,1:T(2,128)(2,1)S(1)}, bf16[1280,2]{0,1:T(2,128)(2,1)S(1)}, u32[]{:S(2)}, u32[]{:S(2)}) collective-permute-start(bf16[1280,2]{0,1:T(2,128)(2,1)S(1)} %copy.19), channel_id=1, source_target_pairs={{0,16},{16,32},{32,48},{48,64},{64,80},{80,96},{96,112},{112,128},... | collective-permute-start | bytes 15368 | tf_op jit(solution)/shard_map/ppermute | solution.py:18
  3.8 0.2 copy.20
  4.0 1.4 collective-permute-start.1
  5.4 3.9 %fusion.25 = (bf16[384,2048]{1,0:T(8,128)(2,1)}, bf16[384,2048]{1,0:T(8,128)(2,1)}) fusion(bf16[1280,2048]{1,0:T(8,128)(2,1)} %param.8), kind=kLoop, calls=%fused_computation.79 | loop fusion | bytes 6291456 | tf_op jit(solution)/shard_map/slice | solution.py:257
  9.4 3.8 %collective-permute-start.3 = (bf16[384,2048]{1,0:T(8,128)(2,1)}, bf16[384,2048]{1,0:T(8,128)(2,1)S(1)}, u32[]{:S(2)}, u32[]{:S(2)}) collective-permute-start(bf16[384,2048]{1,0:T(8,128)(2,1)} %get-tuple-element.24), channel_id=1, source_target_pairs={{0,1},{1,2},{2,3},{3,4},{4,5},{5,6},{6,7},{7,8},{8,9},{9,10},{10,1... | collective-permute-start | bytes 4718600 | tf_op jit(solution)/shard_map/ppermute | solution.py:256
  13.2 5.6 %collective-permute-start.5 = (bf16[384,2048]{1,0:T(8,128)(2,1)}, bf16[384,2048]{1,0:T(8,128)(2,1)S(1)}, u32[]{:S(2)}, u32[]{:S(2)}) collective-permute-start(bf16[384,2048]{1,0:T(8,128)(2,1)} %get-tuple-element.23), channel_id=1, source_target_pairs={{1,0},{2,1},{3,2},{4,3},{5,4},{6,5},{7,6},{8,7},{9,8},{10,9},{11,1... | collective-permute-start | bytes 4718600 | tf_op jit(solution)/shard_map/ppermute | solution.py:257
  18.8 1.3 collective-permute-start.6
  20.1 0.0 copy-done.11
  20.2 0.0 copy-start.2
  20.2 0.0 copy-start.4
  20.2 0.0 copy-start.6
  20.2 0.0 copy-start.8
  20.2 0.0 copy-done.12
  20.2 0.6 compare_and_fusion.1
  20.8 0.0 copy-done
  20.8 0.8 gather_fusion
  21.6 0.5 and_bitcast_fusion
  22.2 0.6 pad_clamp_fusion
  23.4 0.6 pad_clamp_fusion.2
  24.0 0.6 iota_compare_fusion
  24.6 0.1 copy.14
  24.7 0.7 reshape.45.refs_0_
  25.4 0.0 collective-permute-done
  25.4 0.0 collective-permute-done.1
  25.4 1.9 %collective-permute-start.2 = (bf16[384,4]{0,1:T(4,128)(2,1)S(1)}, bf16[384,4]{0,1:T(4,128)(2,1)S(1)}, u32[]{:S(2)}, u32[]{:S(2)}) collective-permute-start(bf16[384,4]{0,1:T(4,128)(2,1)S(1)} %get-tuple-element.33), channel_id=1, source_target_pairs={{0,1},{1,2},{2,3},{3,4},{4,5},{5,6},{6,7},{7,8},{8,9},{9,10},{10,1... | collective-permute-start | bytes 9224 | tf_op jit(solution)/shard_map/ppermute | solution.py:274
  27.3 7.5 %collective-permute-start.4 = (bf16[384,4]{0,1:T(4,128)(2,1)S(1)}, bf16[384,4]{0,1:T(4,128)(2,1)S(1)}, u32[]{:S(2)}, u32[]{:S(2)}) collective-permute-start(bf16[384,4]{0,1:T(4,128)(2,1)S(1)} %get-tuple-element.32), channel_id=1, source_target_pairs={{1,0},{2,1},{3,2},{4,3},{5,4},{6,5},{7,6},{8,7},{9,8},{10,9},{11,1... | collective-permute-start | bytes 9224 | tf_op jit(solution)/shard_map/ppermute | solution.py:275
  34.9 0.2 copy.11
  35.1 0.9 copy.13
  36.0 23.2 %multiply_reduce_fusion = (f32[1280]{0:T(1024)}, bf16[1280,2048]{1,0:T(8,128)(2,1)}) fusion(bf16[1280,2]{1,0:T(8,128)(2,1)} %copy.13, bf16[1280,2048]{1,0:T(8,128)(2,1)} %param.8, f32[2048]{0:T(1024)S(1)} %bitcast.42, f32[2048]{0:T(1024)S(1)} %bitcast.45, f32[2048]{0:T(1024)S(1)} %bitcast.36, bf16[1280,2]{1,0:T(8,128)(2,1)S(1)} %copy.11, ...), kind=kLoop, calls=%fused_computation.4 | loop fusion | flops 78641920 | bytes 10542080 | tf_op jit(solution)/shard_map/reduce_sum | solution.py:243
  59.2 0.0 copy-done.2
  59.2 0.0 copy-done.4
  59.2 0.0 copy-done.8
  59.2 0.0 collective-permute-done.2
  59.3 0.2 copy.15
  59.4 0.2 copy.16
  59.6 0.0 collective-permute-done.4
  59.7 0.2 copy.17
  59.8 0.2 copy.18
  60.0 0.0 copy-start.5
  60.0 0.0 copy-start.7
  60.1 0.0 copy-start.9
  60.1 0.0 collective-permute-done.6
  60.1 1.6 %broadcast_select_fusion.refs_4_ = bf16[4,128,128]{2,1,0:T(8,128)(2,1)} fusion(bf16[4,128,128]{2,1,0:T(8,128)(2,1)} %param.13, bf16[4,128,128]{2,1,0:T(8,128)(2,1)} %collective-permute-done.6, pred[]{:T(512)S(6)} %eq.6), kind=kLoop, calls=%fused_computation.41 | loop fusion | flops 65536 | bytes 393217 | tf_op jit(solution)/shard_map/jit(_where)/select_n | solution.py:269
  61.7 0.0 collective-permute-done.3
  61.7 5.2 %multiply_reduce_fusion.2 = (f32[384]{0:T(512)S(1)}, bf16[384,2048]{1,0:T(8,128)(2,1)}) fusion(bf16[384,2]{1,0:T(8,128)(2,1)S(1)} %copy.16, bf16[384,2048]{1,0:T(8,128)(2,1)S(1)} %collective-permute-done.3, f32[2048]{0:T(1024)} %bitcast.43, f32[2048]{0:T(1024)} %bitcast.46, f32[2048]{0:T(1024)} %bitcast.37, bf16[384,2]{1,0:T(8,128)(2,1)S(1)} %copy.15, ...), kind=kLoop, calls=%fused_computation.15 | loop fusion | flops 23592576 | bytes 3191296 | tf_op jit(solution)/shard_map/reduce_sum | solution.py:243
  66.9 0.0 collective-permute-done.5
  66.9 0.0 copy-done.3
  66.9 4.5 %multiply_reduce_fusion.1 = (f32[384]{0:T(512)S(1)}, bf16[384,2048]{1,0:T(8,128)(2,1)}) fusion(bf16[384,2]{1,0:T(8,128)(2,1)S(1)} %copy.18, bf16[384,2048]{1,0:T(8,128)(2,1)S(1)} %collective-permute-done.5, f32[2048]{0:T(1024)S(1)} %bitcast.44, f32[2048]{0:T(1024)S(1)} %bitcast.47, f32[2048]{0:T(1024)S(1)} %bitcast.38, bf16[384,2]{1,0:T(8,128)(2,1)S(1)} %copy.17, ...), kind=kLoop, calls=%fused_computation.14 | loop fusion | flops 23592576 | bytes 3191296 | tf_op jit(solution)/shard_map/reduce_sum | solution.py:243
  71.4 45.3 %shard_map.77 = (f32[2,4,2,48,8,128]{5,4,3,2,1,0:T(8,128)}, bf16[16,4,128,128]{3,2,1,0:T(8,128)(2,1)}) custom-call(s32[96]{0:T(128)} %reshape.45.refs_0_, bf16[3,128,2048]{2,1,0:T(8,128)(2,1)} %bitcast.30, bf16[10,128,2048]{2,1,0:T(8,128)(2,1)} %bitcast.29, bf16[3,128,2048]{2,1,0:T(8,128)(2,1)} %bitcast.31, bf16[4,128,128]{2,1,0:T(8,128)(2,1)} %broadcast_select_fusion.refs_4_), custom_call_target="tpu_custom_call" | custom-call | flops 3221225472 | bytes 11534336 | tf_op jit(solution)/shard_map/pallas_call | solution.py:92
  116.7 0.0 copy-start.14
  116.7 0.0 copy-start.1
  116.7 1.9 %copy-done.1 = f32[2,4,2,48,8,128]{5,4,3,2,1,0:T(8,128)S(1)} copy-done((f32[2,4,2,48,8,128]{5,4,3,2,1,0:T(8,128)S(1)}, f32[2,4,2,48,8,128]{5,4,3,2,1,0:T(8,128)}, u32[]{:S(2)}) %copy-start.1) | copy-done | bytes 3145752
  118.6 30.2 %shard_map.78 = (f32[48,8,128]{2,1,0:T(8,128)S(1)}, f32[16,128]{1,0:T(8,128)S(1)}) custom-call(f32[2,4,2,48,8,128]{5,4,3,2,1,0:T(8,128)S(1)} %copy-done.1, f32[16,128]{1,0:T(8,128)S(1)} %maximum_bitcast_fusion.e_ref), custom_call_target="tpu_custom_call" | custom-call | tf_op jit(solution)/shard_map/pallas_call | solution.py:206
  148.8 0.7 gather_fusion.2
  149.5 0.7 gather_fusion.3
  150.2 0.0 copy-done.14
  150.2 0.1 broadcast_select_fusion.1
  150.3 2.6 %gather_fusion.1 = bf16[48,128,128]{2,1,0:T(8,128)(2,1)S(1)} fusion(bf16[64,128,128]{2,1,0:T(8,128)(2,1)} %bitcast.32, s32[1024]{0:T(1024)} %pad_clamp_fusion), kind=kCustom, calls=%fused_computation.3 | custom fusion | bytes 3145920 | tf_op jit(solution)/shard_map/jit(_take)/gather | solution.py:300
  152.8 0.1 dynamic-slice_select_fusion
  152.9 0.0 copy-done.15
  152.9 1.2 fusion.12
  (23 shorter events, 0.1 us)
Async XLA Ops:
  0.6 20.2 %copy-start = (s32[160]{0:T(256)S(1)}, s32[160]{0:T(256)}, u32[]{:S(2)}) copy-start(s32[160]{0:T(256)} %param.12) | copy-start | bytes 1924
  2.1 23.3 %collective-permute-start = (bf16[1280,2]{0,1:T(2,128)(2,1)S(1)}, bf16[1280,2]{0,1:T(2,128)(2,1)S(1)}, u32[]{:S(2)}, u32[]{:S(2)}) collective-permute-start(bf16[1280,2]{0,1:T(2,128)(2,1)S(1)} %copy.19), channel_id=1, source_target_pairs={{0,16},{16,32},{32,48},{48,64},{64,80},{80,96},{96,112},{112,128},... | collective-permute-start | bytes 15368 | tf_op jit(solution)/shard_map/ppermute | solution.py:18
  4.0 16.1 %copy-start.11 = (f32[5,2048]{1,0:T(8,128)S(1)}, f32[5,2048]{1,0:T(8,128)}, u32[]{:S(2)}) copy-start(f32[5,2048]{1,0:T(8,128)} %param.9) | copy-start | bytes 122884
  4.0 16.2 %copy-start.12 = (s32[48,2]{0,1:T(2,128)S(1)}, s32[48,2]{0,1:T(2,128)}, u32[]{:S(2)}) copy-start(s32[48,2]{0,1:T(2,128)} %param.10) | copy-start | bytes 1156
  4.0 21.4 %collective-permute-start.1 = (bf16[1280,2]{0,1:T(2,128)(2,1)S(1)}, bf16[1280,2]{0,1:T(2,128)(2,1)S(1)}, u32[]{:S(2)}, u32[]{:S(2)}) collective-permute-start(bf16[1280,2]{0,1:T(2,128)(2,1)S(1)} %copy.20), channel_id=1, source_target_pairs={{16,0},{32,16},{48,32},{64,48},{80,64},{96,80},{112,96},{128,112},... | collective-permute-start | bytes 15368 | tf_op jit(solution)/shard_map/ppermute | solution.py:19
  9.4 52.3 %collective-permute-start.3 = (bf16[384,2048]{1,0:T(8,128)(2,1)}, bf16[384,2048]{1,0:T(8,128)(2,1)S(1)}, u32[]{:S(2)}, u32[]{:S(2)}) collective-permute-start(bf16[384,2048]{1,0:T(8,128)(2,1)} %get-tuple-element.24), channel_id=1, source_target_pairs={{0,1},{1,2},{2,3},{3,4},{4,5},{5,6},{6,7},{7,8},{8,9},{9,10},{10,1... | collective-permute-start | bytes 4718600 | tf_op jit(solution)/shard_map/ppermute | solution.py:256
  13.2 53.7 %collective-permute-start.5 = (bf16[384,2048]{1,0:T(8,128)(2,1)}, bf16[384,2048]{1,0:T(8,128)(2,1)S(1)}, u32[]{:S(2)}, u32[]{:S(2)}) collective-permute-start(bf16[384,2048]{1,0:T(8,128)(2,1)} %get-tuple-element.23), channel_id=1, source_target_pairs={{1,0},{2,1},{3,2},{4,3},{5,4},{6,5},{7,6},{8,7},{9,8},{10,9},{11,1... | collective-permute-start | bytes 4718600 | tf_op jit(solution)/shard_map/ppermute | solution.py:257
  18.8 41.3 %collective-permute-start.6 = (bf16[4,128,128]{2,1,0:T(8,128)(2,1)}, bf16[4,128,128]{2,1,0:T(8,128)(2,1)}, u32[]{:S(2)}, u32[]{:S(2)}) collective-permute-start(bf16[4,128,128]{2,1,0:T(8,128)(2,1)} %param.13), channel_id=1, source_target_pairs={{16,31},{32,46},{48,61},{64,76},{80,91},{96,106},{112,121},{128,13... | collective-permute-start | bytes 393224 | tf_op jit(solution)/shard_map/ppermute | solution.py:268
  20.2 39.1 %copy-start.2 = (f32[1,2048]{1,0:T(1,128)}, f32[1,2048]{1,0:T(1,128)S(1)}, u32[]{:S(2)}) copy-start(f32[1,2048]{1,0:T(1,128)S(1)} %get-tuple-element.28) | copy-start | bytes 24580
  20.2 39.1 %copy-start.4 = (f32[1,2048]{1,0:T(1,128)}, f32[1,2048]{1,0:T(1,128)S(1)}, u32[]{:S(2)}) copy-start(f32[1,2048]{1,0:T(1,128)S(1)} %get-tuple-element.29) | copy-start | bytes 24580
  20.2 39.0 %copy-start.6 = (f32[1,2048]{1,0:T(1,128)}, f32[1,2048]{1,0:T(1,128)S(1)}, u32[]{:S(2)}) copy-start(f32[1,2048]{1,0:T(1,128)S(1)} %get-tuple-element.30) | copy-start | bytes 24580
  20.2 39.0 %copy-start.8 = (f32[1,2048]{1,0:T(1,128)}, f32[1,2048]{1,0:T(1,128)S(1)}, u32[]{:S(2)}) copy-start(f32[1,2048]{1,0:T(1,128)S(1)} %get-tuple-element.31) | copy-start | bytes 24580
  25.4 33.9 %collective-permute-start.2 = (bf16[384,4]{0,1:T(4,128)(2,1)S(1)}, bf16[384,4]{0,1:T(4,128)(2,1)S(1)}, u32[]{:S(2)}, u32[]{:S(2)}) collective-permute-start(bf16[384,4]{0,1:T(4,128)(2,1)S(1)} %get-tuple-element.33), channel_id=1, source_target_pairs={{0,1},{1,2},{2,3},{3,4},{4,5},{5,6},{6,7},{7,8},{8,9},{9,10},{10,1... | collective-permute-start | bytes 9224 | tf_op jit(solution)/shard_map/ppermute | solution.py:274
  27.3 32.3 %collective-permute-start.4 = (bf16[384,4]{0,1:T(4,128)(2,1)S(1)}, bf16[384,4]{0,1:T(4,128)(2,1)S(1)}, u32[]{:S(2)}, u32[]{:S(2)}) collective-permute-start(bf16[384,4]{0,1:T(4,128)(2,1)S(1)} %get-tuple-element.32), channel_id=1, source_target_pairs={{1,0},{2,1},{3,2},{4,3},{5,4},{6,5},{7,6},{8,7},{9,8},{10,9},{11,1... | collective-permute-start | bytes 9224 | tf_op jit(solution)/shard_map/ppermute | solution.py:275
  60.0 6.8 %copy-start.3 = (f32[1,2048]{1,0:T(1,128)S(1)}, f32[1,2048]{1,0:T(1,128)}, u32[]{:S(2)}) copy-start(f32[1,2048]{1,0:T(1,128)} %copy-done.2) | copy-start | bytes 24580
  60.0 6.8 %copy-start.5 = (f32[1,2048]{1,0:T(1,128)S(1)}, f32[1,2048]{1,0:T(1,128)}, u32[]{:S(2)}) copy-start(f32[1,2048]{1,0:T(1,128)} %copy-done.4) | copy-start | bytes 24580
  60.0 6.8 %copy-start.7 = (f32[1,2048]{1,0:T(1,128)S(1)}, f32[1,2048]{1,0:T(1,128)}, u32[]{:S(2)}) copy-start(f32[1,2048]{1,0:T(1,128)} %copy-done.6) | copy-start | bytes 24580
  60.1 6.8 %copy-start.9 = (f32[1,2048]{1,0:T(1,128)S(1)}, f32[1,2048]{1,0:T(1,128)}, u32[]{:S(2)}) copy-start(f32[1,2048]{1,0:T(1,128)} %copy-done.8) | copy-start | bytes 24580
  61.7 9.7 %copy-start.10 = (f32[1280]{0:T(1024)S(1)}, f32[1280]{0:T(1024)}, u32[]{:S(2)}) copy-start(f32[1280]{0:T(1024)} %get-tuple-element.17) | copy-start | bytes 15364
  116.7 33.5 %copy-start.14 = (pred[48]{0:T(512)(128)(4,1)S(1)}, pred[48]{0:T(512)(128)(4,1)}, u32[]{:S(2)}) copy-start(pred[48]{0:T(512)(128)(4,1)} %get-tuple-element.38) | copy-start | bytes 148
  116.7 1.9 %copy-start.1 = (f32[2,4,2,48,8,128]{5,4,3,2,1,0:T(8,128)S(1)}, f32[2,4,2,48,8,128]{5,4,3,2,1,0:T(8,128)}, u32[]{:S(2)}) copy-start(f32[2,4,2,48,8,128]{5,4,3,2,1,0:T(8,128)} %get-tuple-element.7.g_ref) | copy-start | bytes 9437188
  118.6 34.3 %copy-start.13 = (pred[48]{0:T(512)(128)(4,1)S(1)}, pred[48]{0:T(512)(128)(4,1)}, u32[]{:S(2)}) copy-start(pred[48]{0:T(512)(128)(4,1)} %get-tuple-element.11) | copy-start | bytes 148
  118.6 34.3 %copy-start.15 = (pred[48]{0:T(512)(128)(4,1)S(1)}, pred[48]{0:T(512)(128)(4,1)}, u32[]{:S(2)}) copy-start(pred[48]{0:T(512)(128)(4,1)} %get-tuple-element.21) | copy-start | bytes 148
  118.6 34.4 %copy-start.16 = (pred[48]{0:T(512)(128)(4,1)S(1)}, pred[48]{0:T(512)(128)(4,1)}, u32[]{:S(2)}) copy-start(pred[48]{0:T(512)(128)(4,1)} %iota_compare_fusion) | copy-start | bytes 148

commit v8 on v7

--- a/solution.py
+++ b/solution.py
@@ -29,20 +29,35 @@
     width = before_ref.shape[0]
     middle = local_ref.shape[0]
     p = lax.axis_index("pix")
+    c = p % 2
+    x = (p // 2) % 4
+    yl = p // 8
+    partner = p + 1 - 2 * c
+    right = (yl * 4 + (x + 1) % 4) * 2 + c
+    left = (yl * 4 + (x + 3) % 4) * 2 + c
+    ypart = ((1 - yl) * 4 + x) * 2 + c
+    mine = c * 8 + x * 2 + yl
+    theirs = c * 8 + x * 2 + 1 - yl
+    pair_at = c * 8 + x * 2
+    from_left = c * 8 + ((x + 3) % 4) * 2
 
     barrier = pltpu.get_barrier_semaphore()
-    for k in range(1, shares):
-        pl.semaphore_signal(barrier, 1, device_id={"pix": (p + k) % shares}, device_id_type=MESH)
-    pl.semaphore_wait(barrier, shares - 1)
-    sends = []
-    for k in range(1, shares):
-        dest = (p + k) % shares
-        cp = pltpu.make_async_remote_copy(
-            src_ref=chunk_ref, dst_ref=table.at[p], send_sem=send_sems.at[dest],
-            recv_sem=recv_sems.at[p], device_id={"pix": dest}, device_id_type=MESH,
+    for peer in (partner, right, left, ypart):
+        pl.semaphore_signal(barrier, 1, device_id={"pix": peer}, device_id_type=MESH)
+    pl.semaphore_wait(barrier, 4)
+
+    def remote(src, dst, k, peer):
+        return pltpu.make_async_remote_copy(
+            src_ref=src, dst_ref=dst, send_sem=send_sems.at[k], recv_sem=recv_sems.at[k],
+            device_id={"pix": peer}, device_id_type=MESH,
         )
-        cp.start()
-        sends.append(cp)
+
+    sent = []
+    ca = remote(chunk_ref, table.at[mine], 0, ypart)
+    ca.start()
+    sent.append(ca)
+    own = pltpu.make_async_copy(chunk_ref, table.at[mine], sems.at[3])
+    own.start()
 
     copies = [
         pltpu.make_async_copy(local_ref, ext_ref.at[pl.ds(width, middle)], sems.at[0]),
@@ -55,29 +70,43 @@
         cp.wait()
 
     def body(s, carry):
-        left = ext_ref[rel_ref[2 * s]]
-        right = ext_ref[rel_ref[2 * s + 1]]
+        left_rows = ext_ref[rel_ref[2 * s]]
+        right_rows = ext_ref[rel_ref[2 * s + 1]]
         g = lax.dot_general(
-            left, right, (((1,), (1,)), ((), ())), preferred_element_type=jnp.float32
+            left_rows, right_rows, (((1,), (1,)), ((), ())), preferred_element_type=jnp.float32
         )
         for q in range(shares):
             out_ref[q % 2, (q // 2) % 4, q // 8, s] = g[q * rows : (q + 1) * rows, :]
         return carry
 
-    lax.fori_loop(0, slots, body, 0)
-
-    for cp in sends:
+    third = slots // 3
+    lax.fori_loop(0, third, body, 0)
+    ca.wait_recv()
+    b1 = [
+        remote(chunk_ref, table.at[mine], 1, right),
+        remote(table.at[theirs], table.at[theirs], 2, right),
+        remote(chunk_ref, table.at[mine], 3, left),
+        remote(table.at[theirs], table.at[theirs], 4, left),
+    ]
+    for cp in b1:
+        cp.start()
+    sent += b1
+    lax.fori_loop(third, 2 * third, body, 0)
+    for cp in b1:
+        cp.wait_recv()
+    b2 = remote(table.at[pl.ds(from_left, 2)], table.at[pl.ds(from_left, 2)], 5, right)
+    b2.start()
+    sent.append(b2)
+    lax.fori_loop(2 * third, slots, body, 0)
+    b2.wait_recv()
+    own.wait()
+    cc = remote(table.at[pl.ds(c * 8, 8)], table.at[pl.ds(c * 8, 8)], 6, partner)
+    cc.start()
+    sent.append(cc)
+    cc.wait_recv()
+    for cp in sent:
         cp.wait_send()
-    for k in range(1, shares):
-        src = (p + shares - k) % shares
-        pltpu.make_async_remote_copy(
-            src_ref=chunk_ref, dst_ref=table.at[src], send_sem=send_sems.at[src],
-            recv_sem=recv_sems.at[src], device_id={"pix": src}, device_id_type=MESH,
-        ).wait_recv()
-    table_out[p] = chunk_ref[...]
-    for k in range(1, shares):
-        src = (p + shares - k) % shares
-        table_out[src] = table[src]
+    table_out[...] = table[...]
 
 
 def pair_grams(relative, before, local, after, chunk, shares, block):
@@ -102,9 +131,9 @@
         scratch_shapes=[
             pltpu.VMEM((ext_blocks, block, pix_local), local.dtype),
             pltpu.VMEM(table_shape, chunk.dtype),
-            pltpu.SemaphoreType.DMA((3,)),
-            pltpu.SemaphoreType.DMA((shares,)),
-            pltpu.SemaphoreType.DMA((shares,)),
+            pltpu.SemaphoreType.DMA((4,)),
+            pltpu.SemaphoreType.DMA((7,)),
+            pltpu.SemaphoreType.DMA((7,)),
         ],
         compiler_params=pltpu.CompilerParams(
             collective_id=1, has_side_effects=True, vmem_limit_bytes=56 * 1024 * 1024
@@ -296,7 +325,9 @@
     )
     inv_right = jnp.take(inv_blocks, relative[:, 1], axis=0)
     rules = jnp.take(rule_of_block, pairs[:, 1], axis=0)
-    rules = ((rules // per_index - me_ion) % ions) * per_index + rules % per_index
+    source = (rules // per_index - me_ion) % ions
+    slot = (source % 2) * 8 + ((source // 2) % 4) * 2 + source // 8
+    rules = slot * per_index + rules % per_index
     matrices = jnp.take(lookup_tables, rules, axis=0)
     coloc = (gram * inv_left[:, :, None] * inv_right[:, None, :] / pixel_count).astype(jnp.bfloat16)
     scores = jnp.einsum("src,scd->srd", coloc, matrices, preferred_element_type=jnp.float32)

time: 155 us -> 148 us (0.955)
  Pallas kernels: 75.4 us -> 68.5 us
    pallas_call x1, Pallas kernels: 45.3 us -> 37.6 us  [pair_grams(): pl.pallas_call(lambda *refs: gram_kernel(shares, *refs), out_shape=(jax.S...]
  transfers between devices with their start and end apart: 7 -> 7, of which waited for: 0 -> 0; matrix products, arithmetic and copies ran while one was open for 26% -> 28% of each run, Pallas kernels for 0% -> 0%
where the time goes in v8:
time: 148 us; the launch traced here: 147 us
  Pallas kernels  68.5 us (46%)
  other arithmetic  37.6 us (25%)
  starting transfers between devices  23.4 us (16%)
  local copies, waits for them, and re-layouts  14.9 us (10%)
  between operations  1.61 us (1%)
    pallas_call x1, Pallas kernels, pair_grams(): pl.pallas_call(lambda *refs: gram_kernel(shares, *refs), out_shape=(jax.S...  37.6 us
    reduce_sum x3, other arithmetic, row_squares(): return jnp.sum(values * values, axis=1)  32.9 us
    pallas_call x1, Pallas kernels, scatter_grams(): pl.pallas_call(scatter_kernel, out_shape=(jax.ShapeDtypeStruct(part, f32)...  30.9 us
    ppermute x1, starting transfers between devices, on_device(): edge_after = lax.ppermute(edges[:width], 'ion', down)  7.54 us
    ppermute x1, starting transfers between devices, on_device(): raw_after = lax.ppermute(images[:width], 'ion', down)  5.63 us
    slice x1, local copies, waits for them, and re-layouts, on_device(): raw_after = lax.ppermute(images[:width], 'ion', down)  3.93 us
    ppermute x1, starting transfers between devices, on_device(): raw_before = lax.ppermute(images[local_rows - width:], 'ion', up)  3.81 us
  transfers between devices with their start and end apart: 7, of which 0 were waited for; matrix products, arithmetic and copies ran while one was open for 28% of the time, Pallas kernels for 0%

profile of v8, /device:TPU:16, one launch (start us, length us, event | category | flops | bytes accessed | tf_op | source)
XLA Modules:
  0.0 147.3 jit_solution(2029887269057636156)
XLA Ops:
  0.6 0.0 copy-start
  0.6 1.2 fusion.30
  1.9 0.2 copy.19
  2.1 1.7 %collective-permute-start = (bf16[1280,2]{0,1:T(2,128)(2,1)S(1)}, bf16[1280,2]{0,1:T(2,128)(2,1)S(1)}, u32[]{:S(2)}, u32[]{:S(2)}) collective-permute-start(bf16[1280,2]{0,1:T(2,128)(2,1)S(1)} %copy.19), channel_id=1, source_target_pairs={{0,16},{16,32},{32,48},{48,64},{64,80},{80,96},{96,112},{112,128},... | collective-permute-start | bytes 15368 | tf_op jit(solution)/shard_map/ppermute | solution.py:18
  3.8 0.2 copy.20
  4.0 1.4 collective-permute-start.1
  5.4 3.9 %fusion.29 = (bf16[384,2048]{1,0:T(8,128)(2,1)}, bf16[384,2048]{1,0:T(8,128)(2,1)}) fusion(bf16[1280,2048]{1,0:T(8,128)(2,1)} %param.8), kind=kLoop, calls=%fused_computation.94 | loop fusion | bytes 6291456 | tf_op jit(solution)/shard_map/slice | solution.py:286
  9.4 3.8 %collective-permute-start.3 = (bf16[384,2048]{1,0:T(8,128)(2,1)}, bf16[384,2048]{1,0:T(8,128)(2,1)S(1)}, u32[]{:S(2)}, u32[]{:S(2)}) collective-permute-start(bf16[384,2048]{1,0:T(8,128)(2,1)} %get-tuple-element.24), channel_id=1, source_target_pairs={{0,1},{1,2},{2,3},{3,4},{4,5},{5,6},{6,7},{7,8},{8,9},{9,10},{10,1... | collective-permute-start | bytes 4718600 | tf_op jit(solution)/shard_map/ppermute | solution.py:285
  13.2 5.6 %collective-permute-start.5 = (bf16[384,2048]{1,0:T(8,128)(2,1)}, bf16[384,2048]{1,0:T(8,128)(2,1)S(1)}, u32[]{:S(2)}, u32[]{:S(2)}) collective-permute-start(bf16[384,2048]{1,0:T(8,128)(2,1)} %get-tuple-element.23), channel_id=1, source_target_pairs={{1,0},{2,1},{3,2},{4,3},{5,4},{6,5},{7,6},{8,7},{9,8},{10,9},{11,1... | collective-permute-start | bytes 4718600 | tf_op jit(solution)/shard_map/ppermute | solution.py:286
  18.8 1.3 collective-permute-start.6
  20.1 0.0 copy-done.11
  20.2 0.0 copy-start.2
  20.2 0.0 copy-start.4
  20.2 0.0 copy-start.6
  20.2 0.0 copy-start.8
  20.2 0.0 copy-done.12
  20.2 0.6 compare_and_fusion.1
  20.8 0.0 copy-done
  20.8 0.8 gather_fusion
  21.6 0.6 and_bitcast_fusion
  22.2 0.6 pad_clamp_fusion
  23.4 0.6 pad_clamp_fusion.2
  24.0 0.6 iota_compare_fusion
  24.6 0.1 copy.14
  24.7 0.7 reshape.45.refs_0_
  25.4 0.0 collective-permute-done
  25.4 0.0 collective-permute-done.1
  25.4 1.9 %collective-permute-start.2 = (bf16[384,4]{0,1:T(4,128)(2,1)S(1)}, bf16[384,4]{0,1:T(4,128)(2,1)S(1)}, u32[]{:S(2)}, u32[]{:S(2)}) collective-permute-start(bf16[384,4]{0,1:T(4,128)(2,1)S(1)} %get-tuple-element.33), channel_id=1, source_target_pairs={{0,1},{1,2},{2,3},{3,4},{4,5},{5,6},{6,7},{7,8},{8,9},{9,10},{10,1... | collective-permute-start | bytes 9224 | tf_op jit(solution)/shard_map/ppermute | solution.py:303
  27.3 7.5 %collective-permute-start.4 = (bf16[384,4]{0,1:T(4,128)(2,1)S(1)}, bf16[384,4]{0,1:T(4,128)(2,1)S(1)}, u32[]{:S(2)}, u32[]{:S(2)}) collective-permute-start(bf16[384,4]{0,1:T(4,128)(2,1)S(1)} %get-tuple-element.32), channel_id=1, source_target_pairs={{1,0},{2,1},{3,2},{4,3},{5,4},{6,5},{7,6},{8,7},{9,8},{10,9},{11,1... | collective-permute-start | bytes 9224 | tf_op jit(solution)/shard_map/ppermute | solution.py:304
  34.9 0.2 copy.11
  35.1 0.9 copy.13
  36.0 23.2 %multiply_reduce_fusion = (f32[1280]{0:T(1024)}, bf16[1280,2048]{1,0:T(8,128)(2,1)}) fusion(bf16[1280,2]{1,0:T(8,128)(2,1)} %copy.13, bf16[1280,2048]{1,0:T(8,128)(2,1)} %param.8, f32[2048]{0:T(1024)S(1)} %bitcast.42, f32[2048]{0:T(1024)S(1)} %bitcast.45, f32[2048]{0:T(1024)S(1)} %bitcast.36, bf16[1280,2]{1,0:T(8,128)(2,1)S(1)} %copy.11, ...), kind=kLoop, calls=%fused_computation.4 | loop fusion | flops 78641920 | bytes 10542080 | tf_op jit(solution)/shard_map/reduce_sum | solution.py:272
  59.2 0.0 copy-done.2
  59.2 0.0 copy-done.4
  59.3 0.0 copy-done.6
  59.3 0.0 copy-done.8
  59.3 0.0 collective-permute-done.2
  59.3 0.2 copy.15
  59.5 0.2 copy.16
  59.7 0.0 collective-permute-done.4
  59.7 0.2 copy.17
  59.9 0.2 copy.18
  60.1 0.0 copy-start.5
  60.1 0.0 copy-start.7
  60.1 0.0 copy-start.9
  60.1 0.0 collective-permute-done.6
  60.1 1.6 %broadcast_select_fusion.refs_4_ = bf16[4,128,128]{2,1,0:T(8,128)(2,1)} fusion(bf16[4,128,128]{2,1,0:T(8,128)(2,1)} %param.13, bf16[4,128,128]{2,1,0:T(8,128)(2,1)} %collective-permute-done.6, pred[]{:T(512)S(6)} %eq.8), kind=kLoop, calls=%fused_computation.41 | loop fusion | flops 65536 | bytes 393217 | tf_op jit(solution)/shard_map/jit(_where)/select_n | solution.py:298
  61.7 0.0 collective-permute-done.3
  61.7 5.2 %multiply_reduce_fusion.2 = (f32[384]{0:T(512)S(1)}, bf16[384,2048]{1,0:T(8,128)(2,1)}) fusion(bf16[384,2]{1,0:T(8,128)(2,1)S(1)} %copy.16, bf16[384,2048]{1,0:T(8,128)(2,1)S(1)} %collective-permute-done.3, f32[2048]{0:T(1024)} %bitcast.43, f32[2048]{0:T(1024)} %bitcast.46, f32[2048]{0:T(1024)} %bitcast.37, bf16[384,2]{1,0:T(8,128)(2,1)S(1)} %copy.15, ...), kind=kLoop, calls=%fused_computation.15 | loop fusion | flops 23592576 | bytes 3191296 | tf_op jit(solution)/shard_map/reduce_sum | solution.py:272
  66.9 0.0 collective-permute-done.5
  66.9 0.0 copy-done.5
  66.9 0.0 copy-done.7
  66.9 0.0 copy-done.9
  66.9 4.5 %multiply_reduce_fusion.1 = (f32[384]{0:T(512)S(1)}, bf16[384,2048]{1,0:T(8,128)(2,1)}) fusion(bf16[384,2]{1,0:T(8,128)(2,1)S(1)} %copy.18, bf16[384,2048]{1,0:T(8,128)(2,1)S(1)} %collective-permute-done.5, f32[2048]{0:T(1024)S(1)} %bitcast.44, f32[2048]{0:T(1024)S(1)} %bitcast.47, f32[2048]{0:T(1024)S(1)} %bitcast.38, bf16[384,2]{1,0:T(8,128)(2,1)S(1)} %copy.17, ...), kind=kLoop, calls=%fused_computation.14 | loop fusion | flops 23592576 | bytes 3191296 | tf_op jit(solution)/shard_map/reduce_sum | solution.py:272
  71.4 37.6 %shard_map.77 = (f32[2,4,2,48,8,128]{5,4,3,2,1,0:T(8,128)}, bf16[16,4,128,128]{3,2,1,0:T(8,128)(2,1)}) custom-call(s32[96]{0:T(128)} %reshape.45.refs_0_, bf16[3,128,2048]{2,1,0:T(8,128)(2,1)} %bitcast.30, bf16[10,128,2048]{2,1,0:T(8,128)(2,1)} %bitcast.29, bf16[3,128,2048]{2,1,0:T(8,128)(2,1)} %bitcast.31, bf16[4,128,128]{2,1,0:T(8,128)(2,1)} %broadcast_select_fusion.refs_4_), custom_call_target="tpu_custom_call" | custom-call | flops 3221225472 | bytes 11534336 | tf_op jit(solution)/shard_map/pallas_call | solution.py:121
  109.0 1.9 %copy-done.1 = f32[2,4,2,48,8,128]{5,4,3,2,1,0:T(8,128)S(1)} copy-done((f32[2,4,2,48,8,128]{5,4,3,2,1,0:T(8,128)S(1)}, f32[2,4,2,48,8,128]{5,4,3,2,1,0:T(8,128)}, u32[]{:S(2)}) %copy-start.1) | copy-done | bytes 3145752
  110.9 30.9 %shard_map.78 = (f32[48,8,128]{2,1,0:T(8,128)S(1)}, f32[16,128]{1,0:T(8,128)S(1)}) custom-call(f32[2,4,2,48,8,128]{5,4,3,2,1,0:T(8,128)S(1)} %copy-done.1, f32[16,128]{1,0:T(8,128)S(1)} %maximum_bitcast_fusion.e_ref), custom_call_target="tpu_custom_call" | custom-call | tf_op jit(solution)/shard_map/pallas_call | solution.py:235
  141.8 0.7 gather_fusion.2
  142.5 0.7 gather_fusion.3
  143.3 0.1 broadcast_select_fusion.1
  143.3 2.6 %gather_fusion.1 = bf16[48,128,128]{2,1,0:T(8,128)(2,1)S(1)} fusion(bf16[64,128,128]{2,1,0:T(8,128)(2,1)} %bitcast.32, s32[1024]{0:T(1024)} %pad_clamp_fusion), kind=kCustom, calls=%fused_computation.3 | custom fusion | bytes 3145920 | tf_op jit(solution)/shard_map/jit(_take)/gather | solution.py:331
  145.9 0.0 copy-done.13
  145.9 0.1 dynamic-slice_select_fusion
  146.0 1.2 fusion.12
  (23 shorter events, 0.1 us)
Async XLA Ops:
  0.6 20.2 %copy-start = (s32[160]{0:T(256)S(1)}, s32[160]{0:T(256)}, u32[]{:S(2)}) copy-start(s32[160]{0:T(256)} %param.12) | copy-start | bytes 1924
  2.1 23.3 %collective-permute-start = (bf16[1280,2]{0,1:T(2,128)(2,1)S(1)}, bf16[1280,2]{0,1:T(2,128)(2,1)S(1)}, u32[]{:S(2)}, u32[]{:S(2)}) collective-permute-start(bf16[1280,2]{0,1:T(2,128)(2,1)S(1)} %copy.19), channel_id=1, source_target_pairs={{0,16},{16,32},{32,48},{48,64},{64,80},{80,96},{96,112},{112,128},... | collective-permute-start | bytes 15368 | tf_op jit(solution)/shard_map/ppermute | solution.py:18
  4.0 16.1 %copy-start.11 = (f32[5,2048]{1,0:T(8,128)S(1)}, f32[5,2048]{1,0:T(8,128)}, u32[]{:S(2)}) copy-start(f32[5,2048]{1,0:T(8,128)} %param.9) | copy-start | bytes 122884
  4.0 16.2 %copy-start.12 = (s32[48,2]{0,1:T(2,128)S(1)}, s32[48,2]{0,1:T(2,128)}, u32[]{:S(2)}) copy-start(s32[48,2]{0,1:T(2,128)} %param.10) | copy-start | bytes 1156
  4.0 21.4 %collective-permute-start.1 = (bf16[1280,2]{0,1:T(2,128)(2,1)S(1)}, bf16[1280,2]{0,1:T(2,128)(2,1)S(1)}, u32[]{:S(2)}, u32[]{:S(2)}) collective-permute-start(bf16[1280,2]{0,1:T(2,128)(2,1)S(1)} %copy.20), channel_id=1, source_target_pairs={{16,0},{32,16},{48,32},{64,48},{80,64},{96,80},{112,96},{128,112},... | collective-permute-start | bytes 15368 | tf_op jit(solution)/shard_map/ppermute | solution.py:19
  9.4 52.3 %collective-permute-start.3 = (bf16[384,2048]{1,0:T(8,128)(2,1)}, bf16[384,2048]{1,0:T(8,128)(2,1)S(1)}, u32[]{:S(2)}, u32[]{:S(2)}) collective-permute-start(bf16[384,2048]{1,0:T(8,128)(2,1)} %get-tuple-element.24), channel_id=1, source_target_pairs={{0,1},{1,2},{2,3},{3,4},{4,5},{5,6},{6,7},{7,8},{8,9},{9,10},{10,1... | collective-permute-start | bytes 4718600 | tf_op jit(solution)/shard_map/ppermute | solution.py:285
  13.2 53.7 %collective-permute-start.5 = (bf16[384,2048]{1,0:T(8,128)(2,1)}, bf16[384,2048]{1,0:T(8,128)(2,1)S(1)}, u32[]{:S(2)}, u32[]{:S(2)}) collective-permute-start(bf16[384,2048]{1,0:T(8,128)(2,1)} %get-tuple-element.23), channel_id=1, source_target_pairs={{1,0},{2,1},{3,2},{4,3},{5,4},{6,5},{7,6},{8,7},{9,8},{10,9},{11,1... | collective-permute-start | bytes 4718600 | tf_op jit(solution)/shard_map/ppermute | solution.py:286
  18.8 41.3 %collective-permute-start.6 = (bf16[4,128,128]{2,1,0:T(8,128)(2,1)}, bf16[4,128,128]{2,1,0:T(8,128)(2,1)}, u32[]{:S(2)}, u32[]{:S(2)}) collective-permute-start(bf16[4,128,128]{2,1,0:T(8,128)(2,1)} %param.13), channel_id=1, source_target_pairs={{16,31},{32,46},{48,61},{64,76},{80,91},{96,106},{112,121},{128,13... | collective-permute-start | bytes 393224 | tf_op jit(solution)/shard_map/ppermute | solution.py:297
  20.2 39.1 %copy-start.2 = (f32[1,2048]{1,0:T(1,128)}, f32[1,2048]{1,0:T(1,128)S(1)}, u32[]{:S(2)}) copy-start(f32[1,2048]{1,0:T(1,128)S(1)} %get-tuple-element.28) | copy-start | bytes 24580
  20.2 39.1 %copy-start.4 = (f32[1,2048]{1,0:T(1,128)}, f32[1,2048]{1,0:T(1,128)S(1)}, u32[]{:S(2)}) copy-start(f32[1,2048]{1,0:T(1,128)S(1)} %get-tuple-element.29) | copy-start | bytes 24580
  20.2 39.1 %copy-start.6 = (f32[1,2048]{1,0:T(1,128)}, f32[1,2048]{1,0:T(1,128)S(1)}, u32[]{:S(2)}) copy-start(f32[1,2048]{1,0:T(1,128)S(1)} %get-tuple-element.30) | copy-start | bytes 24580
  20.2 39.1 %copy-start.8 = (f32[1,2048]{1,0:T(1,128)}, f32[1,2048]{1,0:T(1,128)S(1)}, u32[]{:S(2)}) copy-start(f32[1,2048]{1,0:T(1,128)S(1)} %get-tuple-element.31) | copy-start | bytes 24580
  25.4 33.9 %collective-permute-start.2 = (bf16[384,4]{0,1:T(4,128)(2,1)S(1)}, bf16[384,4]{0,1:T(4,128)(2,1)S(1)}, u32[]{:S(2)}, u32[]{:S(2)}) collective-permute-start(bf16[384,4]{0,1:T(4,128)(2,1)S(1)} %get-tuple-element.33), channel_id=1, source_target_pairs={{0,1},{1,2},{2,3},{3,4},{4,5},{5,6},{6,7},{7,8},{8,9},{9,10},{10,1... | collective-permute-start | bytes 9224 | tf_op jit(solution)/shard_map/ppermute | solution.py:303
  27.3 32.3 %collective-permute-start.4 = (bf16[384,4]{0,1:T(4,128)(2,1)S(1)}, bf16[384,4]{0,1:T(4,128)(2,1)S(1)}, u32[]{:S(2)}, u32[]{:S(2)}) collective-permute-start(bf16[384,4]{0,1:T(4,128)(2,1)S(1)} %get-tuple-element.32), channel_id=1, source_target_pairs={{1,0},{2,1},{3,2},{4,3},{5,4},{6,5},{7,6},{8,7},{9,8},{10,9},{11,1... | collective-permute-start | bytes 9224 | tf_op jit(solution)/shard_map/ppermute | solution.py:304
  60.0 6.8 %copy-start.3 = (f32[1,2048]{1,0:T(1,128)S(1)}, f32[1,2048]{1,0:T(1,128)}, u32[]{:S(2)}) copy-start(f32[1,2048]{1,0:T(1,128)} %copy-done.2) | copy-start | bytes 24580
  60.1 6.8 %copy-start.5 = (f32[1,2048]{1,0:T(1,128)S(1)}, f32[1,2048]{1,0:T(1,128)}, u32[]{:S(2)}) copy-start(f32[1,2048]{1,0:T(1,128)} %copy-done.4) | copy-start | bytes 24580
  60.1 6.8 %copy-start.7 = (f32[1,2048]{1,0:T(1,128)S(1)}, f32[1,2048]{1,0:T(1,128)}, u32[]{:S(2)}) copy-start(f32[1,2048]{1,0:T(1,128)} %copy-done.6) | copy-start | bytes 24580
  60.1 6.8 %copy-start.9 = (f32[1,2048]{1,0:T(1,128)S(1)}, f32[1,2048]{1,0:T(1,128)}, u32[]{:S(2)}) copy-start(f32[1,2048]{1,0:T(1,128)} %copy-done.8) | copy-start | bytes 24580
  61.7 9.7 %copy-start.10 = (f32[1280]{0:T(1024)S(1)}, f32[1280]{0:T(1024)}, u32[]{:S(2)}) copy-start(f32[1280]{0:T(1024)} %get-tuple-element.17) | copy-start | bytes 15364
  109.0 34.3 %copy-start.14 = (pred[48]{0:T(512)(128)(4,1)S(1)}, pred[48]{0:T(512)(128)(4,1)}, u32[]{:S(2)}) copy-start(pred[48]{0:T(512)(128)(4,1)} %get-tuple-element.38) | copy-start | bytes 148
  109.0 1.9 %copy-start.1 = (f32[2,4,2,48,8,128]{5,4,3,2,1,0:T(8,128)S(1)}, f32[2,4,2,48,8,128]{5,4,3,2,1,0:T(8,128)}, u32[]{:S(2)}) copy-start(f32[2,4,2,48,8,128]{5,4,3,2,1,0:T(8,128)} %get-tuple-element.7.g_ref) | copy-start | bytes 9437188
  110.9 35.0 %copy-start.13 = (pred[48]{0:T(512)(128)(4,1)S(1)}, pred[48]{0:T(512)(128)(4,1)}, u32[]{:S(2)}) copy-start(pred[48]{0:T(512)(128)(4,1)} %get-tuple-element.11) | copy-start | bytes 148
  110.9 35.1 %copy-start.15 = (pred[48]{0:T(512)(128)(4,1)S(1)}, pred[48]{0:T(512)(128)(4,1)}, u32[]{:S(2)}) copy-start(pred[48]{0:T(512)(128)(4,1)} %get-tuple-element.21) | copy-start | bytes 148
  110.9 35.1 %copy-start.16 = (pred[48]{0:T(512)(128)(4,1)S(1)}, pred[48]{0:T(512)(128)(4,1)}, u32[]{:S(2)}) copy-start(pred[48]{0:T(512)(128)(4,1)} %iota_compare_fusion) | copy-start | bytes 148

commit v9 on v8

--- a/solution.py
+++ b/solution.py
@@ -282,8 +282,6 @@
     ions = lax.axis_size("ion")
     up = [(i, i + 1) for i in range(ions - 1)]
     down = [(j, i) for i, j in up]
-    raw_before = lax.ppermute(images[local_rows - width :], "ion", up)
-    raw_after = lax.ppermute(images[:width], "ion", down)
     me_pix = lax.axis_index("pix")
     offset = me_pix * rows
     me_pix = lax.axis_index("pix")
@@ -297,17 +295,12 @@
     fetched = lax.ppermute(adduct, ("pix", "ion"), turn)
     own_turn = jnp.where(me_pix == 0, adduct, fetched)
     padded = extended_2(images, (("pix", 1),), 2)
+    raw_before = lax.ppermute(padded[local_rows - width :], "ion", up)
+    raw_after = lax.ppermute(padded[:width], "ion", down)
     smoothed = smooth_rows(padded, stencil)
     local_squares = row_squares(smoothed)
-    edges = jnp.concatenate([padded[:, :2], padded[:, pix_local + 2 :]], axis=1)
-    edge_before = lax.ppermute(edges[local_rows - width :], "ion", up)
-    edge_after = lax.ppermute(edges[:width], "ion", down)
-    before = smooth_rows(
-        jnp.concatenate([edge_before[:, :2], raw_before, edge_before[:, 2:]], axis=1), stencil
-    )
-    after = smooth_rows(
-        jnp.concatenate([edge_after[:, :2], raw_after, edge_after[:, 2:]], axis=1), stencil
-    )
+    before = smooth_rows(raw_before, stencil)
+    after = smooth_rows(raw_after, stencil)
     squares = jnp.concatenate([row_squares(before), local_squares, row_squares(after)])
     pixel_count = pix_local * shares
     first = lax.axis_index("ion") * local_blocks

time: 148 us -> 182 us (1.23); the launches traced: 147 us -> 179 us
  local copies, waits for them, and re-layouts: 14.9 us -> 53.2 us
  starting transfers between devices: 23.4 us -> 13.8 us
  Pallas kernels: 68.5 us -> 73.2 us
  other arithmetic: 37.6 us -> 33.3 us
  waiting for transfers between devices: 0.02 us -> 2.78 us
    concatenate x0 -> x1, local copies, waits for them, and re-layouts: none -> 27.8 us  [extended_2(): array = jnp.concatenate([before, array, after], axis=dim)]
    ppermute x4 -> x2, starting transfers between devices: 18.9 us -> 9.44 us  [the longest x1 5.63 us: on_device(): raw_after = lax.ppermute(padded[:width], 'ion', down)]
    unnamed x36 -> x19, local copies, waits for them, and re-layouts: 2.29 us -> 9.81 us
    pallas_call x1, Pallas kernels: 37.6 us -> 43.3 us  [pair_grams(): pl.pallas_call(lambda *refs: gram_kernel(shares, *refs), out_shape=(jax.S...]
    convert_element_type x0 -> x2, local copies, waits for them, and re-layouts: none -> 4.4 us  [smooth_rows(): return total.astype(jnp.bfloat16)]
    reduce_sum x3 -> x2, other arithmetic: 32.9 us -> 28.7 us  [row_squares(): return jnp.sum(values * values, axis=1)]
    ppermute x4 -> x2, waiting for transfers between devices: 0.01 us -> 2.77 us  [the longest x1 2.12 us: on_device(): raw_after = lax.ppermute(padded[:width], 'ion', down)]
    slice x7 -> x1, local copies, waits for them, and re-layouts: 4.68 us -> 3.9 us  [on_device(): raw_after = lax.ppermute(padded[:width], 'ion', down)]
  transfers between devices with their start and end apart: 7 -> 5, of which waited for: 0 -> 2; matrix products, arithmetic and copies ran while one was open for 28% -> 34% of each run, Pallas kernels for 0% -> 0%
where the time goes in v9:
time: 182 us; the launch traced here: 179 us
  Pallas kernels  73.2 us (40%)
  local copies, waits for them, and re-layouts  53.2 us (29%)
  other arithmetic  33.3 us (18%)
  starting transfers between devices  13.8 us (8%)
  waiting for transfers between devices  2.78 us (2%)
    pallas_call x1, Pallas kernels, pair_grams(): pl.pallas_call(lambda *refs: gram_kernel(shares, *refs), out_shape=(jax.S...  43.3 us
    pallas_call x1, Pallas kernels, scatter_grams(): pl.pallas_call(scatter_kernel, out_shape=(jax.ShapeDtypeStruct(part, f32)...  29.9 us
    reduce_sum x2, other arithmetic, row_squares(): return jnp.sum(values * values, axis=1)  28.7 us
    concatenate x1, local copies, waits for them, and re-layouts, extended_2(): array = jnp.concatenate([before, array, after], axis=dim)  27.8 us
    unnamed x19, local copies, waits for them, and re-layouts  9.81 us
    ppermute x1, starting transfers between devices, on_device(): raw_after = lax.ppermute(padded[:width], 'ion', down)  5.63 us
    convert_element_type x2, local copies, waits for them, and re-layouts, smooth_rows(): return total.astype(jnp.bfloat16)  4.4 us
    slice x1, local copies, waits for them, and re-layouts, on_device(): raw_after = lax.ppermute(padded[:width], 'ion', down)  3.9 us
  transfers between devices with their start and end apart: 5, of which 2 were waited for; matrix products, arithmetic and copies ran while one was open for 34% of the time, Pallas kernels for 0%

profile of v9, /device:TPU:16, one launch (start us, length us, event | category | flops | bytes accessed | tf_op | source)
XLA Modules:
  0.0 179.0 jit_solution(6601582184356760356)
XLA Ops:
  0.6 0.0 copy-start
  0.6 0.0 copy-start.3
  0.7 0.0 copy-start.4
  0.7 7.9 %copy.10 = bf16[1280,2048]{0,1:T(8,128)(2,1)} copy(bf16[1280,2048]{1,0:T(8,128)(2,1)} %param.8) | data formatting | bytes 10485760 | tf_op args[0]
  8.6 0.8 fusion.26
  9.3 1.7 collective-permute-start
  11.1 1.3 collective-permute-start.1
  12.4 1.3 collective-permute-start.4
  13.7 0.0 copy-done.3
  13.7 0.0 copy-done.4
  13.8 0.5 compare_and_fusion.1
  14.3 0.0 copy-done
  14.3 0.8 gather_fusion
  15.1 0.5 and_bitcast_fusion
  15.6 0.6 pad_clamp_fusion
  16.9 0.6 pad_clamp_fusion.2
  17.5 0.6 iota_compare_fusion
  18.1 0.1 copy.14
  18.2 0.6 reshape.45.refs_0_
  18.8 0.0 collective-permute-done
  18.8 0.0 collective-permute-done.1
  18.8 27.8 %concatenate.16 = bf16[1280,2052]{0,1:T(8,128)(2,1)} concatenate(bf16[1280,2]{0,1:T(2,128)(2,1)S(1)} %collective-permute-done, bf16[1280,2048]{0,1:T(8,128)(2,1)} %copy.10, bf16[1280,2]{0,1:T(2,128)(2,1)S(1)} %collective-permute-done.1), dimensions={1} | concatenate | bytes 10506240 | tf_op jit(solution)/shard_map/concatenate | solution.py:20
  46.6 3.9 %fusion.25 = (bf16[384,2052]{0,1:T(8,128)(2,1)}, bf16[384,2052]{0,1:T(8,128)(2,1)}) fusion(bf16[1280,2052]{0,1:T(8,128)(2,1)} %concatenate.16), kind=kLoop, calls=%fused_computation.76 | loop fusion | bytes 6303744 | tf_op jit(solution)/shard_map/slice | solution.py:299
  50.5 3.8 %collective-permute-start.2 = (bf16[384,2052]{0,1:T(8,128)(2,1)}, bf16[384,2052]{0,1:T(8,128)(2,1)S(1)}, u32[]{:S(2)}, u32[]{:S(2)}) collective-permute-start(bf16[384,2052]{0,1:T(8,128)(2,1)} %get-tuple-element.24), channel_id=1, source_target_pairs={{0,1},{1,2},{2,3},{3,4},{4,5},{5,6},{6,7},{7,8},{8,9},{9,10},{10,1... | collective-permute-start | bytes 4727816 | tf_op jit(solution)/shard_map/ppermute | solution.py:298
  54.3 5.6 %collective-permute-start.3 = (bf16[384,2052]{0,1:T(8,128)(2,1)}, bf16[384,2052]{0,1:T(8,128)(2,1)S(1)}, u32[]{:S(2)}, u32[]{:S(2)}) collective-permute-start(bf16[384,2052]{0,1:T(8,128)(2,1)} %get-tuple-element.23), channel_id=1, source_target_pairs={{1,0},{2,1},{3,2},{4,3},{5,4},{6,5},{7,6},{8,7},{9,8},{10,9},{11,1... | collective-permute-start | bytes 4727816 | tf_op jit(solution)/shard_map/ppermute | solution.py:299
  60.0 0.2 copy.11
  60.2 0.9 copy.13
  61.1 22.8 %multiply_reduce_fusion = (f32[1280]{0:T(1024)S(1)}, bf16[1280,2048]{1,0:T(8,128)(2,1)}) fusion(bf16[1280,2]{1,0:T(8,128)(2,1)} %copy.13, bf16[1280,2048]{1,0:T(8,128)(2,1)} %param.8, f32[2048]{0:T(1024)S(1)} %bitcast.39, f32[2048]{0:T(1024)S(1)} %bitcast.41, f32[2048]{0:T(1024)S(1)} %bitcast.35, bf16[1280,2]{1,0:T(8,128)(2,1)S(1)} %copy.11, ...), kind=kLoop, calls=%fused_computation.4 | loop fusion | flops 78641920 | bytes 10542080 | tf_op jit(solution)/shard_map/reduce_sum | solution.py:272
  83.9 0.0 collective-permute-done.4
  83.9 1.6 broadcast_select_fusion.refs_4_
  85.5 0.6 collective-permute-done.2
  86.1 2.1 %collective-permute-done.3 = bf16[384,2052]{0,1:T(8,128)(2,1)S(1)} collective-permute-done((bf16[384,2052]{0,1:T(8,128)(2,1)}, bf16[384,2052]{0,1:T(8,128)(2,1)S(1)}, u32[]{:S(2)}, u32[]{:S(2)}) %collective-permute-start.3) | collective-permute-done | bytes 1575968 | tf_op jit(solution)/shard_map/ppermute | solution.py:299
  88.3 5.9 %multiply_reduce_fusion.1 = (f32[384]{0:T(512)S(1)}, bf16[384,2048]{0,1:T(8,128)(2,1)}, f32[384]{0:T(512)S(1)}, bf16[384,2048]{0,1:T(8,128)(2,1)}) fusion(bf16[384,2052]{0,1:T(8,128)(2,1)S(1)} %collective-permute-done.3, f32[2048]{0:T(1024)S(1)} %bitcast.40, f32[2048]{0:T(1024)S(1)} %bitcast.42, f32[2048]{0:T(1024)S(1)} %bitcast.36, f32[2048]{0:T(1024)S(1)} %bitcast.38, ...), kind=kLoop, calls=%fused_computation.14 | loop fusion | flops 28310784 | bytes 18918400 | tf_op jit(solution)/shard_map/reduce_sum | solution.py:272
  94.1 0.0 copy-start.2
  94.1 2.7 %copy.16 = bf16[384,2048]{1,0:T(8,128)(2,1)} copy(bf16[384,2048]{0,1:T(8,128)(2,1)} %get-tuple-element.33) | data formatting | bytes 3145728 | tf_op jit(solution)/shard_map/convert_element_type | solution.py:267
  96.9 0.0 copy-done.2
  96.9 1.7 copy.17
  98.6 43.3 %shard_map.77 = (f32[2,4,2,48,8,128]{5,4,3,2,1,0:T(8,128)}, bf16[16,4,128,128]{3,2,1,0:T(8,128)(2,1)}) custom-call(s32[96]{0:T(128)} %reshape.45.refs_0_, bf16[3,128,2048]{2,1,0:T(8,128)(2,1)} %bitcast.30, bf16[10,128,2048]{2,1,0:T(8,128)(2,1)} %bitcast.29, bf16[3,128,2048]{2,1,0:T(8,128)(2,1)} %bitcast.31, bf16[4,128,128]{2,1,0:T(8,128)(2,1)} %broadcast_select_fusion.refs_4_), custom_call_target="tpu_custom_call" | custom-call | flops 3221225472 | bytes 11534336 | tf_op jit(solution)/shard_map/pallas_call | solution.py:121
  141.9 0.0 copy-start.6
  141.9 0.0 copy-start.1
  141.9 1.9 %copy-done.1 = f32[2,4,2,48,8,128]{5,4,3,2,1,0:T(8,128)S(1)} copy-done((f32[2,4,2,48,8,128]{5,4,3,2,1,0:T(8,128)S(1)}, f32[2,4,2,48,8,128]{5,4,3,2,1,0:T(8,128)}, u32[]{:S(2)}) %copy-start.1) | copy-done | bytes 3145752
  143.8 0.0 copy-start.5
  143.8 0.0 copy-start.7
  143.8 0.0 copy-start.8
  143.8 29.9 %shard_map.78 = (f32[48,8,128]{2,1,0:T(8,128)S(1)}, f32[16,128]{1,0:T(8,128)S(1)}) custom-call(f32[2,4,2,48,8,128]{5,4,3,2,1,0:T(8,128)S(1)} %copy-done.1, f32[16,128]{1,0:T(8,128)S(1)} %maximum_bitcast_fusion.e_ref), custom_call_target="tpu_custom_call" | custom-call | tf_op jit(solution)/shard_map/pallas_call | solution.py:235
  173.7 0.7 gather_fusion.2
  174.4 0.6 gather_fusion.3
  175.0 0.0 copy-done.6
  175.0 0.1 broadcast_select_fusion.1
  175.1 2.6 %gather_fusion.1 = bf16[48,128,128]{2,1,0:T(8,128)(2,1)S(1)} fusion(bf16[64,128,128]{2,1,0:T(8,128)(2,1)} %bitcast.32, s32[1024]{0:T(1024)} %pad_clamp_fusion), kind=kCustom, calls=%fused_computation.3 | custom fusion | bytes 3145920 | tf_op jit(solution)/shard_map/jit(_take)/gather | solution.py:324
  177.7 0.0 copy-done.5
  177.7 0.1 dynamic-slice_select_fusion
  177.8 0.0 copy-done.7
  177.8 0.0 copy-done.8
  177.8 1.2 fusion.8
  (6 shorter events, 0.1 us)
Async XLA Ops:
  0.6 13.7 %copy-start = (s32[160]{0:T(256)S(1)}, s32[160]{0:T(256)}, u32[]{:S(2)}) copy-start(s32[160]{0:T(256)} %param.12) | copy-start | bytes 1924
  0.6 13.0 %copy-start.3 = (f32[5,2048]{1,0:T(8,128)S(1)}, f32[5,2048]{1,0:T(8,128)}, u32[]{:S(2)}) copy-start(f32[5,2048]{1,0:T(8,128)} %param.9) | copy-start | bytes 122884
  0.7 13.1 %copy-start.4 = (s32[48,2]{0,1:T(2,128)S(1)}, s32[48,2]{0,1:T(2,128)}, u32[]{:S(2)}) copy-start(s32[48,2]{0,1:T(2,128)} %param.10) | copy-start | bytes 1156
  9.3 9.5 %collective-permute-start = (bf16[1280,2]{0,1:T(2,128)(2,1)S(1)}, bf16[1280,2]{0,1:T(2,128)(2,1)S(1)}, u32[]{:S(2)}, u32[]{:S(2)}) collective-permute-start(bf16[1280,2]{0,1:T(2,128)(2,1)S(1)} %get-tuple-element.25), channel_id=1, source_target_pairs={{0,16},{16,32},{32,48},{48,64},{64,80},{80,96},{96,112},{112,128},... | collective-permute-start | bytes 15368 | tf_op jit(solution)/shard_map/ppermute | solution.py:18
  11.1 7.7 %collective-permute-start.1 = (bf16[1280,2]{0,1:T(2,128)(2,1)S(1)}, bf16[1280,2]{0,1:T(2,128)(2,1)S(1)}, u32[]{:S(2)}, u32[]{:S(2)}) collective-permute-start(bf16[1280,2]{0,1:T(2,128)(2,1)S(1)} %get-tuple-element.26), channel_id=1, source_target_pairs={{16,0},{32,16},{48,32},{64,48},{80,64},{96,80},{112,96},{128,112},... | collective-permute-start | bytes 15368 | tf_op jit(solution)/shard_map/ppermute | solution.py:19
  12.4 71.5 %collective-permute-start.4 = (bf16[4,128,128]{2,1,0:T(8,128)(2,1)}, bf16[4,128,128]{2,1,0:T(8,128)(2,1)}, u32[]{:S(2)}, u32[]{:S(2)}) collective-permute-start(bf16[4,128,128]{2,1,0:T(8,128)(2,1)} %param.13), channel_id=1, source_target_pairs={{16,31},{32,46},{48,61},{64,76},{80,91},{96,106},{112,121},{128,13... | collective-permute-start | bytes 393224 | tf_op jit(solution)/shard_map/ppermute | solution.py:295
  50.5 35.6 %collective-permute-start.2 = (bf16[384,2052]{0,1:T(8,128)(2,1)}, bf16[384,2052]{0,1:T(8,128)(2,1)S(1)}, u32[]{:S(2)}, u32[]{:S(2)}) collective-permute-start(bf16[384,2052]{0,1:T(8,128)(2,1)} %get-tuple-element.24), channel_id=1, source_target_pairs={{0,1},{1,2},{2,3},{3,4},{4,5},{5,6},{6,7},{7,8},{8,9},{9,10},{10,1... | collective-permute-start | bytes 4727816 | tf_op jit(solution)/shard_map/ppermute | solution.py:298
  54.3 33.9 %collective-permute-start.3 = (bf16[384,2052]{0,1:T(8,128)(2,1)}, bf16[384,2052]{0,1:T(8,128)(2,1)S(1)}, u32[]{:S(2)}, u32[]{:S(2)}) collective-permute-start(bf16[384,2052]{0,1:T(8,128)(2,1)} %get-tuple-element.23), channel_id=1, source_target_pairs={{1,0},{2,1},{3,2},{4,3},{5,4},{6,5},{7,6},{8,7},{9,8},{10,9},{11,1... | collective-permute-start | bytes 4727816 | tf_op jit(solution)/shard_map/ppermute | solution.py:299
  94.1 2.7 %copy-start.2 = (bf16[384,2048]{0,1:T(8,128)(2,1)S(1)}, bf16[384,2048]{0,1:T(8,128)(2,1)}, u32[]{:S(2)}) copy-start(bf16[384,2048]{0,1:T(8,128)(2,1)} %get-tuple-element.20) | copy-start | bytes 4718596
  141.9 33.1 %copy-start.6 = (pred[48]{0:T(512)(128)(4,1)S(1)}, pred[48]{0:T(512)(128)(4,1)}, u32[]{:S(2)}) copy-start(pred[48]{0:T(512)(128)(4,1)} %get-tuple-element.34) | copy-start | bytes 148
  141.9 1.9 %copy-start.1 = (f32[2,4,2,48,8,128]{5,4,3,2,1,0:T(8,128)S(1)}, f32[2,4,2,48,8,128]{5,4,3,2,1,0:T(8,128)}, u32[]{:S(2)}) copy-start(f32[2,4,2,48,8,128]{5,4,3,2,1,0:T(8,128)} %get-tuple-element.7.g_ref) | copy-start | bytes 9437188
  143.8 33.9 %copy-start.5 = (pred[48]{0:T(512)(128)(4,1)S(1)}, pred[48]{0:T(512)(128)(4,1)}, u32[]{:S(2)}) copy-start(pred[48]{0:T(512)(128)(4,1)} %get-tuple-element.11) | copy-start | bytes 148
  143.8 34.0 %copy-start.7 = (pred[48]{0:T(512)(128)(4,1)S(1)}, pred[48]{0:T(512)(128)(4,1)}, u32[]{:S(2)}) copy-start(pred[48]{0:T(512)(128)(4,1)} %get-tuple-element.21) | copy-start | bytes 148
  143.8 34.0 %copy-start.8 = (pred[48]{0:T(512)(128)(4,1)S(1)}, pred[48]{0:T(512)(128)(4,1)}, u32[]{:S(2)}) copy-start(pred[48]{0:T(512)(128)(4,1)} %iota_compare_fusion) | copy-start | bytes 148

commit v10 on v8

--- a/solution.py
+++ b/solution.py
@@ -294,12 +294,15 @@
         for j in range(ions)
         for p in range(1, shares)
     ]
-    fetched = lax.ppermute(adduct, ("pix", "ion"), turn)
-    own_turn = jnp.where(me_pix == 0, adduct, fetched)
     padded = extended_2(images, (("pix", 1),), 2)
     smoothed = smooth_rows(padded, stencil)
     local_squares = row_squares(smoothed)
     edges = jnp.concatenate([padded[:, :2], padded[:, pix_local + 2 :]], axis=1)
+    edges, late_adduct, smoothed, local_squares = lax.optimization_barrier(
+        (edges, adduct, smoothed, local_squares)
+    )
+    fetched = lax.ppermute(late_adduct, ("pix", "ion"), turn)
+    own_turn = jnp.where(me_pix == 0, late_adduct, fetched)
     edge_before = lax.ppermute(edges[local_rows - width :], "ion", up)
     edge_after = lax.ppermute(edges[:width], "ion", down)
     before = smooth_rows(

time: 148 us -> 157 us (1.061)
  waiting for transfers between devices: 0.02 us -> 5.5 us
  Pallas kernels: 68.5 us -> 71.1 us
    ppermute x1, waiting for transfers between devices: 0.01 us -> 5.48 us  [on_device(): edge_before = lax.ppermute(edges[local_rows - width:], 'ion', up)]
    pallas_call x1, Pallas kernels: 37.6 us -> 42.6 us  [pair_grams(): pl.pallas_call(lambda *refs: gram_kernel(shares, *refs), out_shape=(jax.S...]
    pallas_call x1, Pallas kernels: 30.9 us -> 28.5 us  [scatter_grams(): pl.pallas_call(scatter_kernel, out_shape=(jax.ShapeDtypeStruct(part, f32)...]
    ppermute x1, starting transfers between devices: 3.81 us -> 1.92 us  [on_device(): raw_before = lax.ppermute(images[local_rows - width:], 'ion', up)]
    ppermute x1, starting transfers between devices: 5.63 us -> 7.52 us  [on_device(): raw_after = lax.ppermute(images[:width], 'ion', down)]
  transfers between devices with their start and end apart: 7 -> 7, of which waited for: 0 -> 1; matrix products, arithmetic and copies ran while one was open for 28% -> 26% of each run, Pallas kernels for 0% -> 0%
where the time goes in v10:
time: 157 us; the launch traced here: 156 us
  Pallas kernels  71.1 us (45%)
  other arithmetic  37.6 us (24%)
  starting transfers between devices  23.4 us (15%)
  local copies, waits for them, and re-layouts  15.6 us (10%)
  waiting for transfers between devices  5.5 us (4%)
  between operations  1.62 us (1%)
    pallas_call x1, Pallas kernels, pair_grams(): pl.pallas_call(lambda *refs: gram_kernel(shares, *refs), out_shape=(jax.S...  42.6 us
    reduce_sum x3, other arithmetic, row_squares(): return jnp.sum(values * values, axis=1)  32.9 us
    pallas_call x1, Pallas kernels, scatter_grams(): pl.pallas_call(scatter_kernel, out_shape=(jax.ShapeDtypeStruct(part, f32)...  28.5 us
    ppermute x1, starting transfers between devices, on_device(): edge_after = lax.ppermute(edges[:width], 'ion', down)  7.54 us
    ppermute x1, starting transfers between devices, on_device(): raw_after = lax.ppermute(images[:width], 'ion', down)  7.52 us
    ppermute x1, waiting for transfers between devices, on_device(): edge_before = lax.ppermute(edges[local_rows - width:], 'ion', up)  5.48 us
    slice x1, local copies, waits for them, and re-layouts, on_device(): raw_after = lax.ppermute(images[:width], 'ion', down)  3.95 us
  transfers between devices with their start and end apart: 7, of which 1 were waited for; matrix products, arithmetic and copies ran while one was open for 26% of the time, Pallas kernels for 0%

profile of v10, /device:TPU:16, one launch (start us, length us, event | category | flops | bytes accessed | tf_op | source)
XLA Modules:
  0.0 155.9 jit_solution(5070638898008327099)
XLA Ops:
  0.6 0.0 copy-start
  0.6 1.2 fusion.30
  1.9 0.2 copy.19
  2.1 1.7 %collective-permute-start = (bf16[1280,2]{0,1:T(2,128)(2,1)S(1)}, bf16[1280,2]{0,1:T(2,128)(2,1)S(1)}, u32[]{:S(2)}, u32[]{:S(2)}) collective-permute-start(bf16[1280,2]{0,1:T(2,128)(2,1)S(1)} %copy.19), channel_id=1, source_target_pairs={{0,16},{16,32},{32,48},{48,64},{64,80},{80,96},{96,112},{112,128},... | collective-permute-start | bytes 15368 | tf_op jit(solution)/shard_map/ppermute | solution.py:18
  3.8 0.8 copy.20
  4.6 1.4 collective-permute-start.1
  6.0 4.0 %fusion.29 = (bf16[384,2048]{1,0:T(8,128)(2,1)}, bf16[384,2048]{1,0:T(8,128)(2,1)}) fusion(bf16[1280,2048]{1,0:T(8,128)(2,1)} %param.8), kind=kLoop, calls=%fused_computation.93 | loop fusion | bytes 6291456 | tf_op jit(solution)/shard_map/slice | solution.py:286
  10.0 7.5 %collective-permute-start.5 = (bf16[384,2048]{1,0:T(8,128)(2,1)}, bf16[384,2048]{1,0:T(8,128)(2,1)S(1)}, u32[]{:S(2)}, u32[]{:S(2)}) collective-permute-start(bf16[384,2048]{1,0:T(8,128)(2,1)} %get-tuple-element.31), channel_id=1, source_target_pairs={{1,0},{2,1},{3,2},{4,3},{5,4},{6,5},{7,6},{8,7},{9,8},{10,9},{11,1... | collective-permute-start | bytes 4718600 | tf_op jit(solution)/shard_map/ppermute | solution.py:286
  17.5 1.9 %collective-permute-start.3 = (bf16[384,2048]{1,0:T(8,128)(2,1)}, bf16[384,2048]{1,0:T(8,128)(2,1)S(1)}, u32[]{:S(2)}, u32[]{:S(2)}) collective-permute-start(bf16[384,2048]{1,0:T(8,128)(2,1)} %get-tuple-element.32), channel_id=1, source_target_pairs={{0,1},{1,2},{2,3},{3,4},{4,5},{5,6},{6,7},{7,8},{8,9},{9,10},{10,1... | collective-permute-start | bytes 4718600 | tf_op jit(solution)/shard_map/ppermute | solution.py:285
  19.4 0.0 copy-done.11
  19.5 0.0 copy-start.2
  19.5 0.0 copy-start.4
  19.5 0.0 copy-start.6
  19.5 0.0 copy-start.8
  19.5 0.0 copy-done.12
  19.6 0.6 compare_and_fusion.1
  20.1 0.0 copy-done
  20.2 0.8 gather_fusion
  20.9 0.6 and_bitcast_fusion
  21.5 0.6 pad_clamp_fusion.2
  22.1 0.6 pad_clamp_fusion
  23.4 0.0 collective-permute-done
  23.4 0.2 copy.12
  23.6 0.0 collective-permute-done.1
  23.6 0.9 copy.13
  24.5 23.2 %multiply_reduce_fusion = (f32[1280]{0:T(1024)}, bf16[1280,2048]{1,0:T(8,128)(2,1)}) fusion(bf16[1280,2]{1,0:T(8,128)(2,1)} %copy.13, bf16[1280,2048]{1,0:T(8,128)(2,1)} %param.8, f32[2048]{0:T(1024)S(1)} %bitcast.42, f32[2048]{0:T(1024)S(1)} %bitcast.45, f32[2048]{0:T(1024)S(1)} %bitcast.36, bf16[1280,2]{1,0:T(8,128)(2,1)S(1)} %copy.12, ...), kind=kLoop, calls=%fused_computation.4 | loop fusion | flops 78641920 | bytes 10542080 | tf_op jit(solution)/shard_map/reduce_sum | solution.py:272
  47.7 0.0 copy-done.2
  47.7 0.0 copy-done.4
  47.7 0.0 copy-done.6
  47.7 0.0 copy-done.8
  47.8 7.5 %collective-permute-start.4 = (bf16[384,4]{0,1:T(4,128)(2,1)S(1)}, bf16[384,4]{0,1:T(4,128)(2,1)S(1)}, u32[]{:S(2)}, u32[]{:S(2)}) collective-permute-start(bf16[384,4]{0,1:T(4,128)(2,1)S(1)} %get-tuple-element.40), channel_id=1, source_target_pairs={{1,0},{2,1},{3,2},{4,3},{5,4},{6,5},{7,6},{8,7},{9,8},{10,9},{11,1... | collective-permute-start | bytes 9224 | tf_op jit(solution)/shard_map/ppermute | solution.py:307
  55.3 0.6 iota_compare_fusion
  55.9 0.1 copy.14
  56.0 0.7 reshape.45.refs_0_
  56.7 1.9 %collective-permute-start.2 = (bf16[384,4]{0,1:T(4,128)(2,1)S(1)}, bf16[384,4]{0,1:T(4,128)(2,1)S(1)}, u32[]{:S(2)}, u32[]{:S(2)}) collective-permute-start(bf16[384,4]{0,1:T(4,128)(2,1)S(1)} %get-tuple-element.41), channel_id=1, source_target_pairs={{0,1},{1,2},{2,3},{3,4},{4,5},{5,6},{6,7},{7,8},{8,9},{9,10},{10,1... | collective-permute-start | bytes 9224 | tf_op jit(solution)/shard_map/ppermute | solution.py:306
  58.6 1.3 collective-permute-start.6
  59.9 0.0 collective-permute-done.4
  59.9 0.2 copy.17
  60.1 0.2 copy.18
  60.3 5.5 %collective-permute-done.2 = bf16[384,4]{0,1:T(4,128)(2,1)S(1)} collective-permute-done((bf16[384,4]{0,1:T(4,128)(2,1)S(1)}, bf16[384,4]{0,1:T(4,128)(2,1)S(1)}, u32[]{:S(2)}, u32[]{:S(2)}) %collective-permute-start.2) | collective-permute-done | bytes 3104 | tf_op jit(solution)/shard_map/ppermute | solution.py:306
  65.8 0.2 copy.15
  66.0 0.2 copy.16
  66.2 0.0 copy-start.5
  66.2 0.0 copy-start.7
  66.2 0.0 copy-start.9
  66.2 0.0 collective-permute-done.6
  66.2 1.6 %broadcast_select_fusion.refs_4_ = bf16[4,128,128]{2,1,0:T(8,128)(2,1)} fusion(bf16[4,128,128]{2,1,0:T(8,128)(2,1)} %param.13, bf16[4,128,128]{2,1,0:T(8,128)(2,1)} %collective-permute-done.6, pred[]{:T(512)S(6)} %eq.8), kind=kLoop, calls=%fused_computation.41 | loop fusion | flops 65536 | bytes 393217 | tf_op jit(solution)/shard_map/jit(_where)/select_n | solution.py:305
  67.8 0.0 collective-permute-done.5
  67.8 5.2 %multiply_reduce_fusion.1 = (f32[384]{0:T(512)S(1)}, bf16[384,2048]{1,0:T(8,128)(2,1)}) fusion(bf16[384,2]{1,0:T(8,128)(2,1)S(1)} %copy.18, bf16[384,2048]{1,0:T(8,128)(2,1)S(1)} %collective-permute-done.5, f32[2048]{0:T(1024)} %bitcast.43, f32[2048]{0:T(1024)} %bitcast.46, f32[2048]{0:T(1024)} %bitcast.37, bf16[384,2]{1,0:T(8,128)(2,1)S(1)} %copy.17, ...), kind=kLoop, calls=%fused_computation.14 | loop fusion | flops 23592576 | bytes 3191296 | tf_op jit(solution)/shard_map/reduce_sum | solution.py:272
  73.0 0.0 collective-permute-done.3
  73.0 0.0 copy-done.3
  73.0 0.0 copy-done.5
  73.0 4.5 %multiply_reduce_fusion.2 = (f32[384]{0:T(512)S(1)}, bf16[384,2048]{1,0:T(8,128)(2,1)}) fusion(bf16[384,2]{1,0:T(8,128)(2,1)S(1)} %copy.16, bf16[384,2048]{1,0:T(8,128)(2,1)S(1)} %collective-permute-done.3, f32[2048]{0:T(1024)S(1)} %bitcast.44, f32[2048]{0:T(1024)S(1)} %bitcast.47, f32[2048]{0:T(1024)S(1)} %bitcast.38, bf16[384,2]{1,0:T(8,128)(2,1)S(1)} %copy.15, ...), kind=kLoop, calls=%fused_computation.15 | loop fusion | flops 23592576 | bytes 3191296 | tf_op jit(solution)/shard_map/reduce_sum | solution.py:272
  77.5 0.0 copy-done.10
  77.5 42.6 %shard_map.77 = (f32[2,4,2,48,8,128]{5,4,3,2,1,0:T(8,128)}, bf16[16,4,128,128]{3,2,1,0:T(8,128)(2,1)}) custom-call(s32[96]{0:T(128)} %reshape.45.refs_0_, bf16[3,128,2048]{2,1,0:T(8,128)(2,1)} %bitcast.31, bf16[10,128,2048]{2,1,0:T(8,128)(2,1)} %bitcast.29, bf16[3,128,2048]{2,1,0:T(8,128)(2,1)} %bitcast.30, bf16[4,128,128]{2,1,0:T(8,128)(2,1)} %broadcast_select_fusion.refs_4_), custom_call_target="tpu_custom_call" | custom-call | flops 3221225472 | bytes 11534336 | tf_op jit(solution)/shard_map/pallas_call | solution.py:121
  120.1 1.9 %copy-done.1 = f32[2,4,2,48,8,128]{5,4,3,2,1,0:T(8,128)S(1)} copy-done((f32[2,4,2,48,8,128]{5,4,3,2,1,0:T(8,128)S(1)}, f32[2,4,2,48,8,128]{5,4,3,2,1,0:T(8,128)}, u32[]{:S(2)}) %copy-start.1) | copy-done | bytes 3145752
  122.0 28.5 %shard_map.78 = (f32[48,8,128]{2,1,0:T(8,128)S(1)}, f32[16,128]{1,0:T(8,128)S(1)}) custom-call(f32[2,4,2,48,8,128]{5,4,3,2,1,0:T(8,128)S(1)} %copy-done.1, f32[16,128]{1,0:T(8,128)S(1)} %maximum_bitcast_fusion.e_ref), custom_call_target="tpu_custom_call" | custom-call | tf_op jit(solution)/shard_map/pallas_call | solution.py:235
  150.5 0.7 gather_fusion.2
  151.2 0.7 gather_fusion.3
  151.9 0.0 copy-done.14
  151.9 0.1 broadcast_select_fusion.1
  152.0 2.6 %gather_fusion.1 = bf16[48,128,128]{2,1,0:T(8,128)(2,1)S(1)} fusion(bf16[64,128,128]{2,1,0:T(8,128)(2,1)} %bitcast.32, s32[1024]{0:T(1024)} %pad_clamp_fusion), kind=kCustom, calls=%fused_computation.3 | custom fusion | bytes 3145920 | tf_op jit(solution)/shard_map/jit(_take)/gather | solution.py:334
  154.6 0.1 dynamic-slice_select_fusion
  154.7 1.2 fusion.12
  (24 shorter events, 0.1 us)
Async XLA Ops:
  0.6 19.5 %copy-start = (s32[160]{0:T(256)S(1)}, s32[160]{0:T(256)}, u32[]{:S(2)}) copy-start(s32[160]{0:T(256)} %param.12) | copy-start | bytes 1924
  2.1 21.3 %collective-permute-start = (bf16[1280,2]{0,1:T(2,128)(2,1)S(1)}, bf16[1280,2]{0,1:T(2,128)(2,1)S(1)}, u32[]{:S(2)}, u32[]{:S(2)}) collective-permute-start(bf16[1280,2]{0,1:T(2,128)(2,1)S(1)} %copy.19), channel_id=1, source_target_pairs={{0,16},{16,32},{32,48},{48,64},{64,80},{80,96},{96,112},{112,128},... | collective-permute-start | bytes 15368 | tf_op jit(solution)/shard_map/ppermute | solution.py:18
  4.6 14.8 %copy-start.11 = (f32[5,2048]{1,0:T(8,128)S(1)}, f32[5,2048]{1,0:T(8,128)}, u32[]{:S(2)}) copy-start(f32[5,2048]{1,0:T(8,128)} %param.9) | copy-start | bytes 122884
  4.6 14.9 %copy-start.12 = (s32[48,2]{0,1:T(2,128)S(1)}, s32[48,2]{0,1:T(2,128)}, u32[]{:S(2)}) copy-start(s32[48,2]{0,1:T(2,128)} %param.10) | copy-start | bytes 1156
  4.6 19.0 %collective-permute-start.1 = (bf16[1280,2]{0,1:T(2,128)(2,1)}, bf16[1280,2]{0,1:T(2,128)(2,1)S(1)}, u32[]{:S(2)}, u32[]{:S(2)}) collective-permute-start(bf16[1280,2]{0,1:T(2,128)(2,1)} %copy.20), channel_id=1, source_target_pairs={{16,0},{32,16},{48,32},{64,48},{80,64},{96,80},{112,96},{128,112},... | collective-permute-start | bytes 15368 | tf_op jit(solution)/shard_map/ppermute | solution.py:19
  10.0 57.8 %collective-permute-start.5 = (bf16[384,2048]{1,0:T(8,128)(2,1)}, bf16[384,2048]{1,0:T(8,128)(2,1)S(1)}, u32[]{:S(2)}, u32[]{:S(2)}) collective-permute-start(bf16[384,2048]{1,0:T(8,128)(2,1)} %get-tuple-element.31), channel_id=1, source_target_pairs={{1,0},{2,1},{3,2},{4,3},{5,4},{6,5},{7,6},{8,7},{9,8},{10,9},{11,1... | collective-permute-start | bytes 4718600 | tf_op jit(solution)/shard_map/ppermute | solution.py:286
  17.5 55.5 %collective-permute-start.3 = (bf16[384,2048]{1,0:T(8,128)(2,1)}, bf16[384,2048]{1,0:T(8,128)(2,1)S(1)}, u32[]{:S(2)}, u32[]{:S(2)}) collective-permute-start(bf16[384,2048]{1,0:T(8,128)(2,1)} %get-tuple-element.32), channel_id=1, source_target_pairs={{0,1},{1,2},{2,3},{3,4},{4,5},{5,6},{6,7},{7,8},{8,9},{9,10},{10,1... | collective-permute-start | bytes 4718600 | tf_op jit(solution)/shard_map/ppermute | solution.py:285
  19.5 28.3 %copy-start.2 = (f32[1,2048]{1,0:T(1,128)}, f32[1,2048]{1,0:T(1,128)S(1)}, u32[]{:S(2)}) copy-start(f32[1,2048]{1,0:T(1,128)S(1)} %get-tuple-element.36) | copy-start | bytes 24580
  19.5 28.3 %copy-start.4 = (f32[1,2048]{1,0:T(1,128)}, f32[1,2048]{1,0:T(1,128)S(1)}, u32[]{:S(2)}) copy-start(f32[1,2048]{1,0:T(1,128)S(1)} %get-tuple-element.37) | copy-start | bytes 24580
  19.5 28.2 %copy-start.6 = (f32[1,2048]{1,0:T(1,128)}, f32[1,2048]{1,0:T(1,128)S(1)}, u32[]{:S(2)}) copy-start(f32[1,2048]{1,0:T(1,128)S(1)} %get-tuple-element.38) | copy-start | bytes 24580
  19.5 28.2 %copy-start.8 = (f32[1,2048]{1,0:T(1,128)}, f32[1,2048]{1,0:T(1,128)S(1)}, u32[]{:S(2)}) copy-start(f32[1,2048]{1,0:T(1,128)S(1)} %get-tuple-element.39) | copy-start | bytes 24580
  47.8 12.1 %collective-permute-start.4 = (bf16[384,4]{0,1:T(4,128)(2,1)S(1)}, bf16[384,4]{0,1:T(4,128)(2,1)S(1)}, u32[]{:S(2)}, u32[]{:S(2)}) collective-permute-start(bf16[384,4]{0,1:T(4,128)(2,1)S(1)} %get-tuple-element.40), channel_id=1, source_target_pairs={{1,0},{2,1},{3,2},{4,3},{5,4},{6,5},{7,6},{8,7},{9,8},{10,9},{11,1... | collective-permute-start | bytes 9224 | tf_op jit(solution)/shard_map/ppermute | solution.py:307
  56.7 9.1 %collective-permute-start.2 = (bf16[384,4]{0,1:T(4,128)(2,1)S(1)}, bf16[384,4]{0,1:T(4,128)(2,1)S(1)}, u32[]{:S(2)}, u32[]{:S(2)}) collective-permute-start(bf16[384,4]{0,1:T(4,128)(2,1)S(1)} %get-tuple-element.41), channel_id=1, source_target_pairs={{0,1},{1,2},{2,3},{3,4},{4,5},{5,6},{6,7},{7,8},{8,9},{9,10},{10,1... | collective-permute-start | bytes 9224 | tf_op jit(solution)/shard_map/ppermute | solution.py:306
  58.6 7.6 %collective-permute-start.6 = (bf16[4,128,128]{2,1,0:T(8,128)(2,1)}, bf16[4,128,128]{2,1,0:T(8,128)(2,1)}, u32[]{:S(2)}, u32[]{:S(2)}) collective-permute-start(bf16[4,128,128]{2,1,0:T(8,128)(2,1)} %param.13), channel_id=1, source_target_pairs={{16,31},{32,46},{48,61},{64,76},{80,91},{96,106},{112,121},{128,13... | collective-permute-start | bytes 393224 | tf_op jit(solution)/shard_map/ppermute | solution.py:304
  66.1 6.8 %copy-start.3 = (f32[1,2048]{1,0:T(1,128)S(1)}, f32[1,2048]{1,0:T(1,128)}, u32[]{:S(2)}) copy-start(f32[1,2048]{1,0:T(1,128)} %copy-done.2) | copy-start | bytes 24580
  66.2 6.8 %copy-start.5 = (f32[1,2048]{1,0:T(1,128)S(1)}, f32[1,2048]{1,0:T(1,128)}, u32[]{:S(2)}) copy-start(f32[1,2048]{1,0:T(1,128)} %copy-done.4) | copy-start | bytes 24580
  66.2 6.8 %copy-start.7 = (f32[1,2048]{1,0:T(1,128)S(1)}, f32[1,2048]{1,0:T(1,128)}, u32[]{:S(2)}) copy-start(f32[1,2048]{1,0:T(1,128)} %copy-done.6) | copy-start | bytes 24580
  66.2 6.8 %copy-start.9 = (f32[1,2048]{1,0:T(1,128)S(1)}, f32[1,2048]{1,0:T(1,128)}, u32[]{:S(2)}) copy-start(f32[1,2048]{1,0:T(1,128)} %copy-done.8) | copy-start | bytes 24580
  67.8 9.7 %copy-start.10 = (f32[1280]{0:T(1024)S(1)}, f32[1280]{0:T(1024)}, u32[]{:S(2)}) copy-start(f32[1280]{0:T(1024)} %get-tuple-element.15) | copy-start | bytes 15364
  120.1 31.8 %copy-start.14 = (pred[48]{0:T(512)(128)(4,1)S(1)}, pred[48]{0:T(512)(128)(4,1)}, u32[]{:S(2)}) copy-start(pred[48]{0:T(512)(128)(4,1)} %get-tuple-element.46) | copy-start | bytes 148
  120.1 1.9 %copy-start.1 = (f32[2,4,2,48,8,128]{5,4,3,2,1,0:T(8,128)S(1)}, f32[2,4,2,48,8,128]{5,4,3,2,1,0:T(8,128)}, u32[]{:S(2)}) copy-start(f32[2,4,2,48,8,128]{5,4,3,2,1,0:T(8,128)} %get-tuple-element.14.g_ref) | copy-start | bytes 9437188
  122.0 32.6 %copy-start.13 = (pred[48]{0:T(512)(128)(4,1)S(1)}, pred[48]{0:T(512)(128)(4,1)}, u32[]{:S(2)}) copy-start(pred[48]{0:T(512)(128)(4,1)} %get-tuple-element.19) | copy-start | bytes 148
  122.0 32.7 %copy-start.15 = (pred[48]{0:T(512)(128)(4,1)S(1)}, pred[48]{0:T(512)(128)(4,1)}, u32[]{:S(2)}) copy-start(pred[48]{0:T(512)(128)(4,1)} %get-tuple-element.27) | copy-start | bytes 148
  122.0 32.7 %copy-start.16 = (pred[48]{0:T(512)(128)(4,1)S(1)}, pred[48]{0:T(512)(128)(4,1)}, u32[]{:S(2)}) copy-start(pred[48]{0:T(512)(128)(4,1)} %iota_compare_fusion) | copy-start | bytes 148

commit v11 on v8

--- a/solution.py
+++ b/solution.py
@@ -300,6 +300,7 @@
     smoothed = smooth_rows(padded, stencil)
     local_squares = row_squares(smoothed)
     edges = jnp.concatenate([padded[:, :2], padded[:, pix_local + 2 :]], axis=1)
+    edges, smoothed, local_squares = lax.optimization_barrier((edges, smoothed, local_squares))
     edge_before = lax.ppermute(edges[local_rows - width :], "ion", up)
     edge_after = lax.ppermute(edges[:width], "ion", down)
     before = smooth_rows(

time: 148 us -> 152 us (1.027)
  waiting for transfers between devices: 0.02 us -> 6.79 us
  Pallas kernels: 68.5 us -> 66.1 us
    ppermute x1, waiting for transfers between devices: 0.01 us -> 6.78 us  [on_device(): edge_before = lax.ppermute(edges[local_rows - width:], 'ion', up)]
    pallas_call x1, Pallas kernels: 37.6 us -> 33.7 us  [pair_grams(): pl.pallas_call(lambda *refs: gram_kernel(shares, *refs), out_shape=(jax.S...]
    ppermute x1, starting transfers between devices: 3.81 us -> 1.92 us  [on_device(): raw_before = lax.ppermute(images[local_rows - width:], 'ion', up)]
    ppermute x1, starting transfers between devices: 5.63 us -> 7.52 us  [on_device(): raw_after = lax.ppermute(images[:width], 'ion', down)]
  transfers between devices with their start and end apart: 7 -> 7, of which waited for: 0 -> 1; matrix products, arithmetic and copies ran while one was open for 28% -> 27% of each run, Pallas kernels for 0% -> 0%
where the time goes in v11:
time: 152 us
  Pallas kernels  66.1 us (43%)
  other arithmetic  37.6 us (25%)
  starting transfers between devices  23.4 us (15%)
  local copies, waits for them, and re-layouts  15 us (10%)
  waiting for transfers between devices  6.79 us (4%)
  between operations  1.62 us (1%)
    pallas_call x1, Pallas kernels, pair_grams(): pl.pallas_call(lambda *refs: gram_kernel(shares, *refs), out_shape=(jax.S...  33.7 us
    reduce_sum x3, other arithmetic, row_squares(): return jnp.sum(values * values, axis=1)  32.9 us
    pallas_call x1, Pallas kernels, scatter_grams(): pl.pallas_call(scatter_kernel, out_shape=(jax.ShapeDtypeStruct(part, f32)...  32.4 us
    ppermute x1, starting transfers between devices, on_device(): edge_after = lax.ppermute(edges[:width], 'ion', down)  7.54 us
    ppermute x1, starting transfers between devices, on_device(): raw_after = lax.ppermute(images[:width], 'ion', down)  7.52 us
    ppermute x1, waiting for transfers between devices, on_device(): edge_before = lax.ppermute(edges[local_rows - width:], 'ion', up)  6.78 us
    slice x1, local copies, waits for them, and re-layouts, on_device(): raw_after = lax.ppermute(images[:width], 'ion', down)  3.95 us
  transfers between devices with their start and end apart: 7, of which 1 were waited for; matrix products, arithmetic and copies ran while one was open for 27% of the time, Pallas kernels for 0%

profile of v11, /device:TPU:16, one launch (start us, length us, event | category | flops | bytes accessed | tf_op | source)
XLA Modules:
  0.0 151.7 jit_solution(3443474801516398160)
XLA Ops:
  0.6 0.0 copy-start
  0.6 1.2 fusion.30
  1.9 0.2 copy.19
  2.1 1.7 %collective-permute-start = (bf16[1280,2]{0,1:T(2,128)(2,1)S(1)}, bf16[1280,2]{0,1:T(2,128)(2,1)S(1)}, u32[]{:S(2)}, u32[]{:S(2)}) collective-permute-start(bf16[1280,2]{0,1:T(2,128)(2,1)S(1)} %copy.19), channel_id=1, source_target_pairs={{0,16},{16,32},{32,48},{48,64},{64,80},{80,96},{96,112},{112,128},... | collective-permute-start | bytes 15368 | tf_op jit(solution)/shard_map/ppermute | solution.py:18
  3.8 0.2 copy.20
  4.0 1.4 collective-permute-start.1
  5.4 4.0 %fusion.29 = (bf16[384,2048]{1,0:T(8,128)(2,1)}, bf16[384,2048]{1,0:T(8,128)(2,1)}) fusion(bf16[1280,2048]{1,0:T(8,128)(2,1)} %param.8), kind=kLoop, calls=%fused_computation.93 | loop fusion | bytes 6291456 | tf_op jit(solution)/shard_map/slice | solution.py:286
  9.4 7.5 %collective-permute-start.5 = (bf16[384,2048]{1,0:T(8,128)(2,1)}, bf16[384,2048]{1,0:T(8,128)(2,1)S(1)}, u32[]{:S(2)}, u32[]{:S(2)}) collective-permute-start(bf16[384,2048]{1,0:T(8,128)(2,1)} %get-tuple-element.29), channel_id=1, source_target_pairs={{1,0},{2,1},{3,2},{4,3},{5,4},{6,5},{7,6},{8,7},{9,8},{10,9},{11,1... | collective-permute-start | bytes 4718600 | tf_op jit(solution)/shard_map/ppermute | solution.py:286
  16.9 1.9 %collective-permute-start.3 = (bf16[384,2048]{1,0:T(8,128)(2,1)}, bf16[384,2048]{1,0:T(8,128)(2,1)S(1)}, u32[]{:S(2)}, u32[]{:S(2)}) collective-permute-start(bf16[384,2048]{1,0:T(8,128)(2,1)} %get-tuple-element.30), channel_id=1, source_target_pairs={{0,1},{1,2},{2,3},{3,4},{4,5},{5,6},{6,7},{7,8},{8,9},{9,10},{10,1... | collective-permute-start | bytes 4718600 | tf_op jit(solution)/shard_map/ppermute | solution.py:285
  18.8 1.3 collective-permute-start.6
  20.2 0.0 copy-done.11
  20.2 0.0 copy-start.2
  20.2 0.0 copy-start.4
  20.2 0.0 copy-start.6
  20.2 0.0 copy-start.8
  20.2 0.0 copy-done.12
  20.3 0.6 compare_and_fusion.1
  20.9 0.0 copy-done
  20.9 0.8 gather_fusion
  21.7 0.6 and_bitcast_fusion
  22.2 0.6 pad_clamp_fusion.2
  22.8 0.6 pad_clamp_fusion
  24.1 0.0 collective-permute-done
  24.1 0.3 copy.12
  24.3 0.0 collective-permute-done.1
  24.4 0.9 copy.13
  25.3 23.2 %multiply_reduce_fusion = (f32[1280]{0:T(1024)}, bf16[1280,2048]{1,0:T(8,128)(2,1)}) fusion(bf16[1280,2]{1,0:T(8,128)(2,1)} %copy.13, bf16[1280,2048]{1,0:T(8,128)(2,1)} %param.8, f32[2048]{0:T(1024)S(1)} %bitcast.42, f32[2048]{0:T(1024)S(1)} %bitcast.45, f32[2048]{0:T(1024)S(1)} %bitcast.36, bf16[1280,2]{1,0:T(8,128)(2,1)S(1)} %copy.12, ...), kind=kLoop, calls=%fused_computation.4 | loop fusion | flops 78641920 | bytes 10542080 | tf_op jit(solution)/shard_map/reduce_sum | solution.py:272
  48.5 0.0 copy-done.2
  48.5 0.0 copy-done.4
  48.5 0.0 copy-done.6
  48.5 0.0 copy-done.8
  48.5 7.5 %collective-permute-start.4 = (bf16[384,4]{0,1:T(4,128)(2,1)S(1)}, bf16[384,4]{0,1:T(4,128)(2,1)S(1)}, u32[]{:S(2)}, u32[]{:S(2)}) collective-permute-start(bf16[384,4]{0,1:T(4,128)(2,1)S(1)} %get-tuple-element.38), channel_id=1, source_target_pairs={{1,0},{2,1},{3,2},{4,3},{5,4},{6,5},{7,6},{8,7},{9,8},{10,9},{11,1... | collective-permute-start | bytes 9224 | tf_op jit(solution)/shard_map/ppermute | solution.py:305
  56.1 0.6 iota_compare_fusion
  56.6 0.1 copy.14
  56.7 0.7 reshape.45.refs_0_
  57.4 1.9 %collective-permute-start.2 = (bf16[384,4]{0,1:T(4,128)(2,1)S(1)}, bf16[384,4]{0,1:T(4,128)(2,1)S(1)}, u32[]{:S(2)}, u32[]{:S(2)}) collective-permute-start(bf16[384,4]{0,1:T(4,128)(2,1)S(1)} %get-tuple-element.39), channel_id=1, source_target_pairs={{0,1},{1,2},{2,3},{3,4},{4,5},{5,6},{6,7},{7,8},{8,9},{9,10},{10,1... | collective-permute-start | bytes 9224 | tf_op jit(solution)/shard_map/ppermute | solution.py:304
  59.3 0.0 collective-permute-done.4
  59.3 0.2 copy.17
  59.5 0.2 copy.18
  59.7 6.8 %collective-permute-done.2 = bf16[384,4]{0,1:T(4,128)(2,1)S(1)} collective-permute-done((bf16[384,4]{0,1:T(4,128)(2,1)S(1)}, bf16[384,4]{0,1:T(4,128)(2,1)S(1)}, u32[]{:S(2)}, u32[]{:S(2)}) %collective-permute-start.2) | collective-permute-done | bytes 3104 | tf_op jit(solution)/shard_map/ppermute | solution.py:304
  66.5 0.2 copy.15
  66.7 0.2 copy.16
  66.9 0.0 copy-start.3
  66.9 0.0 copy-start.5
  66.9 0.0 collective-permute-done.6
  66.9 1.6 %broadcast_select_fusion.refs_4_ = bf16[4,128,128]{2,1,0:T(8,128)(2,1)} fusion(bf16[4,128,128]{2,1,0:T(8,128)(2,1)} %param.13, bf16[4,128,128]{2,1,0:T(8,128)(2,1)} %collective-permute-done.6, pred[]{:T(512)S(6)} %eq.8), kind=kLoop, calls=%fused_computation.41 | loop fusion | flops 65536 | bytes 393217 | tf_op jit(solution)/shard_map/jit(_where)/select_n | solution.py:298
  68.5 0.0 collective-permute-done.5
  68.5 5.2 %multiply_reduce_fusion.1 = (f32[384]{0:T(512)S(1)}, bf16[384,2048]{1,0:T(8,128)(2,1)}) fusion(bf16[384,2]{1,0:T(8,128)(2,1)S(1)} %copy.18, bf16[384,2048]{1,0:T(8,128)(2,1)S(1)} %collective-permute-done.5, f32[2048]{0:T(1024)} %bitcast.43, f32[2048]{0:T(1024)} %bitcast.46, f32[2048]{0:T(1024)} %bitcast.37, bf16[384,2]{1,0:T(8,128)(2,1)S(1)} %copy.17, ...), kind=kLoop, calls=%fused_computation.14 | loop fusion | flops 23592576 | bytes 3191296 | tf_op jit(solution)/shard_map/reduce_sum | solution.py:272
  73.7 0.0 collective-permute-done.3
  73.7 0.0 copy-done.3
  73.7 0.0 copy-done.5
  73.7 0.0 copy-done.7
  73.7 0.0 copy-done.9
  73.8 4.5 %multiply_reduce_fusion.2 = (f32[384]{0:T(512)S(1)}, bf16[384,2048]{1,0:T(8,128)(2,1)}) fusion(bf16[384,2]{1,0:T(8,128)(2,1)S(1)} %copy.16, bf16[384,2048]{1,0:T(8,128)(2,1)S(1)} %collective-permute-done.3, f32[2048]{0:T(1024)S(1)} %bitcast.44, f32[2048]{0:T(1024)S(1)} %bitcast.47, f32[2048]{0:T(1024)S(1)} %bitcast.38, bf16[384,2]{1,0:T(8,128)(2,1)S(1)} %copy.15, ...), kind=kLoop, calls=%fused_computation.15 | loop fusion | flops 23592576 | bytes 3191296 | tf_op jit(solution)/shard_map/reduce_sum | solution.py:272
  78.2 33.7 %shard_map.77 = (f32[2,4,2,48,8,128]{5,4,3,2,1,0:T(8,128)}, bf16[16,4,128,128]{3,2,1,0:T(8,128)(2,1)}) custom-call(s32[96]{0:T(128)} %reshape.45.refs_0_, bf16[3,128,2048]{2,1,0:T(8,128)(2,1)} %bitcast.31, bf16[10,128,2048]{2,1,0:T(8,128)(2,1)} %bitcast.29, bf16[3,128,2048]{2,1,0:T(8,128)(2,1)} %bitcast.30, bf16[4,128,128]{2,1,0:T(8,128)(2,1)} %broadcast_select_fusion.refs_4_), custom_call_target="tpu_custom_call" | custom-call | flops 3221225472 | bytes 11534336 | tf_op jit(solution)/shard_map/pallas_call | solution.py:121
  112.0 1.9 %copy-done.1 = f32[2,4,2,48,8,128]{5,4,3,2,1,0:T(8,128)S(1)} copy-done((f32[2,4,2,48,8,128]{5,4,3,2,1,0:T(8,128)S(1)}, f32[2,4,2,48,8,128]{5,4,3,2,1,0:T(8,128)}, u32[]{:S(2)}) %copy-start.1) | copy-done | bytes 3145752
  113.9 32.4 %shard_map.78 = (f32[48,8,128]{2,1,0:T(8,128)S(1)}, f32[16,128]{1,0:T(8,128)S(1)}) custom-call(f32[2,4,2,48,8,128]{5,4,3,2,1,0:T(8,128)S(1)} %copy-done.1, f32[16,128]{1,0:T(8,128)S(1)} %maximum_bitcast_fusion.e_ref), custom_call_target="tpu_custom_call" | custom-call | tf_op jit(solution)/shard_map/pallas_call | solution.py:235
  146.3 0.7 gather_fusion.2
  147.0 0.7 gather_fusion.3
  147.7 0.1 broadcast_select_fusion.1
  147.8 2.6 %gather_fusion.1 = bf16[48,128,128]{2,1,0:T(8,128)(2,1)S(1)} fusion(bf16[64,128,128]{2,1,0:T(8,128)(2,1)} %bitcast.32, s32[1024]{0:T(1024)} %pad_clamp_fusion), kind=kCustom, calls=%fused_computation.3 | custom fusion | bytes 3145920 | tf_op jit(solution)/shard_map/jit(_take)/gather | solution.py:332
  150.4 0.0 copy-done.13
  150.4 0.1 dynamic-slice_select_fusion
  150.5 1.2 fusion.12
  (24 shorter events, 0.1 us)
Async XLA Ops:
  0.6 20.2 %copy-start = (s32[160]{0:T(256)S(1)}, s32[160]{0:T(256)}, u32[]{:S(2)}) copy-start(s32[160]{0:T(256)} %param.12) | copy-start | bytes 1924
  2.1 22.0 %collective-permute-start = (bf16[1280,2]{0,1:T(2,128)(2,1)S(1)}, bf16[1280,2]{0,1:T(2,128)(2,1)S(1)}, u32[]{:S(2)}, u32[]{:S(2)}) collective-permute-start(bf16[1280,2]{0,1:T(2,128)(2,1)S(1)} %copy.19), channel_id=1, source_target_pairs={{0,16},{16,32},{32,48},{48,64},{64,80},{80,96},{96,112},{112,128},... | collective-permute-start | bytes 15368 | tf_op jit(solution)/shard_map/ppermute | solution.py:18
  4.0 16.2 %copy-start.11 = (f32[5,2048]{1,0:T(8,128)S(1)}, f32[5,2048]{1,0:T(8,128)}, u32[]{:S(2)}) copy-start(f32[5,2048]{1,0:T(8,128)} %param.9) | copy-start | bytes 122884
  4.0 16.2 %copy-start.12 = (s32[48,2]{0,1:T(2,128)S(1)}, s32[48,2]{0,1:T(2,128)}, u32[]{:S(2)}) copy-start(s32[48,2]{0,1:T(2,128)} %param.10) | copy-start | bytes 1156
  4.0 20.4 %collective-permute-start.1 = (bf16[1280,2]{0,1:T(2,128)(2,1)S(1)}, bf16[1280,2]{0,1:T(2,128)(2,1)S(1)}, u32[]{:S(2)}, u32[]{:S(2)}) collective-permute-start(bf16[1280,2]{0,1:T(2,128)(2,1)S(1)} %copy.20), channel_id=1, source_target_pairs={{16,0},{32,16},{48,32},{64,48},{80,64},{96,80},{112,96},{128,112},... | collective-permute-start | bytes 15368 | tf_op jit(solution)/shard_map/ppermute | solution.py:19
  9.4 59.1 %collective-permute-start.5 = (bf16[384,2048]{1,0:T(8,128)(2,1)}, bf16[384,2048]{1,0:T(8,128)(2,1)S(1)}, u32[]{:S(2)}, u32[]{:S(2)}) collective-permute-start(bf16[384,2048]{1,0:T(8,128)(2,1)} %get-tuple-element.29), channel_id=1, source_target_pairs={{1,0},{2,1},{3,2},{4,3},{5,4},{6,5},{7,6},{8,7},{9,8},{10,9},{11,1... | collective-permute-start | bytes 4718600 | tf_op jit(solution)/shard_map/ppermute | solution.py:286
  16.9 56.8 %collective-permute-start.3 = (bf16[384,2048]{1,0:T(8,128)(2,1)}, bf16[384,2048]{1,0:T(8,128)(2,1)S(1)}, u32[]{:S(2)}, u32[]{:S(2)}) collective-permute-start(bf16[384,2048]{1,0:T(8,128)(2,1)} %get-tuple-element.30), channel_id=1, source_target_pairs={{0,1},{1,2},{2,3},{3,4},{4,5},{5,6},{6,7},{7,8},{8,9},{9,10},{10,1... | collective-permute-start | bytes 4718600 | tf_op jit(solution)/shard_map/ppermute | solution.py:285
  18.8 48.1 %collective-permute-start.6 = (bf16[4,128,128]{2,1,0:T(8,128)(2,1)}, bf16[4,128,128]{2,1,0:T(8,128)(2,1)}, u32[]{:S(2)}, u32[]{:S(2)}) collective-permute-start(bf16[4,128,128]{2,1,0:T(8,128)(2,1)} %param.13), channel_id=1, source_target_pairs={{16,31},{32,46},{48,61},{64,76},{80,91},{96,106},{112,121},{128,13... | collective-permute-start | bytes 393224 | tf_op jit(solution)/shard_map/ppermute | solution.py:297
  20.2 28.3 %copy-start.2 = (f32[1,2048]{1,0:T(1,128)}, f32[1,2048]{1,0:T(1,128)S(1)}, u32[]{:S(2)}) copy-start(f32[1,2048]{1,0:T(1,128)S(1)} %get-tuple-element.34) | copy-start | bytes 24580
  20.2 28.3 %copy-start.4 = (f32[1,2048]{1,0:T(1,128)}, f32[1,2048]{1,0:T(1,128)S(1)}, u32[]{:S(2)}) copy-start(f32[1,2048]{1,0:T(1,128)S(1)} %get-tuple-element.35) | copy-start | bytes 24580
  20.2 28.3 %copy-start.6 = (f32[1,2048]{1,0:T(1,128)}, f32[1,2048]{1,0:T(1,128)S(1)}, u32[]{:S(2)}) copy-start(f32[1,2048]{1,0:T(1,128)S(1)} %get-tuple-element.36) | copy-start | bytes 24580
  20.2 28.3 %copy-start.8 = (f32[1,2048]{1,0:T(1,128)}, f32[1,2048]{1,0:T(1,128)S(1)}, u32[]{:S(2)}) copy-start(f32[1,2048]{1,0:T(1,128)S(1)} %get-tuple-element.37) | copy-start | bytes 24580
  48.5 10.8 %collective-permute-start.4 = (bf16[384,4]{0,1:T(4,128)(2,1)S(1)}, bf16[384,4]{0,1:T(4,128)(2,1)S(1)}, u32[]{:S(2)}, u32[]{:S(2)}) collective-permute-start(bf16[384,4]{0,1:T(4,128)(2,1)S(1)} %get-tuple-element.38), channel_id=1, source_target_pairs={{1,0},{2,1},{3,2},{4,3},{5,4},{6,5},{7,6},{8,7},{9,8},{10,9},{11,1... | collective-permute-start | bytes 9224 | tf_op jit(solution)/shard_map/ppermute | solution.py:305
  57.4 9.1 %collective-permute-start.2 = (bf16[384,4]{0,1:T(4,128)(2,1)S(1)}, bf16[384,4]{0,1:T(4,128)(2,1)S(1)}, u32[]{:S(2)}, u32[]{:S(2)}) collective-permute-start(bf16[384,4]{0,1:T(4,128)(2,1)S(1)} %get-tuple-element.39), channel_id=1, source_target_pairs={{0,1},{1,2},{2,3},{3,4},{4,5},{5,6},{6,7},{7,8},{8,9},{9,10},{10,1... | collective-permute-start | bytes 9224 | tf_op jit(solution)/shard_map/ppermute | solution.py:304
  66.9 6.8 %copy-start.3 = (f32[1,2048]{1,0:T(1,128)S(1)}, f32[1,2048]{1,0:T(1,128)}, u32[]{:S(2)}) copy-start(f32[1,2048]{1,0:T(1,128)} %copy-done.2) | copy-start | bytes 24580
  66.9 6.8 %copy-start.5 = (f32[1,2048]{1,0:T(1,128)S(1)}, f32[1,2048]{1,0:T(1,128)}, u32[]{:S(2)}) copy-start(f32[1,2048]{1,0:T(1,128)} %copy-done.4) | copy-start | bytes 24580
  66.9 6.8 %copy-start.7 = (f32[1,2048]{1,0:T(1,128)S(1)}, f32[1,2048]{1,0:T(1,128)}, u32[]{:S(2)}) copy-start(f32[1,2048]{1,0:T(1,128)} %copy-done.6) | copy-start | bytes 24580
  66.9 6.8 %copy-start.9 = (f32[1,2048]{1,0:T(1,128)S(1)}, f32[1,2048]{1,0:T(1,128)}, u32[]{:S(2)}) copy-start(f32[1,2048]{1,0:T(1,128)} %copy-done.8) | copy-start | bytes 24580
  68.5 9.7 %copy-start.10 = (f32[1280]{0:T(1024)S(1)}, f32[1280]{0:T(1024)}, u32[]{:S(2)}) copy-start(f32[1280]{0:T(1024)} %get-tuple-element.13) | copy-start | bytes 15364
  111.9 35.8 %copy-start.14 = (pred[48]{0:T(512)(128)(4,1)S(1)}, pred[48]{0:T(512)(128)(4,1)}, u32[]{:S(2)}) copy-start(pred[48]{0:T(512)(128)(4,1)} %get-tuple-element.44) | copy-start | bytes 148
  112.0 1.9 %copy-start.1 = (f32[2,4,2,48,8,128]{5,4,3,2,1,0:T(8,128)S(1)}, f32[2,4,2,48,8,128]{5,4,3,2,1,0:T(8,128)}, u32[]{:S(2)}) copy-start(f32[2,4,2,48,8,128]{5,4,3,2,1,0:T(8,128)} %get-tuple-element.12.g_ref) | copy-start | bytes 9437188
  113.8 36.5 %copy-start.13 = (pred[48]{0:T(512)(128)(4,1)S(1)}, pred[48]{0:T(512)(128)(4,1)}, u32[]{:S(2)}) copy-start(pred[48]{0:T(512)(128)(4,1)} %get-tuple-element.17) | copy-start | bytes 148
  113.8 36.6 %copy-start.15 = (pred[48]{0:T(512)(128)(4,1)S(1)}, pred[48]{0:T(512)(128)(4,1)}, u32[]{:S(2)}) copy-start(pred[48]{0:T(512)(128)(4,1)} %get-tuple-element.25) | copy-start | bytes 148
  113.8 36.6 %copy-start.16 = (pred[48]{0:T(512)(128)(4,1)S(1)}, pred[48]{0:T(512)(128)(4,1)}, u32[]{:S(2)}) copy-start(pred[48]{0:T(512)(128)(4,1)} %iota_compare_fusion) | copy-start | bytes 148

commit v12 on v8

--- a/solution.py
+++ b/solution.py
@@ -79,7 +79,7 @@
             out_ref[q % 2, (q // 2) % 4, q // 8, s] = g[q * rows : (q + 1) * rows, :]
         return carry
 
-    third = slots // 3
+    third = slots // 4
     lax.fori_loop(0, third, body, 0)
     ca.wait_recv()
     b1 = [
@@ -97,12 +97,13 @@
     b2 = remote(table.at[pl.ds(from_left, 2)], table.at[pl.ds(from_left, 2)], 5, right)
     b2.start()
     sent.append(b2)
-    lax.fori_loop(2 * third, slots, body, 0)
+    lax.fori_loop(2 * third, 3 * third, body, 0)
     b2.wait_recv()
     own.wait()
     cc = remote(table.at[pl.ds(c * 8, 8)], table.at[pl.ds(c * 8, 8)], 6, partner)
     cc.start()
     sent.append(cc)
+    lax.fori_loop(3 * third, slots, body, 0)
     cc.wait_recv()
     for cp in sent:
         cp.wait_send()

time: 148 us -> 148 us (level)
  transfers between devices with their start and end apart: 7 -> 7, of which waited for: 0 -> 0; matrix products, arithmetic and copies ran while one was open for 28% -> 27% of each run, Pallas kernels for 0% -> 0%
where the time goes in v12:
time: 148 us; the launch traced here: 147 us
  Pallas kernels  68.6 us (46%)
  other arithmetic  37.6 us (25%)
  starting transfers between devices  23.4 us (16%)
  local copies, waits for them, and re-layouts  14.9 us (10%)
  between operations  1.61 us (1%)
    pallas_call x1, Pallas kernels, pair_grams(): pl.pallas_call(lambda *refs: gram_kernel(shares, *refs), out_shape=(jax.S...  38.8 us
    reduce_sum x3, other arithmetic, row_squares(): return jnp.sum(values * values, axis=1)  32.9 us
    pallas_call x1, Pallas kernels, scatter_grams(): pl.pallas_call(scatter_kernel, out_shape=(jax.ShapeDtypeStruct(part, f32)...  29.8 us
    ppermute x1, starting transfers between devices, on_device(): edge_after = lax.ppermute(edges[:width], 'ion', down)  7.54 us
    ppermute x1, starting transfers between devices, on_device(): raw_after = lax.ppermute(images[:width], 'ion', down)  5.63 us
    slice x1, local copies, waits for them, and re-layouts, on_device(): raw_after = lax.ppermute(images[:width], 'ion', down)  3.93 us
    ppermute x1, starting transfers between devices, on_device(): raw_before = lax.ppermute(images[local_rows - width:], 'ion', up)  3.81 us
  transfers between devices with their start and end apart: 7, of which 0 were waited for; matrix products, arithmetic and copies ran while one was open for 27% of the time, Pallas kernels for 0%

profile of v12, /device:TPU:16, one launch (start us, length us, event | category | flops | bytes accessed | tf_op | source)
XLA Modules:
  0.0 147.4 jit_solution(4988802465380045669)
XLA Ops:
  0.6 0.0 copy-start
  0.6 1.2 fusion.30
  1.9 0.2 copy.19
  2.1 1.7 %collective-permute-start = (bf16[1280,2]{0,1:T(2,128)(2,1)S(1)}, bf16[1280,2]{0,1:T(2,128)(2,1)S(1)}, u32[]{:S(2)}, u32[]{:S(2)}) collective-permute-start(bf16[1280,2]{0,1:T(2,128)(2,1)S(1)} %copy.19), channel_id=1, source_target_pairs={{0,16},{16,32},{32,48},{48,64},{64,80},{80,96},{96,112},{112,128},... | collective-permute-start | bytes 15368 | tf_op jit(solution)/shard_map/ppermute | solution.py:18
  3.8 0.2 copy.20
  4.0 1.4 collective-permute-start.1
  5.4 3.9 %fusion.29 = (bf16[384,2048]{1,0:T(8,128)(2,1)}, bf16[384,2048]{1,0:T(8,128)(2,1)}) fusion(bf16[1280,2048]{1,0:T(8,128)(2,1)} %param.8), kind=kLoop, calls=%fused_computation.94 | loop fusion | bytes 6291456 | tf_op jit(solution)/shard_map/slice | solution.py:287
  9.4 3.8 %collective-permute-start.3 = (bf16[384,2048]{1,0:T(8,128)(2,1)}, bf16[384,2048]{1,0:T(8,128)(2,1)S(1)}, u32[]{:S(2)}, u32[]{:S(2)}) collective-permute-start(bf16[384,2048]{1,0:T(8,128)(2,1)} %get-tuple-element.24), channel_id=1, source_target_pairs={{0,1},{1,2},{2,3},{3,4},{4,5},{5,6},{6,7},{7,8},{8,9},{9,10},{10,1... | collective-permute-start | bytes 4718600 | tf_op jit(solution)/shard_map/ppermute | solution.py:286
  13.2 5.6 %collective-permute-start.5 = (bf16[384,2048]{1,0:T(8,128)(2,1)}, bf16[384,2048]{1,0:T(8,128)(2,1)S(1)}, u32[]{:S(2)}, u32[]{:S(2)}) collective-permute-start(bf16[384,2048]{1,0:T(8,128)(2,1)} %get-tuple-element.23), channel_id=1, source_target_pairs={{1,0},{2,1},{3,2},{4,3},{5,4},{6,5},{7,6},{8,7},{9,8},{10,9},{11,1... | collective-permute-start | bytes 4718600 | tf_op jit(solution)/shard_map/ppermute | solution.py:287
  18.8 1.3 collective-permute-start.6
  20.1 0.0 copy-done.11
  20.2 0.0 copy-start.2
  20.2 0.0 copy-start.4
  20.2 0.0 copy-start.6
  20.2 0.0 copy-start.8
  20.2 0.0 copy-done.12
  20.2 0.6 compare_and_fusion.1
  20.8 0.0 copy-done
  20.8 0.8 gather_fusion
  21.6 0.6 and_bitcast_fusion
  22.2 0.6 pad_clamp_fusion
  23.4 0.6 pad_clamp_fusion.2
  24.0 0.6 iota_compare_fusion
  24.6 0.1 copy.14
  24.7 0.7 reshape.45.refs_0_
  25.4 0.0 collective-permute-done
  25.4 0.0 collective-permute-done.1
  25.4 1.9 %collective-permute-start.2 = (bf16[384,4]{0,1:T(4,128)(2,1)S(1)}, bf16[384,4]{0,1:T(4,128)(2,1)S(1)}, u32[]{:S(2)}, u32[]{:S(2)}) collective-permute-start(bf16[384,4]{0,1:T(4,128)(2,1)S(1)} %get-tuple-element.33), channel_id=1, source_target_pairs={{0,1},{1,2},{2,3},{3,4},{4,5},{5,6},{6,7},{7,8},{8,9},{9,10},{10,1... | collective-permute-start | bytes 9224 | tf_op jit(solution)/shard_map/ppermute | solution.py:304
  27.3 7.5 %collective-permute-start.4 = (bf16[384,4]{0,1:T(4,128)(2,1)S(1)}, bf16[384,4]{0,1:T(4,128)(2,1)S(1)}, u32[]{:S(2)}, u32[]{:S(2)}) collective-permute-start(bf16[384,4]{0,1:T(4,128)(2,1)S(1)} %get-tuple-element.32), channel_id=1, source_target_pairs={{1,0},{2,1},{3,2},{4,3},{5,4},{6,5},{7,6},{8,7},{9,8},{10,9},{11,1... | collective-permute-start | bytes 9224 | tf_op jit(solution)/shard_map/ppermute | solution.py:305
  34.9 0.2 copy.11
  35.1 0.9 copy.13
  36.0 23.2 %multiply_reduce_fusion = (f32[1280]{0:T(1024)}, bf16[1280,2048]{1,0:T(8,128)(2,1)}) fusion(bf16[1280,2]{1,0:T(8,128)(2,1)} %copy.13, bf16[1280,2048]{1,0:T(8,128)(2,1)} %param.8, f32[2048]{0:T(1024)S(1)} %bitcast.42, f32[2048]{0:T(1024)S(1)} %bitcast.45, f32[2048]{0:T(1024)S(1)} %bitcast.36, bf16[1280,2]{1,0:T(8,128)(2,1)S(1)} %copy.11, ...), kind=kLoop, calls=%fused_computation.4 | loop fusion | flops 78641920 | bytes 10542080 | tf_op jit(solution)/shard_map/reduce_sum | solution.py:273
  59.2 0.0 copy-done.2
  59.2 0.0 copy-done.4
  59.3 0.0 copy-done.6
  59.3 0.0 copy-done.8
  59.3 0.0 collective-permute-done.2
  59.3 0.2 copy.15
  59.5 0.2 copy.16
  59.7 0.0 collective-permute-done.4
  59.7 0.2 copy.17
  59.9 0.2 copy.18
  60.1 0.0 copy-start.5
  60.1 0.0 collective-permute-done.6
  60.1 1.6 %broadcast_select_fusion.refs_4_ = bf16[4,128,128]{2,1,0:T(8,128)(2,1)} fusion(bf16[4,128,128]{2,1,0:T(8,128)(2,1)} %param.13, bf16[4,128,128]{2,1,0:T(8,128)(2,1)} %collective-permute-done.6, pred[]{:T(512)S(6)} %eq.8), kind=kLoop, calls=%fused_computation.41 | loop fusion | flops 65536 | bytes 393217 | tf_op jit(solution)/shard_map/jit(_where)/select_n | solution.py:299
  61.7 0.0 collective-permute-done.3
  61.7 5.2 %multiply_reduce_fusion.2 = (f32[384]{0:T(512)S(1)}, bf16[384,2048]{1,0:T(8,128)(2,1)}) fusion(bf16[384,2]{1,0:T(8,128)(2,1)S(1)} %copy.16, bf16[384,2048]{1,0:T(8,128)(2,1)S(1)} %collective-permute-done.3, f32[2048]{0:T(1024)} %bitcast.43, f32[2048]{0:T(1024)} %bitcast.46, f32[2048]{0:T(1024)} %bitcast.37, bf16[384,2]{1,0:T(8,128)(2,1)S(1)} %copy.15, ...), kind=kLoop, calls=%fused_computation.15 | loop fusion | flops 23592576 | bytes 3191296 | tf_op jit(solution)/shard_map/reduce_sum | solution.py:273
  66.9 0.0 collective-permute-done.5
  66.9 0.0 copy-done.5
  66.9 0.0 copy-done.7
  66.9 0.0 copy-done.9
  66.9 4.5 %multiply_reduce_fusion.1 = (f32[384]{0:T(512)S(1)}, bf16[384,2048]{1,0:T(8,128)(2,1)}) fusion(bf16[384,2]{1,0:T(8,128)(2,1)S(1)} %copy.18, bf16[384,2048]{1,0:T(8,128)(2,1)S(1)} %collective-permute-done.5, f32[2048]{0:T(1024)S(1)} %bitcast.44, f32[2048]{0:T(1024)S(1)} %bitcast.47, f32[2048]{0:T(1024)S(1)} %bitcast.38, bf16[384,2]{1,0:T(8,128)(2,1)S(1)} %copy.17, ...), kind=kLoop, calls=%fused_computation.14 | loop fusion | flops 23592576 | bytes 3191296 | tf_op jit(solution)/shard_map/reduce_sum | solution.py:273
  71.4 38.8 %shard_map.77 = (f32[2,4,2,48,8,128]{5,4,3,2,1,0:T(8,128)}, bf16[16,4,128,128]{3,2,1,0:T(8,128)(2,1)}) custom-call(s32[96]{0:T(128)} %reshape.45.refs_0_, bf16[3,128,2048]{2,1,0:T(8,128)(2,1)} %bitcast.30, bf16[10,128,2048]{2,1,0:T(8,128)(2,1)} %bitcast.29, bf16[3,128,2048]{2,1,0:T(8,128)(2,1)} %bitcast.31, bf16[4,128,128]{2,1,0:T(8,128)(2,1)} %broadcast_select_fusion.refs_4_), custom_call_target="tpu_custom_call" | custom-call | flops 3221225472 | bytes 11534336 | tf_op jit(solution)/shard_map/pallas_call | solution.py:122
  110.2 0.0 copy-start.14
  110.2 0.0 copy-start.1
  110.3 1.9 %copy-done.1 = f32[2,4,2,48,8,128]{5,4,3,2,1,0:T(8,128)S(1)} copy-done((f32[2,4,2,48,8,128]{5,4,3,2,1,0:T(8,128)S(1)}, f32[2,4,2,48,8,128]{5,4,3,2,1,0:T(8,128)}, u32[]{:S(2)}) %copy-start.1) | copy-done | bytes 3145752
  112.1 29.8 %shard_map.78 = (f32[48,8,128]{2,1,0:T(8,128)S(1)}, f32[16,128]{1,0:T(8,128)S(1)}) custom-call(f32[2,4,2,48,8,128]{5,4,3,2,1,0:T(8,128)S(1)} %copy-done.1, f32[16,128]{1,0:T(8,128)S(1)} %maximum_bitcast_fusion.e_ref), custom_call_target="tpu_custom_call" | custom-call | tf_op jit(solution)/shard_map/pallas_call | solution.py:236
  142.0 0.7 gather_fusion.2
  142.7 0.7 gather_fusion.3
  143.4 0.1 broadcast_select_fusion.1
  143.5 2.6 %gather_fusion.1 = bf16[48,128,128]{2,1,0:T(8,128)(2,1)S(1)} fusion(bf16[64,128,128]{2,1,0:T(8,128)(2,1)} %bitcast.32, s32[1024]{0:T(1024)} %pad_clamp_fusion), kind=kCustom, calls=%fused_computation.3 | custom fusion | bytes 3145920 | tf_op jit(solution)/shard_map/jit(_take)/gather | solution.py:332
  146.0 0.1 dynamic-slice_select_fusion
  146.1 0.0 copy-done.15
  146.1 1.2 fusion.12
  (23 shorter events, 0.1 us)
Async XLA Ops:
  0.6 20.2 %copy-start = (s32[160]{0:T(256)S(1)}, s32[160]{0:T(256)}, u32[]{:S(2)}) copy-start(s32[160]{0:T(256)} %param.12) | copy-start | bytes 1924
  2.1 23.3 %collective-permute-start = (bf16[1280,2]{0,1:T(2,128)(2,1)S(1)}, bf16[1280,2]{0,1:T(2,128)(2,1)S(1)}, u32[]{:S(2)}, u32[]{:S(2)}) collective-permute-start(bf16[1280,2]{0,1:T(2,128)(2,1)S(1)} %copy.19), channel_id=1, source_target_pairs={{0,16},{16,32},{32,48},{48,64},{64,80},{80,96},{96,112},{112,128},... | collective-permute-start | bytes 15368 | tf_op jit(solution)/shard_map/ppermute | solution.py:18
  4.0 16.1 %copy-start.11 = (f32[5,2048]{1,0:T(8,128)S(1)}, f32[5,2048]{1,0:T(8,128)}, u32[]{:S(2)}) copy-start(f32[5,2048]{1,0:T(8,128)} %param.9) | copy-start | bytes 122884
  4.0 16.2 %copy-start.12 = (s32[48,2]{0,1:T(2,128)S(1)}, s32[48,2]{0,1:T(2,128)}, u32[]{:S(2)}) copy-start(s32[48,2]{0,1:T(2,128)} %param.10) | copy-start | bytes 1156
  4.0 21.4 %collective-permute-start.1 = (bf16[1280,2]{0,1:T(2,128)(2,1)S(1)}, bf16[1280,2]{0,1:T(2,128)(2,1)S(1)}, u32[]{:S(2)}, u32[]{:S(2)}) collective-permute-start(bf16[1280,2]{0,1:T(2,128)(2,1)S(1)} %copy.20), channel_id=1, source_target_pairs={{16,0},{32,16},{48,32},{64,48},{80,64},{96,80},{112,96},{128,112},... | collective-permute-start | bytes 15368 | tf_op jit(solution)/shard_map/ppermute | solution.py:19
  9.4 52.3 %collective-permute-start.3 = (bf16[384,2048]{1,0:T(8,128)(2,1)}, bf16[384,2048]{1,0:T(8,128)(2,1)S(1)}, u32[]{:S(2)}, u32[]{:S(2)}) collective-permute-start(bf16[384,2048]{1,0:T(8,128)(2,1)} %get-tuple-element.24), channel_id=1, source_target_pairs={{0,1},{1,2},{2,3},{3,4},{4,5},{5,6},{6,7},{7,8},{8,9},{9,10},{10,1... | collective-permute-start | bytes 4718600 | tf_op jit(solution)/shard_map/ppermute | solution.py:286
  13.2 53.7 %collective-permute-start.5 = (bf16[384,2048]{1,0:T(8,128)(2,1)}, bf16[384,2048]{1,0:T(8,128)(2,1)S(1)}, u32[]{:S(2)}, u32[]{:S(2)}) collective-permute-start(bf16[384,2048]{1,0:T(8,128)(2,1)} %get-tuple-element.23), channel_id=1, source_target_pairs={{1,0},{2,1},{3,2},{4,3},{5,4},{6,5},{7,6},{8,7},{9,8},{10,9},{11,1... | collective-permute-start | bytes 4718600 | tf_op jit(solution)/shard_map/ppermute | solution.py:287
  18.8 41.3 %collective-permute-start.6 = (bf16[4,128,128]{2,1,0:T(8,128)(2,1)}, bf16[4,128,128]{2,1,0:T(8,128)(2,1)}, u32[]{:S(2)}, u32[]{:S(2)}) collective-permute-start(bf16[4,128,128]{2,1,0:T(8,128)(2,1)} %param.13), channel_id=1, source_target_pairs={{16,31},{32,46},{48,61},{64,76},{80,91},{96,106},{112,121},{128,13... | collective-permute-start | bytes 393224 | tf_op jit(solution)/shard_map/ppermute | solution.py:298
  20.2 39.1 %copy-start.2 = (f32[1,2048]{1,0:T(1,128)}, f32[1,2048]{1,0:T(1,128)S(1)}, u32[]{:S(2)}) copy-start(f32[1,2048]{1,0:T(1,128)S(1)} %get-tuple-element.28) | copy-start | bytes 24580
  20.2 39.1 %copy-start.4 = (f32[1,2048]{1,0:T(1,128)}, f32[1,2048]{1,0:T(1,128)S(1)}, u32[]{:S(2)}) copy-start(f32[1,2048]{1,0:T(1,128)S(1)} %get-tuple-element.29) | copy-start | bytes 24580
  20.2 39.1 %copy-start.6 = (f32[1,2048]{1,0:T(1,128)}, f32[1,2048]{1,0:T(1,128)S(1)}, u32[]{:S(2)}) copy-start(f32[1,2048]{1,0:T(1,128)S(1)} %get-tuple-element.30) | copy-start | bytes 24580
  20.2 39.1 %copy-start.8 = (f32[1,2048]{1,0:T(1,128)}, f32[1,2048]{1,0:T(1,128)S(1)}, u32[]{:S(2)}) copy-start(f32[1,2048]{1,0:T(1,128)S(1)} %get-tuple-element.31) | copy-start | bytes 24580
  25.4 33.9 %collective-permute-start.2 = (bf16[384,4]{0,1:T(4,128)(2,1)S(1)}, bf16[384,4]{0,1:T(4,128)(2,1)S(1)}, u32[]{:S(2)}, u32[]{:S(2)}) collective-permute-start(bf16[384,4]{0,1:T(4,128)(2,1)S(1)} %get-tuple-element.33), channel_id=1, source_target_pairs={{0,1},{1,2},{2,3},{3,4},{4,5},{5,6},{6,7},{7,8},{8,9},{9,10},{10,1... | collective-permute-start | bytes 9224 | tf_op jit(solution)/shard_map/ppermute | solution.py:304
  27.3 32.3 %collective-permute-start.4 = (bf16[384,4]{0,1:T(4,128)(2,1)S(1)}, bf16[384,4]{0,1:T(4,128)(2,1)S(1)}, u32[]{:S(2)}, u32[]{:S(2)}) collective-permute-start(bf16[384,4]{0,1:T(4,128)(2,1)S(1)} %get-tuple-element.32), channel_id=1, source_target_pairs={{1,0},{2,1},{3,2},{4,3},{5,4},{6,5},{7,6},{8,7},{9,8},{10,9},{11,1... | collective-permute-start | bytes 9224 | tf_op jit(solution)/shard_map/ppermute | solution.py:305
  60.0 6.8 %copy-start.3 = (f32[1,2048]{1,0:T(1,128)S(1)}, f32[1,2048]{1,0:T(1,128)}, u32[]{:S(2)}) copy-start(f32[1,2048]{1,0:T(1,128)} %copy-done.2) | copy-start | bytes 24580
  60.1 6.8 %copy-start.5 = (f32[1,2048]{1,0:T(1,128)S(1)}, f32[1,2048]{1,0:T(1,128)}, u32[]{:S(2)}) copy-start(f32[1,2048]{1,0:T(1,128)} %copy-done.4) | copy-start | bytes 24580
  60.1 6.8 %copy-start.7 = (f32[1,2048]{1,0:T(1,128)S(1)}, f32[1,2048]{1,0:T(1,128)}, u32[]{:S(2)}) copy-start(f32[1,2048]{1,0:T(1,128)} %copy-done.6) | copy-start | bytes 24580
  60.1 6.8 %copy-start.9 = (f32[1,2048]{1,0:T(1,128)S(1)}, f32[1,2048]{1,0:T(1,128)}, u32[]{:S(2)}) copy-start(f32[1,2048]{1,0:T(1,128)} %copy-done.8) | copy-start | bytes 24580
  61.7 9.7 %copy-start.10 = (f32[1280]{0:T(1024)S(1)}, f32[1280]{0:T(1024)}, u32[]{:S(2)}) copy-start(f32[1280]{0:T(1024)} %get-tuple-element.17) | copy-start | bytes 15364
  110.2 33.2 %copy-start.14 = (pred[48]{0:T(512)(128)(4,1)S(1)}, pred[48]{0:T(512)(128)(4,1)}, u32[]{:S(2)}) copy-start(pred[48]{0:T(512)(128)(4,1)} %get-tuple-element.38) | copy-start | bytes 148
  110.2 1.9 %copy-start.1 = (f32[2,4,2,48,8,128]{5,4,3,2,1,0:T(8,128)S(1)}, f32[2,4,2,48,8,128]{5,4,3,2,1,0:T(8,128)}, u32[]{:S(2)}) copy-start(f32[2,4,2,48,8,128]{5,4,3,2,1,0:T(8,128)} %get-tuple-element.7.g_ref) | copy-start | bytes 9437188
  112.1 33.9 %copy-start.13 = (pred[48]{0:T(512)(128)(4,1)S(1)}, pred[48]{0:T(512)(128)(4,1)}, u32[]{:S(2)}) copy-start(pred[48]{0:T(512)(128)(4,1)} %get-tuple-element.11) | copy-start | bytes 148
  112.1 34.0 %copy-start.15 = (pred[48]{0:T(512)(128)(4,1)S(1)}, pred[48]{0:T(512)(128)(4,1)}, u32[]{:S(2)}) copy-start(pred[48]{0:T(512)(128)(4,1)} %get-tuple-element.21) | copy-start | bytes 148
  112.1 34.0 %copy-start.16 = (pred[48]{0:T(512)(128)(4,1)S(1)}, pred[48]{0:T(512)(128)(4,1)}, u32[]{:S(2)}) copy-start(pred[48]{0:T(512)(128)(4,1)} %iota_compare_fusion) | copy-start | bytes 148

commit v13 on v12

--- a/solution.py
+++ b/solution.py
@@ -69,17 +69,19 @@
     for cp in copies:
         cp.wait()
 
-    def body(s, carry):
-        left_rows = ext_ref[rel_ref[2 * s]]
-        right_rows = ext_ref[rel_ref[2 * s + 1]]
+    def body(t, carry):
+        left_rows = jnp.concatenate([ext_ref[rel_ref[4 * t]], ext_ref[rel_ref[4 * t + 2]]], axis=0)
+        right_rows = jnp.concatenate([ext_ref[rel_ref[4 * t + 1]], ext_ref[rel_ref[4 * t + 3]]], axis=0)
         g = lax.dot_general(
             left_rows, right_rows, (((1,), (1,)), ((), ())), preferred_element_type=jnp.float32
         )
-        for q in range(shares):
-            out_ref[q % 2, (q // 2) % 4, q // 8, s] = g[q * rows : (q + 1) * rows, :]
+        for half in range(2):
+            part = g[half * block : (half + 1) * block, half * block : (half + 1) * block]
+            for q in range(shares):
+                out_ref[q % 2, (q // 2) % 4, q // 8, 2 * t + half] = part[q * rows : (q + 1) * rows, :]
         return carry
 
-    third = slots // 4
+    third = slots // 8
     lax.fori_loop(0, third, body, 0)
     ca.wait_recv()
     b1 = [
@@ -103,7 +105,7 @@
     cc = remote(table.at[pl.ds(c * 8, 8)], table.at[pl.ds(c * 8, 8)], 6, partner)
     cc.start()
     sent.append(cc)
-    lax.fori_loop(3 * third, slots, body, 0)
+    lax.fori_loop(3 * third, slots // 2, body, 0)
     cc.wait_recv()
     for cp in sent:
         cp.wait_send()

time: 148 us -> 146 us (0.986)
  Pallas kernels: 68.6 us -> 67 us
    pallas_call x1, Pallas kernels: 38.8 us -> 37.2 us  [pair_grams(): pl.pallas_call(lambda *refs: gram_kernel(shares, *refs), out_shape=(jax.S...]
  transfers between devices with their start and end apart: 7 -> 7, of which waited for: 0 -> 0; matrix products, arithmetic and copies ran while one was open for 27% -> 28% of each run, Pallas kernels for 0% -> 0%
where the time goes in v13:
time: 146 us
  Pallas kernels  67 us (46%)
  other arithmetic  37.6 us (26%)
  starting transfers between devices  23.4 us (16%)
  local copies, waits for them, and re-layouts  14.9 us (10%)
  between operations  1.61 us (1%)
    pallas_call x1, Pallas kernels, pair_grams(): pl.pallas_call(lambda *refs: gram_kernel(shares, *refs), out_shape=(jax.S...  37.2 us
    reduce_sum x3, other arithmetic, row_squares(): return jnp.sum(values * values, axis=1)  32.9 us
    pallas_call x1, Pallas kernels, scatter_grams(): pl.pallas_call(scatter_kernel, out_shape=(jax.ShapeDtypeStruct(part, f32)...  29.8 us
    ppermute x1, starting transfers between devices, on_device(): edge_after = lax.ppermute(edges[:width], 'ion', down)  7.54 us
    ppermute x1, starting transfers between devices, on_device(): raw_after = lax.ppermute(images[:width], 'ion', down)  5.63 us
    slice x1, local copies, waits for them, and re-layouts, on_device(): raw_after = lax.ppermute(images[:width], 'ion', down)  3.93 us
    ppermute x1, starting transfers between devices, on_device(): raw_before = lax.ppermute(images[local_rows - width:], 'ion', up)  3.81 us
  transfers between devices with their start and end apart: 7, of which 0 were waited for; matrix products, arithmetic and copies ran while one was open for 28% of the time, Pallas kernels for 0%

profile of v13, /device:TPU:16, one launch (start us, length us, event | category | flops | bytes accessed | tf_op | source)
XLA Modules:
  0.0 145.8 jit_solution(5052145297512579570)
XLA Ops:
  0.6 0.0 copy-start
  0.6 1.2 fusion.30
  1.9 0.2 copy.19
  2.1 1.7 %collective-permute-start = (bf16[1280,2]{0,1:T(2,128)(2,1)S(1)}, bf16[1280,2]{0,1:T(2,128)(2,1)S(1)}, u32[]{:S(2)}, u32[]{:S(2)}) collective-permute-start(bf16[1280,2]{0,1:T(2,128)(2,1)S(1)} %copy.19), channel_id=1, source_target_pairs={{0,16},{16,32},{32,48},{48,64},{64,80},{80,96},{96,112},{112,128},... | collective-permute-start | bytes 15368 | tf_op jit(solution)/shard_map/ppermute | solution.py:18
  3.8 0.2 copy.20
  4.0 1.4 collective-permute-start.1
  5.4 3.9 %fusion.29 = (bf16[384,2048]{1,0:T(8,128)(2,1)}, bf16[384,2048]{1,0:T(8,128)(2,1)}) fusion(bf16[1280,2048]{1,0:T(8,128)(2,1)} %param.8), kind=kLoop, calls=%fused_computation.94 | loop fusion | bytes 6291456 | tf_op jit(solution)/shard_map/slice | solution.py:289
  9.4 3.8 %collective-permute-start.3 = (bf16[384,2048]{1,0:T(8,128)(2,1)}, bf16[384,2048]{1,0:T(8,128)(2,1)S(1)}, u32[]{:S(2)}, u32[]{:S(2)}) collective-permute-start(bf16[384,2048]{1,0:T(8,128)(2,1)} %get-tuple-element.24), channel_id=1, source_target_pairs={{0,1},{1,2},{2,3},{3,4},{4,5},{5,6},{6,7},{7,8},{8,9},{9,10},{10,1... | collective-permute-start | bytes 4718600 | tf_op jit(solution)/shard_map/ppermute | solution.py:288
  13.2 5.6 %collective-permute-start.5 = (bf16[384,2048]{1,0:T(8,128)(2,1)}, bf16[384,2048]{1,0:T(8,128)(2,1)S(1)}, u32[]{:S(2)}, u32[]{:S(2)}) collective-permute-start(bf16[384,2048]{1,0:T(8,128)(2,1)} %get-tuple-element.23), channel_id=1, source_target_pairs={{1,0},{2,1},{3,2},{4,3},{5,4},{6,5},{7,6},{8,7},{9,8},{10,9},{11,1... | collective-permute-start | bytes 4718600 | tf_op jit(solution)/shard_map/ppermute | solution.py:289
  18.8 1.3 collective-permute-start.6
  20.1 0.0 copy-done.11
  20.2 0.0 copy-start.2
  20.2 0.0 copy-start.4
  20.2 0.0 copy-start.6
  20.2 0.0 copy-start.8
  20.2 0.0 copy-done.12
  20.2 0.6 compare_and_fusion.1
  20.8 0.0 copy-done
  20.8 0.8 gather_fusion
  21.6 0.6 and_bitcast_fusion
  22.2 0.6 pad_clamp_fusion
  23.4 0.6 pad_clamp_fusion.2
  24.0 0.6 iota_compare_fusion
  24.6 0.1 copy.14
  24.7 0.7 reshape.45.refs_0_
  25.4 0.0 collective-permute-done
  25.4 0.0 collective-permute-done.1
  25.4 1.9 %collective-permute-start.2 = (bf16[384,4]{0,1:T(4,128)(2,1)S(1)}, bf16[384,4]{0,1:T(4,128)(2,1)S(1)}, u32[]{:S(2)}, u32[]{:S(2)}) collective-permute-start(bf16[384,4]{0,1:T(4,128)(2,1)S(1)} %get-tuple-element.33), channel_id=1, source_target_pairs={{0,1},{1,2},{2,3},{3,4},{4,5},{5,6},{6,7},{7,8},{8,9},{9,10},{10,1... | collective-permute-start | bytes 9224 | tf_op jit(solution)/shard_map/ppermute | solution.py:306
  27.3 7.5 %collective-permute-start.4 = (bf16[384,4]{0,1:T(4,128)(2,1)S(1)}, bf16[384,4]{0,1:T(4,128)(2,1)S(1)}, u32[]{:S(2)}, u32[]{:S(2)}) collective-permute-start(bf16[384,4]{0,1:T(4,128)(2,1)S(1)} %get-tuple-element.32), channel_id=1, source_target_pairs={{1,0},{2,1},{3,2},{4,3},{5,4},{6,5},{7,6},{8,7},{9,8},{10,9},{11,1... | collective-permute-start | bytes 9224 | tf_op jit(solution)/shard_map/ppermute | solution.py:307
  34.9 0.2 copy.11
  35.1 0.9 copy.13
  36.0 23.2 %multiply_reduce_fusion = (f32[1280]{0:T(1024)}, bf16[1280,2048]{1,0:T(8,128)(2,1)}) fusion(bf16[1280,2]{1,0:T(8,128)(2,1)} %copy.13, bf16[1280,2048]{1,0:T(8,128)(2,1)} %param.8, f32[2048]{0:T(1024)S(1)} %bitcast.42, f32[2048]{0:T(1024)S(1)} %bitcast.45, f32[2048]{0:T(1024)S(1)} %bitcast.36, bf16[1280,2]{1,0:T(8,128)(2,1)S(1)} %copy.11, ...), kind=kLoop, calls=%fused_computation.4 | loop fusion | flops 78641920 | bytes 10542080 | tf_op jit(solution)/shard_map/reduce_sum | solution.py:275
  59.2 0.0 copy-done.2
  59.2 0.0 copy-done.4
  59.3 0.0 copy-done.6
  59.3 0.0 copy-done.8
  59.3 0.0 collective-permute-done.2
  59.3 0.2 copy.15
  59.5 0.2 copy.16
  59.7 0.0 collective-permute-done.4
  59.7 0.2 copy.17
  59.9 0.2 copy.18
  60.1 0.0 copy-start.5
  60.1 0.0 copy-start.7
  60.1 0.0 collective-permute-done.6
  60.1 1.6 %broadcast_select_fusion.refs_4_ = bf16[4,128,128]{2,1,0:T(8,128)(2,1)} fusion(bf16[4,128,128]{2,1,0:T(8,128)(2,1)} %param.13, bf16[4,128,128]{2,1,0:T(8,128)(2,1)} %collective-permute-done.6, pred[]{:T(512)S(6)} %eq.8), kind=kLoop, calls=%fused_computation.41 | loop fusion | flops 65536 | bytes 393217 | tf_op jit(solution)/shard_map/jit(_where)/select_n | solution.py:301
  61.7 0.0 collective-permute-done.3
  61.7 5.2 %multiply_reduce_fusion.2 = (f32[384]{0:T(512)S(1)}, bf16[384,2048]{1,0:T(8,128)(2,1)}) fusion(bf16[384,2]{1,0:T(8,128)(2,1)S(1)} %copy.16, bf16[384,2048]{1,0:T(8,128)(2,1)S(1)} %collective-permute-done.3, f32[2048]{0:T(1024)} %bitcast.43, f32[2048]{0:T(1024)} %bitcast.46, f32[2048]{0:T(1024)} %bitcast.37, bf16[384,2]{1,0:T(8,128)(2,1)S(1)} %copy.15, ...), kind=kLoop, calls=%fused_computation.15 | loop fusion | flops 23592576 | bytes 3191296 | tf_op jit(solution)/shard_map/reduce_sum | solution.py:275
  66.9 0.0 collective-permute-done.5
  66.9 0.0 copy-done.5
  66.9 0.0 copy-done.7
  66.9 0.0 copy-done.9
  66.9 4.5 %multiply_reduce_fusion.1 = (f32[384]{0:T(512)S(1)}, bf16[384,2048]{1,0:T(8,128)(2,1)}) fusion(bf16[384,2]{1,0:T(8,128)(2,1)S(1)} %copy.18, bf16[384,2048]{1,0:T(8,128)(2,1)S(1)} %collective-permute-done.5, f32[2048]{0:T(1024)S(1)} %bitcast.44, f32[2048]{0:T(1024)S(1)} %bitcast.47, f32[2048]{0:T(1024)S(1)} %bitcast.38, bf16[384,2]{1,0:T(8,128)(2,1)S(1)} %copy.17, ...), kind=kLoop, calls=%fused_computation.14 | loop fusion | flops 23592576 | bytes 3191296 | tf_op jit(solution)/shard_map/reduce_sum | solution.py:275
  71.4 37.2 %shard_map.77 = (f32[2,4,2,48,8,128]{5,4,3,2,1,0:T(8,128)}, bf16[16,4,128,128]{3,2,1,0:T(8,128)(2,1)}) custom-call(s32[96]{0:T(128)} %reshape.45.refs_0_, bf16[3,128,2048]{2,1,0:T(8,128)(2,1)} %bitcast.30, bf16[10,128,2048]{2,1,0:T(8,128)(2,1)} %bitcast.29, bf16[3,128,2048]{2,1,0:T(8,128)(2,1)} %bitcast.31, bf16[4,128,128]{2,1,0:T(8,128)(2,1)} %broadcast_select_fusion.refs_4_), custom_call_target="tpu_custom_call" | custom-call | flops 3221225472 | bytes 11534336 | tf_op jit(solution)/shard_map/pallas_call | solution.py:124
  108.6 1.9 %copy-done.1 = f32[2,4,2,48,8,128]{5,4,3,2,1,0:T(8,128)S(1)} copy-done((f32[2,4,2,48,8,128]{5,4,3,2,1,0:T(8,128)S(1)}, f32[2,4,2,48,8,128]{5,4,3,2,1,0:T(8,128)}, u32[]{:S(2)}) %copy-start.1) | copy-done | bytes 3145752
  110.5 29.8 %shard_map.78 = (f32[48,8,128]{2,1,0:T(8,128)S(1)}, f32[16,128]{1,0:T(8,128)S(1)}) custom-call(f32[2,4,2,48,8,128]{5,4,3,2,1,0:T(8,128)S(1)} %copy-done.1, f32[16,128]{1,0:T(8,128)S(1)} %maximum_bitcast_fusion.e_ref), custom_call_target="tpu_custom_call" | custom-call | tf_op jit(solution)/shard_map/pallas_call | solution.py:238
  140.3 0.7 gather_fusion.2
  141.1 0.7 gather_fusion.3
  141.8 0.0 copy-done.14
  141.8 0.1 broadcast_select_fusion.1
  141.8 2.6 %gather_fusion.1 = bf16[48,128,128]{2,1,0:T(8,128)(2,1)S(1)} fusion(bf16[64,128,128]{2,1,0:T(8,128)(2,1)} %bitcast.32, s32[1024]{0:T(1024)} %pad_clamp_fusion), kind=kCustom, calls=%fused_computation.3 | custom fusion | bytes 3145920 | tf_op jit(solution)/shard_map/jit(_take)/gather | solution.py:334
  144.4 0.1 dynamic-slice_select_fusion
  144.5 0.0 copy-done.16
  144.5 1.2 fusion.12
  (23 shorter events, 0.1 us)
Async XLA Ops:
  0.6 20.2 %copy-start = (s32[160]{0:T(256)S(1)}, s32[160]{0:T(256)}, u32[]{:S(2)}) copy-start(s32[160]{0:T(256)} %param.12) | copy-start | bytes 1924
  2.1 23.3 %collective-permute-start = (bf16[1280,2]{0,1:T(2,128)(2,1)S(1)}, bf16[1280,2]{0,1:T(2,128)(2,1)S(1)}, u32[]{:S(2)}, u32[]{:S(2)}) collective-permute-start(bf16[1280,2]{0,1:T(2,128)(2,1)S(1)} %copy.19), channel_id=1, source_target_pairs={{0,16},{16,32},{32,48},{48,64},{64,80},{80,96},{96,112},{112,128},... | collective-permute-start | bytes 15368 | tf_op jit(solution)/shard_map/ppermute | solution.py:18
  4.0 16.1 %copy-start.11 = (f32[5,2048]{1,0:T(8,128)S(1)}, f32[5,2048]{1,0:T(8,128)}, u32[]{:S(2)}) copy-start(f32[5,2048]{1,0:T(8,128)} %param.9) | copy-start | bytes 122884
  4.0 16.2 %copy-start.12 = (s32[48,2]{0,1:T(2,128)S(1)}, s32[48,2]{0,1:T(2,128)}, u32[]{:S(2)}) copy-start(s32[48,2]{0,1:T(2,128)} %param.10) | copy-start | bytes 1156
  4.0 21.4 %collective-permute-start.1 = (bf16[1280,2]{0,1:T(2,128)(2,1)S(1)}, bf16[1280,2]{0,1:T(2,128)(2,1)S(1)}, u32[]{:S(2)}, u32[]{:S(2)}) collective-permute-start(bf16[1280,2]{0,1:T(2,128)(2,1)S(1)} %copy.20), channel_id=1, source_target_pairs={{16,0},{32,16},{48,32},{64,48},{80,64},{96,80},{112,96},{128,112},... | collective-permute-start | bytes 15368 | tf_op jit(solution)/shard_map/ppermute | solution.py:19
  9.4 52.3 %collective-permute-start.3 = (bf16[384,2048]{1,0:T(8,128)(2,1)}, bf16[384,2048]{1,0:T(8,128)(2,1)S(1)}, u32[]{:S(2)}, u32[]{:S(2)}) collective-permute-start(bf16[384,2048]{1,0:T(8,128)(2,1)} %get-tuple-element.24), channel_id=1, source_target_pairs={{0,1},{1,2},{2,3},{3,4},{4,5},{5,6},{6,7},{7,8},{8,9},{9,10},{10,1... | collective-permute-start | bytes 4718600 | tf_op jit(solution)/shard_map/ppermute | solution.py:288
  13.2 53.7 %collective-permute-start.5 = (bf16[384,2048]{1,0:T(8,128)(2,1)}, bf16[384,2048]{1,0:T(8,128)(2,1)S(1)}, u32[]{:S(2)}, u32[]{:S(2)}) collective-permute-start(bf16[384,2048]{1,0:T(8,128)(2,1)} %get-tuple-element.23), channel_id=1, source_target_pairs={{1,0},{2,1},{3,2},{4,3},{5,4},{6,5},{7,6},{8,7},{9,8},{10,9},{11,1... | collective-permute-start | bytes 4718600 | tf_op jit(solution)/shard_map/ppermute | solution.py:289
  18.8 41.3 %collective-permute-start.6 = (bf16[4,128,128]{2,1,0:T(8,128)(2,1)}, bf16[4,128,128]{2,1,0:T(8,128)(2,1)}, u32[]{:S(2)}, u32[]{:S(2)}) collective-permute-start(bf16[4,128,128]{2,1,0:T(8,128)(2,1)} %param.13), channel_id=1, source_target_pairs={{16,31},{32,46},{48,61},{64,76},{80,91},{96,106},{112,121},{128,13... | collective-permute-start | bytes 393224 | tf_op jit(solution)/shard_map/ppermute | solution.py:300
  20.2 39.1 %copy-start.2 = (f32[1,2048]{1,0:T(1,128)}, f32[1,2048]{1,0:T(1,128)S(1)}, u32[]{:S(2)}) copy-start(f32[1,2048]{1,0:T(1,128)S(1)} %get-tuple-element.28) | copy-start | bytes 24580
  20.2 39.1 %copy-start.4 = (f32[1,2048]{1,0:T(1,128)}, f32[1,2048]{1,0:T(1,128)S(1)}, u32[]{:S(2)}) copy-start(f32[1,2048]{1,0:T(1,128)S(1)} %get-tuple-element.29) | copy-start | bytes 24580
  20.2 39.1 %copy-start.6 = (f32[1,2048]{1,0:T(1,128)}, f32[1,2048]{1,0:T(1,128)S(1)}, u32[]{:S(2)}) copy-start(f32[1,2048]{1,0:T(1,128)S(1)} %get-tuple-element.30) | copy-start | bytes 24580
  20.2 39.1 %copy-start.8 = (f32[1,2048]{1,0:T(1,128)}, f32[1,2048]{1,0:T(1,128)S(1)}, u32[]{:S(2)}) copy-start(f32[1,2048]{1,0:T(1,128)S(1)} %get-tuple-element.31) | copy-start | bytes 24580
  25.4 33.9 %collective-permute-start.2 = (bf16[384,4]{0,1:T(4,128)(2,1)S(1)}, bf16[384,4]{0,1:T(4,128)(2,1)S(1)}, u32[]{:S(2)}, u32[]{:S(2)}) collective-permute-start(bf16[384,4]{0,1:T(4,128)(2,1)S(1)} %get-tuple-element.33), channel_id=1, source_target_pairs={{0,1},{1,2},{2,3},{3,4},{4,5},{5,6},{6,7},{7,8},{8,9},{9,10},{10,1... | collective-permute-start | bytes 9224 | tf_op jit(solution)/shard_map/ppermute | solution.py:306
  27.3 32.3 %collective-permute-start.4 = (bf16[384,4]{0,1:T(4,128)(2,1)S(1)}, bf16[384,4]{0,1:T(4,128)(2,1)S(1)}, u32[]{:S(2)}, u32[]{:S(2)}) collective-permute-start(bf16[384,4]{0,1:T(4,128)(2,1)S(1)} %get-tuple-element.32), channel_id=1, source_target_pairs={{1,0},{2,1},{3,2},{4,3},{5,4},{6,5},{7,6},{8,7},{9,8},{10,9},{11,1... | collective-permute-start | bytes 9224 | tf_op jit(solution)/shard_map/ppermute | solution.py:307
  60.0 6.8 %copy-start.3 = (f32[1,2048]{1,0:T(1,128)S(1)}, f32[1,2048]{1,0:T(1,128)}, u32[]{:S(2)}) copy-start(f32[1,2048]{1,0:T(1,128)} %copy-done.2) | copy-start | bytes 24580
  60.1 6.8 %copy-start.5 = (f32[1,2048]{1,0:T(1,128)S(1)}, f32[1,2048]{1,0:T(1,128)}, u32[]{:S(2)}) copy-start(f32[1,2048]{1,0:T(1,128)} %copy-done.4) | copy-start | bytes 24580
  60.1 6.8 %copy-start.7 = (f32[1,2048]{1,0:T(1,128)S(1)}, f32[1,2048]{1,0:T(1,128)}, u32[]{:S(2)}) copy-start(f32[1,2048]{1,0:T(1,128)} %copy-done.6) | copy-start | bytes 24580
  60.1 6.8 %copy-start.9 = (f32[1,2048]{1,0:T(1,128)S(1)}, f32[1,2048]{1,0:T(1,128)}, u32[]{:S(2)}) copy-start(f32[1,2048]{1,0:T(1,128)} %copy-done.8) | copy-start | bytes 24580
  61.7 9.7 %copy-start.10 = (f32[1280]{0:T(1024)S(1)}, f32[1280]{0:T(1024)}, u32[]{:S(2)}) copy-start(f32[1280]{0:T(1024)} %get-tuple-element.17) | copy-start | bytes 15364
  108.6 33.2 %copy-start.14 = (pred[48]{0:T(512)(128)(4,1)S(1)}, pred[48]{0:T(512)(128)(4,1)}, u32[]{:S(2)}) copy-start(pred[48]{0:T(512)(128)(4,1)} %get-tuple-element.38) | copy-start | bytes 148
  108.6 1.9 %copy-start.1 = (f32[2,4,2,48,8,128]{5,4,3,2,1,0:T(8,128)S(1)}, f32[2,4,2,48,8,128]{5,4,3,2,1,0:T(8,128)}, u32[]{:S(2)}) copy-start(f32[2,4,2,48,8,128]{5,4,3,2,1,0:T(8,128)} %get-tuple-element.7.g_ref) | copy-start | bytes 9437188
  110.5 33.9 %copy-start.13 = (pred[48]{0:T(512)(128)(4,1)S(1)}, pred[48]{0:T(512)(128)(4,1)}, u32[]{:S(2)}) copy-start(pred[48]{0:T(512)(128)(4,1)} %get-tuple-element.11) | copy-start | bytes 148
  110.5 34.0 %copy-start.15 = (pred[48]{0:T(512)(128)(4,1)S(1)}, pred[48]{0:T(512)(128)(4,1)}, u32[]{:S(2)}) copy-start(pred[48]{0:T(512)(128)(4,1)} %get-tuple-element.21) | copy-start | bytes 148
  110.5 34.0 %copy-start.16 = (pred[48]{0:T(512)(128)(4,1)S(1)}, pred[48]{0:T(512)(128)(4,1)}, u32[]{:S(2)}) copy-start(pred[48]{0:T(512)(128)(4,1)} %iota_compare_fusion) | copy-start | bytes 148

commit v14 on v13

--- a/solution.py
+++ b/solution.py
@@ -172,14 +172,22 @@
             device_id={"pix": peer}, device_id_type=MESH,
         )
 
-    c1 = remote(g_ref.at[1 - c], r1, 0, partner)
-    c1.start()
+    order = [(x + 3) % 4, (x + 1) % 4, (x + 2) % 4, x]
+    stage1 = []
+    for n, j in enumerate(order):
+        cp = remote(g_ref.at[1 - c, j], r1.at[j], 12 + n if n else 0, partner)
+        cp.start()
+        stage1.append(cp)
     ce1 = remote(e_ref, ebuf.at[0], 1, partner)
     ce1.start()
-    c1.wait()
+
+    def settle(n):
+        stage1[n].wait()
+        s1[order[n]] = g_ref[c, order[n]] + r1[order[n]]
+
+    settle(0)
+    settle(1)
     ce1.wait()
-    for j in range(4):
-        s1[j] = g_ref[c, j] + r1[j]
     ebuf[1] = e_ref[...] + ebuf[0]
 
     done = []
@@ -190,6 +198,8 @@
         if k == 0:
             src_r, src_l = s1.at[jr, 0], s1.at[jl, 1]
         else:
+            if k == 1:
+                settle(2)
             cr.wait_recv()
             cl.wait_recv()
             acc_r[k] = s1[jr, 0] + recv_r[k - 1]
@@ -211,6 +221,7 @@
             ef = remote(ebuf.at[2], ebuf.at[4], 10, right)
             ef.start()
             done.append(ef)
+    settle(3)
     cr.wait_recv()
     cl.wait_recv()
     tbuf[0] = s1[x, 0] + recv_r[2]
@@ -253,8 +264,8 @@
             pltpu.VMEM((2,) + part, f32),
             pltpu.VMEM(part, f32),
             pltpu.VMEM((7,) + energy_part.shape, f32),
-            pltpu.SemaphoreType.DMA((13,)),
-            pltpu.SemaphoreType.DMA((13,)),
+            pltpu.SemaphoreType.DMA((16,)),
+            pltpu.SemaphoreType.DMA((16,)),
         ],
         compiler_params=pltpu.CompilerParams(
             collective_id=0, has_side_effects=True, vmem_limit_bytes=48 * 1024 * 1024

time: 146 us -> 146 us (level)
  no operation moved by 1% of the time
where the time goes in v14:
time: 146 us
  Pallas kernels  66.8 us (46%)
  other arithmetic  37.6 us (26%)
  starting transfers between devices  23.4 us (16%)
  local copies, waits for them, and re-layouts  14.9 us (10%)
  between operations  1.61 us (1%)
    pallas_call x1, Pallas kernels, pair_grams(): pl.pallas_call(lambda *refs: gram_kernel(shares, *refs), out_shape=(jax.S...  37.2 us
    reduce_sum x3, other arithmetic, row_squares(): return jnp.sum(values * values, axis=1)  32.9 us
    pallas_call x1, Pallas kernels, scatter_grams(): pl.pallas_call(scatter_kernel, out_shape=(jax.ShapeDtypeStruct(part, f32)...  29.6 us
    ppermute x1, starting transfers between devices, on_device(): edge_after = lax.ppermute(edges[:width], 'ion', down)  7.54 us
    ppermute x1, starting transfers between devices, on_device(): raw_after = lax.ppermute(images[:width], 'ion', down)  5.63 us
    slice x1, local copies, waits for them, and re-layouts, on_device(): raw_after = lax.ppermute(images[:width], 'ion', down)  3.93 us
    ppermute x1, starting transfers between devices, on_device(): raw_before = lax.ppermute(images[local_rows - width:], 'ion', up)  3.81 us
  transfers between devices with their start and end apart: 7, of which 0 were waited for; matrix products, arithmetic and copies ran while one was open for 28% of the time, Pallas kernels for 0%

profile of v14, /device:TPU:16, one launch (start us, length us, event | category | flops | bytes accessed | tf_op | source)
XLA Modules:
  0.0 145.5 jit_solution(6040070838756468602)
XLA Ops:
  0.6 0.0 copy-start
  0.6 1.2 fusion.30
  1.9 0.2 copy.19
  2.1 1.7 %collective-permute-start = (bf16[1280,2]{0,1:T(2,128)(2,1)S(1)}, bf16[1280,2]{0,1:T(2,128)(2,1)S(1)}, u32[]{:S(2)}, u32[]{:S(2)}) collective-permute-start(bf16[1280,2]{0,1:T(2,128)(2,1)S(1)} %copy.19), channel_id=1, source_target_pairs={{0,16},{16,32},{32,48},{48,64},{64,80},{80,96},{96,112},{112,128},... | collective-permute-start | bytes 15368 | tf_op jit(solution)/shard_map/ppermute | solution.py:18
  3.8 0.2 copy.20
  4.0 1.4 collective-permute-start.1
  5.4 3.9 %fusion.29 = (bf16[384,2048]{1,0:T(8,128)(2,1)}, bf16[384,2048]{1,0:T(8,128)(2,1)}) fusion(bf16[1280,2048]{1,0:T(8,128)(2,1)} %param.8), kind=kLoop, calls=%fused_computation.94 | loop fusion | bytes 6291456 | tf_op jit(solution)/shard_map/slice | solution.py:300
  9.4 3.8 %collective-permute-start.3 = (bf16[384,2048]{1,0:T(8,128)(2,1)}, bf16[384,2048]{1,0:T(8,128)(2,1)S(1)}, u32[]{:S(2)}, u32[]{:S(2)}) collective-permute-start(bf16[384,2048]{1,0:T(8,128)(2,1)} %get-tuple-element.24), channel_id=1, source_target_pairs={{0,1},{1,2},{2,3},{3,4},{4,5},{5,6},{6,7},{7,8},{8,9},{9,10},{10,1... | collective-permute-start | bytes 4718600 | tf_op jit(solution)/shard_map/ppermute | solution.py:299
  13.2 5.6 %collective-permute-start.5 = (bf16[384,2048]{1,0:T(8,128)(2,1)}, bf16[384,2048]{1,0:T(8,128)(2,1)S(1)}, u32[]{:S(2)}, u32[]{:S(2)}) collective-permute-start(bf16[384,2048]{1,0:T(8,128)(2,1)} %get-tuple-element.23), channel_id=1, source_target_pairs={{1,0},{2,1},{3,2},{4,3},{5,4},{6,5},{7,6},{8,7},{9,8},{10,9},{11,1... | collective-permute-start | bytes 4718600 | tf_op jit(solution)/shard_map/ppermute | solution.py:300
  18.8 1.3 collective-permute-start.6
  20.1 0.0 copy-done.11
  20.2 0.0 copy-start.2
  20.2 0.0 copy-start.4
  20.2 0.0 copy-start.6
  20.2 0.0 copy-start.8
  20.2 0.0 copy-done.12
  20.2 0.6 compare_and_fusion.1
  20.8 0.0 copy-done
  20.8 0.8 gather_fusion
  21.6 0.6 and_bitcast_fusion
  22.2 0.6 pad_clamp_fusion
  23.4 0.6 pad_clamp_fusion.2
  24.0 0.6 iota_compare_fusion
  24.6 0.1 copy.14
  24.7 0.7 reshape.45.refs_0_
  25.4 0.0 collective-permute-done
  25.4 0.0 collective-permute-done.1
  25.4 1.9 %collective-permute-start.2 = (bf16[384,4]{0,1:T(4,128)(2,1)S(1)}, bf16[384,4]{0,1:T(4,128)(2,1)S(1)}, u32[]{:S(2)}, u32[]{:S(2)}) collective-permute-start(bf16[384,4]{0,1:T(4,128)(2,1)S(1)} %get-tuple-element.33), channel_id=1, source_target_pairs={{0,1},{1,2},{2,3},{3,4},{4,5},{5,6},{6,7},{7,8},{8,9},{9,10},{10,1... | collective-permute-start | bytes 9224 | tf_op jit(solution)/shard_map/ppermute | solution.py:317
  27.3 7.5 %collective-permute-start.4 = (bf16[384,4]{0,1:T(4,128)(2,1)S(1)}, bf16[384,4]{0,1:T(4,128)(2,1)S(1)}, u32[]{:S(2)}, u32[]{:S(2)}) collective-permute-start(bf16[384,4]{0,1:T(4,128)(2,1)S(1)} %get-tuple-element.32), channel_id=1, source_target_pairs={{1,0},{2,1},{3,2},{4,3},{5,4},{6,5},{7,6},{8,7},{9,8},{10,9},{11,1... | collective-permute-start | bytes 9224 | tf_op jit(solution)/shard_map/ppermute | solution.py:318
  34.9 0.2 copy.11
  35.1 0.9 copy.13
  36.0 23.2 %multiply_reduce_fusion = (f32[1280]{0:T(1024)}, bf16[1280,2048]{1,0:T(8,128)(2,1)}) fusion(bf16[1280,2]{1,0:T(8,128)(2,1)} %copy.13, bf16[1280,2048]{1,0:T(8,128)(2,1)} %param.8, f32[2048]{0:T(1024)S(1)} %bitcast.42, f32[2048]{0:T(1024)S(1)} %bitcast.45, f32[2048]{0:T(1024)S(1)} %bitcast.36, bf16[1280,2]{1,0:T(8,128)(2,1)S(1)} %copy.11, ...), kind=kLoop, calls=%fused_computation.4 | loop fusion | flops 78641920 | bytes 10542080 | tf_op jit(solution)/shard_map/reduce_sum | solution.py:286
  59.2 0.0 copy-done.2
  59.2 0.0 copy-done.4
  59.3 0.0 copy-done.6
  59.3 0.0 copy-done.8
  59.3 0.0 collective-permute-done.2
  59.3 0.2 copy.15
  59.5 0.2 copy.16
  59.7 0.0 collective-permute-done.4
  59.7 0.2 copy.17
  59.9 0.2 copy.18
  60.1 0.0 copy-start.5
  60.1 0.0 copy-start.7
  60.1 0.0 collective-permute-done.6
  60.1 1.6 %broadcast_select_fusion.refs_4_ = bf16[4,128,128]{2,1,0:T(8,128)(2,1)} fusion(bf16[4,128,128]{2,1,0:T(8,128)(2,1)} %param.13, bf16[4,128,128]{2,1,0:T(8,128)(2,1)} %collective-permute-done.6, pred[]{:T(512)S(6)} %eq.8), kind=kLoop, calls=%fused_computation.41 | loop fusion | flops 65536 | bytes 393217 | tf_op jit(solution)/shard_map/jit(_where)/select_n | solution.py:312
  61.7 0.0 collective-permute-done.3
  61.7 5.2 %multiply_reduce_fusion.2 = (f32[384]{0:T(512)S(1)}, bf16[384,2048]{1,0:T(8,128)(2,1)}) fusion(bf16[384,2]{1,0:T(8,128)(2,1)S(1)} %copy.16, bf16[384,2048]{1,0:T(8,128)(2,1)S(1)} %collective-permute-done.3, f32[2048]{0:T(1024)} %bitcast.43, f32[2048]{0:T(1024)} %bitcast.46, f32[2048]{0:T(1024)} %bitcast.37, bf16[384,2]{1,0:T(8,128)(2,1)S(1)} %copy.15, ...), kind=kLoop, calls=%fused_computation.15 | loop fusion | flops 23592576 | bytes 3191296 | tf_op jit(solution)/shard_map/reduce_sum | solution.py:286
  66.9 0.0 collective-permute-done.5
  66.9 0.0 copy-done.3
  66.9 0.0 copy-done.5
  66.9 0.0 copy-done.7
  66.9 0.0 copy-done.9
  66.9 4.5 %multiply_reduce_fusion.1 = (f32[384]{0:T(512)S(1)}, bf16[384,2048]{1,0:T(8,128)(2,1)}) fusion(bf16[384,2]{1,0:T(8,128)(2,1)S(1)} %copy.18, bf16[384,2048]{1,0:T(8,128)(2,1)S(1)} %collective-permute-done.5, f32[2048]{0:T(1024)S(1)} %bitcast.44, f32[2048]{0:T(1024)S(1)} %bitcast.47, f32[2048]{0:T(1024)S(1)} %bitcast.38, bf16[384,2]{1,0:T(8,128)(2,1)S(1)} %copy.17, ...), kind=kLoop, calls=%fused_computation.14 | loop fusion | flops 23592576 | bytes 3191296 | tf_op jit(solution)/shard_map/reduce_sum | solution.py:286
  71.4 37.2 %shard_map.77 = (f32[2,4,2,48,8,128]{5,4,3,2,1,0:T(8,128)}, bf16[16,4,128,128]{3,2,1,0:T(8,128)(2,1)}) custom-call(s32[96]{0:T(128)} %reshape.45.refs_0_, bf16[3,128,2048]{2,1,0:T(8,128)(2,1)} %bitcast.30, bf16[10,128,2048]{2,1,0:T(8,128)(2,1)} %bitcast.29, bf16[3,128,2048]{2,1,0:T(8,128)(2,1)} %bitcast.31, bf16[4,128,128]{2,1,0:T(8,128)(2,1)} %broadcast_select_fusion.refs_4_), custom_call_target="tpu_custom_call" | custom-call | flops 3221225472 | bytes 11534336 | tf_op jit(solution)/shard_map/pallas_call | solution.py:124
  108.6 1.9 %copy-done.1 = f32[2,4,2,48,8,128]{5,4,3,2,1,0:T(8,128)S(1)} copy-done((f32[2,4,2,48,8,128]{5,4,3,2,1,0:T(8,128)S(1)}, f32[2,4,2,48,8,128]{5,4,3,2,1,0:T(8,128)}, u32[]{:S(2)}) %copy-start.1) | copy-done | bytes 3145752
  110.5 29.6 %shard_map.78 = (f32[48,8,128]{2,1,0:T(8,128)S(1)}, f32[16,128]{1,0:T(8,128)S(1)}) custom-call(f32[2,4,2,48,8,128]{5,4,3,2,1,0:T(8,128)S(1)} %copy-done.1, f32[16,128]{1,0:T(8,128)S(1)} %maximum_bitcast_fusion.e_ref), custom_call_target="tpu_custom_call" | custom-call | tf_op jit(solution)/shard_map/pallas_call | solution.py:249
  140.1 0.7 gather_fusion.2
  140.8 0.7 gather_fusion.3
  141.5 0.1 broadcast_select_fusion.1
  141.6 2.6 %gather_fusion.1 = bf16[48,128,128]{2,1,0:T(8,128)(2,1)S(1)} fusion(bf16[64,128,128]{2,1,0:T(8,128)(2,1)} %bitcast.32, s32[1024]{0:T(1024)} %pad_clamp_fusion), kind=kCustom, calls=%fused_computation.3 | custom fusion | bytes 3145920 | tf_op jit(solution)/shard_map/jit(_take)/gather | solution.py:345
  144.2 0.1 dynamic-slice_select_fusion
  144.3 0.0 copy-done.16
  144.3 1.2 fusion.12
  (23 shorter events, 0.1 us)
Async XLA Ops:
  0.6 20.2 %copy-start = (s32[160]{0:T(256)S(1)}, s32[160]{0:T(256)}, u32[]{:S(2)}) copy-start(s32[160]{0:T(256)} %param.12) | copy-start | bytes 1924
  2.1 23.3 %collective-permute-start = (bf16[1280,2]{0,1:T(2,128)(2,1)S(1)}, bf16[1280,2]{0,1:T(2,128)(2,1)S(1)}, u32[]{:S(2)}, u32[]{:S(2)}) collective-permute-start(bf16[1280,2]{0,1:T(2,128)(2,1)S(1)} %copy.19), channel_id=1, source_target_pairs={{0,16},{16,32},{32,48},{48,64},{64,80},{80,96},{96,112},{112,128},... | collective-permute-start | bytes 15368 | tf_op jit(solution)/shard_map/ppermute | solution.py:18
  4.0 16.1 %copy-start.11 = (f32[5,2048]{1,0:T(8,128)S(1)}, f32[5,2048]{1,0:T(8,128)}, u32[]{:S(2)}) copy-start(f32[5,2048]{1,0:T(8,128)} %param.9) | copy-start | bytes 122884
  4.0 16.2 %copy-start.12 = (s32[48,2]{0,1:T(2,128)S(1)}, s32[48,2]{0,1:T(2,128)}, u32[]{:S(2)}) copy-start(s32[48,2]{0,1:T(2,128)} %param.10) | copy-start | bytes 1156
  4.0 21.4 %collective-permute-start.1 = (bf16[1280,2]{0,1:T(2,128)(2,1)S(1)}, bf16[1280,2]{0,1:T(2,128)(2,1)S(1)}, u32[]{:S(2)}, u32[]{:S(2)}) collective-permute-start(bf16[1280,2]{0,1:T(2,128)(2,1)S(1)} %copy.20), channel_id=1, source_target_pairs={{16,0},{32,16},{48,32},{64,48},{80,64},{96,80},{112,96},{128,112},... | collective-permute-start | bytes 15368 | tf_op jit(solution)/shard_map/ppermute | solution.py:19
  9.4 52.3 %collective-permute-start.3 = (bf16[384,2048]{1,0:T(8,128)(2,1)}, bf16[384,2048]{1,0:T(8,128)(2,1)S(1)}, u32[]{:S(2)}, u32[]{:S(2)}) collective-permute-start(bf16[384,2048]{1,0:T(8,128)(2,1)} %get-tuple-element.24), channel_id=1, source_target_pairs={{0,1},{1,2},{2,3},{3,4},{4,5},{5,6},{6,7},{7,8},{8,9},{9,10},{10,1... | collective-permute-start | bytes 4718600 | tf_op jit(solution)/shard_map/ppermute | solution.py:299
  13.2 53.7 %collective-permute-start.5 = (bf16[384,2048]{1,0:T(8,128)(2,1)}, bf16[384,2048]{1,0:T(8,128)(2,1)S(1)}, u32[]{:S(2)}, u32[]{:S(2)}) collective-permute-start(bf16[384,2048]{1,0:T(8,128)(2,1)} %get-tuple-element.23), channel_id=1, source_target_pairs={{1,0},{2,1},{3,2},{4,3},{5,4},{6,5},{7,6},{8,7},{9,8},{10,9},{11,1... | collective-permute-start | bytes 4718600 | tf_op jit(solution)/shard_map/ppermute | solution.py:300
  18.8 41.3 %collective-permute-start.6 = (bf16[4,128,128]{2,1,0:T(8,128)(2,1)}, bf16[4,128,128]{2,1,0:T(8,128)(2,1)}, u32[]{:S(2)}, u32[]{:S(2)}) collective-permute-start(bf16[4,128,128]{2,1,0:T(8,128)(2,1)} %param.13), channel_id=1, source_target_pairs={{16,31},{32,46},{48,61},{64,76},{80,91},{96,106},{112,121},{128,13... | collective-permute-start | bytes 393224 | tf_op jit(solution)/shard_map/ppermute | solution.py:311
  20.2 39.1 %copy-start.2 = (f32[1,2048]{1,0:T(1,128)}, f32[1,2048]{1,0:T(1,128)S(1)}, u32[]{:S(2)}) copy-start(f32[1,2048]{1,0:T(1,128)S(1)} %get-tuple-element.28) | copy-start | bytes 24580
  20.2 39.1 %copy-start.4 = (f32[1,2048]{1,0:T(1,128)}, f32[1,2048]{1,0:T(1,128)S(1)}, u32[]{:S(2)}) copy-start(f32[1,2048]{1,0:T(1,128)S(1)} %get-tuple-element.29) | copy-start | bytes 24580
  20.2 39.1 %copy-start.6 = (f32[1,2048]{1,0:T(1,128)}, f32[1,2048]{1,0:T(1,128)S(1)}, u32[]{:S(2)}) copy-start(f32[1,2048]{1,0:T(1,128)S(1)} %get-tuple-element.30) | copy-start | bytes 24580
  20.2 39.1 %copy-start.8 = (f32[1,2048]{1,0:T(1,128)}, f32[1,2048]{1,0:T(1,128)S(1)}, u32[]{:S(2)}) copy-start(f32[1,2048]{1,0:T(1,128)S(1)} %get-tuple-element.31) | copy-start | bytes 24580
  25.4 33.9 %collective-permute-start.2 = (bf16[384,4]{0,1:T(4,128)(2,1)S(1)}, bf16[384,4]{0,1:T(4,128)(2,1)S(1)}, u32[]{:S(2)}, u32[]{:S(2)}) collective-permute-start(bf16[384,4]{0,1:T(4,128)(2,1)S(1)} %get-tuple-element.33), channel_id=1, source_target_pairs={{0,1},{1,2},{2,3},{3,4},{4,5},{5,6},{6,7},{7,8},{8,9},{9,10},{10,1... | collective-permute-start | bytes 9224 | tf_op jit(solution)/shard_map/ppermute | solution.py:317
  27.3 32.3 %collective-permute-start.4 = (bf16[384,4]{0,1:T(4,128)(2,1)S(1)}, bf16[384,4]{0,1:T(4,128)(2,1)S(1)}, u32[]{:S(2)}, u32[]{:S(2)}) collective-permute-start(bf16[384,4]{0,1:T(4,128)(2,1)S(1)} %get-tuple-element.32), channel_id=1, source_target_pairs={{1,0},{2,1},{3,2},{4,3},{5,4},{6,5},{7,6},{8,7},{9,8},{10,9},{11,1... | collective-permute-start | bytes 9224 | tf_op jit(solution)/shard_map/ppermute | solution.py:318
  60.0 6.8 %copy-start.3 = (f32[1,2048]{1,0:T(1,128)S(1)}, f32[1,2048]{1,0:T(1,128)}, u32[]{:S(2)}) copy-start(f32[1,2048]{1,0:T(1,128)} %copy-done.2) | copy-start | bytes 24580
  60.1 6.8 %copy-start.5 = (f32[1,2048]{1,0:T(1,128)S(1)}, f32[1,2048]{1,0:T(1,128)}, u32[]{:S(2)}) copy-start(f32[1,2048]{1,0:T(1,128)} %copy-done.4) | copy-start | bytes 24580
  60.1 6.8 %copy-start.7 = (f32[1,2048]{1,0:T(1,128)S(1)}, f32[1,2048]{1,0:T(1,128)}, u32[]{:S(2)}) copy-start(f32[1,2048]{1,0:T(1,128)} %copy-done.6) | copy-start | bytes 24580
  60.1 6.8 %copy-start.9 = (f32[1,2048]{1,0:T(1,128)S(1)}, f32[1,2048]{1,0:T(1,128)}, u32[]{:S(2)}) copy-start(f32[1,2048]{1,0:T(1,128)} %copy-done.8) | copy-start | bytes 24580
  61.7 9.7 %copy-start.10 = (f32[1280]{0:T(1024)S(1)}, f32[1280]{0:T(1024)}, u32[]{:S(2)}) copy-start(f32[1280]{0:T(1024)} %get-tuple-element.17) | copy-start | bytes 15364
  108.6 32.9 %copy-start.14 = (pred[48]{0:T(512)(128)(4,1)S(1)}, pred[48]{0:T(512)(128)(4,1)}, u32[]{:S(2)}) copy-start(pred[48]{0:T(512)(128)(4,1)} %get-tuple-element.38) | copy-start | bytes 148
  108.6 1.9 %copy-start.1 = (f32[2,4,2,48,8,128]{5,4,3,2,1,0:T(8,128)S(1)}, f32[2,4,2,48,8,128]{5,4,3,2,1,0:T(8,128)}, u32[]{:S(2)}) copy-start(f32[2,4,2,48,8,128]{5,4,3,2,1,0:T(8,128)} %get-tuple-element.7.g_ref) | copy-start | bytes 9437188
  110.5 33.7 %copy-start.13 = (pred[48]{0:T(512)(128)(4,1)S(1)}, pred[48]{0:T(512)(128)(4,1)}, u32[]{:S(2)}) copy-start(pred[48]{0:T(512)(128)(4,1)} %get-tuple-element.11) | copy-start | bytes 148
  110.5 33.8 %copy-start.15 = (pred[48]{0:T(512)(128)(4,1)S(1)}, pred[48]{0:T(512)(128)(4,1)}, u32[]{:S(2)}) copy-start(pred[48]{0:T(512)(128)(4,1)} %get-tuple-element.21) | copy-start | bytes 148
  110.5 33.8 %copy-start.16 = (pred[48]{0:T(512)(128)(4,1)S(1)}, pred[48]{0:T(512)(128)(4,1)}, u32[]{:S(2)}) copy-start(pred[48]{0:T(512)(128)(4,1)} %iota_compare_fusion) | copy-start | bytes 148

commit v15 on v14

--- a/solution.py
+++ b/solution.py
@@ -172,18 +172,22 @@
             device_id={"pix": peer}, device_id_type=MESH,
         )
 
-    order = [(x + 3) % 4, (x + 1) % 4, (x + 2) % 4, x]
+    order = [
+        ((x + 3) % 4, 0), ((x + 1) % 4, 1), ((x + 2) % 4, 0), ((x + 2) % 4, 1),
+        ((x + 1) % 4, 0), ((x + 3) % 4, 1), (x, 0), (x, 1),
+    ]
     stage1 = []
-    for n, j in enumerate(order):
-        cp = remote(g_ref.at[1 - c, j], r1.at[j], 12 + n if n else 0, partner)
+    for n, (j, h) in enumerate(order):
+        cp = remote(g_ref.at[1 - c, j, h], r1.at[j, h], 12 + n if n else 0, partner)
         cp.start()
         stage1.append(cp)
     ce1 = remote(e_ref, ebuf.at[0], 1, partner)
     ce1.start()
 
     def settle(n):
+        j, h = order[n]
         stage1[n].wait()
-        s1[order[n]] = g_ref[c, order[n]] + r1[order[n]]
+        s1[j, h] = g_ref[c, j, h] + r1[j, h]
 
     settle(0)
     settle(1)
@@ -198,8 +202,8 @@
         if k == 0:
             src_r, src_l = s1.at[jr, 0], s1.at[jl, 1]
         else:
-            if k == 1:
-                settle(2)
+            settle(2 * k)
+            settle(2 * k + 1)
             cr.wait_recv()
             cl.wait_recv()
             acc_r[k] = s1[jr, 0] + recv_r[k - 1]
@@ -221,7 +225,8 @@
             ef = remote(ebuf.at[2], ebuf.at[4], 10, right)
             ef.start()
             done.append(ef)
-    settle(3)
+    settle(6)
+    settle(7)
     cr.wait_recv()
     cl.wait_recv()
     tbuf[0] = s1[x, 0] + recv_r[2]
@@ -264,8 +269,8 @@
             pltpu.VMEM((2,) + part, f32),
             pltpu.VMEM(part, f32),
             pltpu.VMEM((7,) + energy_part.shape, f32),
-            pltpu.SemaphoreType.DMA((16,)),
-            pltpu.SemaphoreType.DMA((16,)),
+            pltpu.SemaphoreType.DMA((20,)),
+            pltpu.SemaphoreType.DMA((20,)),
         ],
         compiler_params=pltpu.CompilerParams(
             collective_id=0, has_side_effects=True, vmem_limit_bytes=48 * 1024 * 1024

time: 146 us -> 146 us (level)
  no operation moved by 1% of the time
where the time goes in v15:
time: 146 us
  Pallas kernels  66.8 us (46%)
  other arithmetic  37.6 us (26%)
  starting transfers between devices  23.4 us (16%)
  local copies, waits for them, and re-layouts  14.9 us (10%)
  between operations  1.61 us (1%)
    pallas_call x1, Pallas kernels, pair_grams(): pl.pallas_call(lambda *refs: gram_kernel(shares, *refs), out_shape=(jax.S...  37.2 us
    reduce_sum x3, other arithmetic, row_squares(): return jnp.sum(values * values, axis=1)  32.9 us
    pallas_call x1, Pallas kernels, scatter_grams(): pl.pallas_call(scatter_kernel, out_shape=(jax.ShapeDtypeStruct(part, f32)...  29.7 us
    ppermute x1, starting transfers between devices, on_device(): edge_after = lax.ppermute(edges[:width], 'ion', down)  7.54 us
    ppermute x1, starting transfers between devices, on_device(): raw_after = lax.ppermute(images[:width], 'ion', down)  5.63 us
    slice x1, local copies, waits for them, and re-layouts, on_device(): raw_after = lax.ppermute(images[:width], 'ion', down)  3.93 us
    ppermute x1, starting transfers between devices, on_device(): raw_before = lax.ppermute(images[local_rows - width:], 'ion', up)  3.81 us
  transfers between devices with their start and end apart: 7, of which 0 were waited for; matrix products, arithmetic and copies ran while one was open for 28% of the time, Pallas kernels for 0%

profile of v15, /device:TPU:16, one launch (start us, length us, event | category | flops | bytes accessed | tf_op | source)
XLA Modules:
  0.0 145.6 jit_solution(15654257986208652868)
XLA Ops:
  0.6 0.0 copy-start
  0.6 1.2 fusion.30
  1.9 0.2 copy.19
  2.1 1.7 %collective-permute-start = (bf16[1280,2]{0,1:T(2,128)(2,1)S(1)}, bf16[1280,2]{0,1:T(2,128)(2,1)S(1)}, u32[]{:S(2)}, u32[]{:S(2)}) collective-permute-start(bf16[1280,2]{0,1:T(2,128)(2,1)S(1)} %copy.19), channel_id=1, source_target_pairs={{0,16},{16,32},{32,48},{48,64},{64,80},{80,96},{96,112},{112,128},... | collective-permute-start | bytes 15368 | tf_op jit(solution)/shard_map/ppermute | solution.py:18
  3.8 0.2 copy.20
  4.0 1.4 collective-permute-start.1
  5.4 3.9 %fusion.29 = (bf16[384,2048]{1,0:T(8,128)(2,1)}, bf16[384,2048]{1,0:T(8,128)(2,1)}) fusion(bf16[1280,2048]{1,0:T(8,128)(2,1)} %param.8), kind=kLoop, calls=%fused_computation.94 | loop fusion | bytes 6291456 | tf_op jit(solution)/shard_map/slice | solution.py:305
  9.4 3.8 %collective-permute-start.3 = (bf16[384,2048]{1,0:T(8,128)(2,1)}, bf16[384,2048]{1,0:T(8,128)(2,1)S(1)}, u32[]{:S(2)}, u32[]{:S(2)}) collective-permute-start(bf16[384,2048]{1,0:T(8,128)(2,1)} %get-tuple-element.24), channel_id=1, source_target_pairs={{0,1},{1,2},{2,3},{3,4},{4,5},{5,6},{6,7},{7,8},{8,9},{9,10},{10,1... | collective-permute-start | bytes 4718600 | tf_op jit(solution)/shard_map/ppermute | solution.py:304
  13.2 5.6 %collective-permute-start.5 = (bf16[384,2048]{1,0:T(8,128)(2,1)}, bf16[384,2048]{1,0:T(8,128)(2,1)S(1)}, u32[]{:S(2)}, u32[]{:S(2)}) collective-permute-start(bf16[384,2048]{1,0:T(8,128)(2,1)} %get-tuple-element.23), channel_id=1, source_target_pairs={{1,0},{2,1},{3,2},{4,3},{5,4},{6,5},{7,6},{8,7},{9,8},{10,9},{11,1... | collective-permute-start | bytes 4718600 | tf_op jit(solution)/shard_map/ppermute | solution.py:305
  18.8 1.3 collective-permute-start.6
  20.1 0.0 copy-done.11
  20.2 0.0 copy-start.2
  20.2 0.0 copy-start.4
  20.2 0.0 copy-start.6
  20.2 0.0 copy-start.8
  20.2 0.0 copy-done.12
  20.2 0.6 compare_and_fusion.1
  20.8 0.0 copy-done
  20.8 0.8 gather_fusion
  21.6 0.6 and_bitcast_fusion
  22.2 0.6 pad_clamp_fusion
  23.4 0.6 pad_clamp_fusion.2
  24.0 0.6 iota_compare_fusion
  24.6 0.1 copy.14
  24.7 0.7 reshape.45.refs_0_
  25.4 0.0 collective-permute-done
  25.4 0.0 collective-permute-done.1
  25.4 1.9 %collective-permute-start.2 = (bf16[384,4]{0,1:T(4,128)(2,1)S(1)}, bf16[384,4]{0,1:T(4,128)(2,1)S(1)}, u32[]{:S(2)}, u32[]{:S(2)}) collective-permute-start(bf16[384,4]{0,1:T(4,128)(2,1)S(1)} %get-tuple-element.33), channel_id=1, source_target_pairs={{0,1},{1,2},{2,3},{3,4},{4,5},{5,6},{6,7},{7,8},{8,9},{9,10},{10,1... | collective-permute-start | bytes 9224 | tf_op jit(solution)/shard_map/ppermute | solution.py:322
  27.3 7.5 %collective-permute-start.4 = (bf16[384,4]{0,1:T(4,128)(2,1)S(1)}, bf16[384,4]{0,1:T(4,128)(2,1)S(1)}, u32[]{:S(2)}, u32[]{:S(2)}) collective-permute-start(bf16[384,4]{0,1:T(4,128)(2,1)S(1)} %get-tuple-element.32), channel_id=1, source_target_pairs={{1,0},{2,1},{3,2},{4,3},{5,4},{6,5},{7,6},{8,7},{9,8},{10,9},{11,1... | collective-permute-start | bytes 9224 | tf_op jit(solution)/shard_map/ppermute | solution.py:323
  34.9 0.2 copy.11
  35.1 0.9 copy.13
  36.0 23.2 %multiply_reduce_fusion = (f32[1280]{0:T(1024)}, bf16[1280,2048]{1,0:T(8,128)(2,1)}) fusion(bf16[1280,2]{1,0:T(8,128)(2,1)} %copy.13, bf16[1280,2048]{1,0:T(8,128)(2,1)} %param.8, f32[2048]{0:T(1024)S(1)} %bitcast.42, f32[2048]{0:T(1024)S(1)} %bitcast.45, f32[2048]{0:T(1024)S(1)} %bitcast.36, bf16[1280,2]{1,0:T(8,128)(2,1)S(1)} %copy.11, ...), kind=kLoop, calls=%fused_computation.4 | loop fusion | flops 78641920 | bytes 10542080 | tf_op jit(solution)/shard_map/reduce_sum | solution.py:291
  59.2 0.0 copy-done.2
  59.2 0.0 copy-done.4
  59.3 0.0 copy-done.6
  59.3 0.0 copy-done.8
  59.3 0.0 collective-permute-done.2
  59.3 0.2 copy.15
  59.5 0.2 copy.16
  59.7 0.0 collective-permute-done.4
  59.7 0.2 copy.17
  59.9 0.2 copy.18
  60.1 0.0 copy-start.5
  60.1 0.0 copy-start.7
  60.1 0.0 collective-permute-done.6
  60.1 1.6 %broadcast_select_fusion.refs_4_ = bf16[4,128,128]{2,1,0:T(8,128)(2,1)} fusion(bf16[4,128,128]{2,1,0:T(8,128)(2,1)} %param.13, bf16[4,128,128]{2,1,0:T(8,128)(2,1)} %collective-permute-done.6, pred[]{:T(512)S(6)} %eq.8), kind=kLoop, calls=%fused_computation.41 | loop fusion | flops 65536 | bytes 393217 | tf_op jit(solution)/shard_map/jit(_where)/select_n | solution.py:317
  61.7 0.0 collective-permute-done.3
  61.7 5.2 %multiply_reduce_fusion.2 = (f32[384]{0:T(512)S(1)}, bf16[384,2048]{1,0:T(8,128)(2,1)}) fusion(bf16[384,2]{1,0:T(8,128)(2,1)S(1)} %copy.16, bf16[384,2048]{1,0:T(8,128)(2,1)S(1)} %collective-permute-done.3, f32[2048]{0:T(1024)} %bitcast.43, f32[2048]{0:T(1024)} %bitcast.46, f32[2048]{0:T(1024)} %bitcast.37, bf16[384,2]{1,0:T(8,128)(2,1)S(1)} %copy.15, ...), kind=kLoop, calls=%fused_computation.15 | loop fusion | flops 23592576 | bytes 3191296 | tf_op jit(solution)/shard_map/reduce_sum | solution.py:291
  66.9 0.0 collective-permute-done.5
  66.9 0.0 copy-done.3
  66.9 0.0 copy-done.5
  66.9 0.0 copy-done.7
  66.9 0.0 copy-done.9
  66.9 4.5 %multiply_reduce_fusion.1 = (f32[384]{0:T(512)S(1)}, bf16[384,2048]{1,0:T(8,128)(2,1)}) fusion(bf16[384,2]{1,0:T(8,128)(2,1)S(1)} %copy.18, bf16[384,2048]{1,0:T(8,128)(2,1)S(1)} %collective-permute-done.5, f32[2048]{0:T(1024)S(1)} %bitcast.44, f32[2048]{0:T(1024)S(1)} %bitcast.47, f32[2048]{0:T(1024)S(1)} %bitcast.38, bf16[384,2]{1,0:T(8,128)(2,1)S(1)} %copy.17, ...), kind=kLoop, calls=%fused_computation.14 | loop fusion | flops 23592576 | bytes 3191296 | tf_op jit(solution)/shard_map/reduce_sum | solution.py:291
  71.4 37.2 %shard_map.77 = (f32[2,4,2,48,8,128]{5,4,3,2,1,0:T(8,128)}, bf16[16,4,128,128]{3,2,1,0:T(8,128)(2,1)}) custom-call(s32[96]{0:T(128)} %reshape.45.refs_0_, bf16[3,128,2048]{2,1,0:T(8,128)(2,1)} %bitcast.30, bf16[10,128,2048]{2,1,0:T(8,128)(2,1)} %bitcast.29, bf16[3,128,2048]{2,1,0:T(8,128)(2,1)} %bitcast.31, bf16[4,128,128]{2,1,0:T(8,128)(2,1)} %broadcast_select_fusion.refs_4_), custom_call_target="tpu_custom_call" | custom-call | flops 3221225472 | bytes 11534336 | tf_op jit(solution)/shard_map/pallas_call | solution.py:124
  108.6 1.9 %copy-done.1 = f32[2,4,2,48,8,128]{5,4,3,2,1,0:T(8,128)S(1)} copy-done((f32[2,4,2,48,8,128]{5,4,3,2,1,0:T(8,128)S(1)}, f32[2,4,2,48,8,128]{5,4,3,2,1,0:T(8,128)}, u32[]{:S(2)}) %copy-start.1) | copy-done | bytes 3145752
  110.5 29.7 %shard_map.78 = (f32[48,8,128]{2,1,0:T(8,128)S(1)}, f32[16,128]{1,0:T(8,128)S(1)}) custom-call(f32[2,4,2,48,8,128]{5,4,3,2,1,0:T(8,128)S(1)} %copy-done.1, f32[16,128]{1,0:T(8,128)S(1)} %maximum_bitcast_fusion.e_ref), custom_call_target="tpu_custom_call" | custom-call | tf_op jit(solution)/shard_map/pallas_call | solution.py:254
  140.2 0.7 gather_fusion.2
  140.9 0.7 gather_fusion.3
  141.6 0.1 broadcast_select_fusion.1
  141.7 2.6 %gather_fusion.1 = bf16[48,128,128]{2,1,0:T(8,128)(2,1)S(1)} fusion(bf16[64,128,128]{2,1,0:T(8,128)(2,1)} %bitcast.32, s32[1024]{0:T(1024)} %pad_clamp_fusion), kind=kCustom, calls=%fused_computation.3 | custom fusion | bytes 3145920 | tf_op jit(solution)/shard_map/jit(_take)/gather | solution.py:350
  144.3 0.1 dynamic-slice_select_fusion
  144.4 0.0 copy-done.16
  144.4 1.2 fusion.12
  (23 shorter events, 0.1 us)
Async XLA Ops:
  0.6 20.2 %copy-start = (s32[160]{0:T(256)S(1)}, s32[160]{0:T(256)}, u32[]{:S(2)}) copy-start(s32[160]{0:T(256)} %param.12) | copy-start | bytes 1924
  2.1 23.3 %collective-permute-start = (bf16[1280,2]{0,1:T(2,128)(2,1)S(1)}, bf16[1280,2]{0,1:T(2,128)(2,1)S(1)}, u32[]{:S(2)}, u32[]{:S(2)}) collective-permute-start(bf16[1280,2]{0,1:T(2,128)(2,1)S(1)} %copy.19), channel_id=1, source_target_pairs={{0,16},{16,32},{32,48},{48,64},{64,80},{80,96},{96,112},{112,128},... | collective-permute-start | bytes 15368 | tf_op jit(solution)/shard_map/ppermute | solution.py:18
  4.0 16.1 %copy-start.11 = (f32[5,2048]{1,0:T(8,128)S(1)}, f32[5,2048]{1,0:T(8,128)}, u32[]{:S(2)}) copy-start(f32[5,2048]{1,0:T(8,128)} %param.9) | copy-start | bytes 122884
  4.0 16.2 %copy-start.12 = (s32[48,2]{0,1:T(2,128)S(1)}, s32[48,2]{0,1:T(2,128)}, u32[]{:S(2)}) copy-start(s32[48,2]{0,1:T(2,128)} %param.10) | copy-start | bytes 1156
  4.0 21.4 %collective-permute-start.1 = (bf16[1280,2]{0,1:T(2,128)(2,1)S(1)}, bf16[1280,2]{0,1:T(2,128)(2,1)S(1)}, u32[]{:S(2)}, u32[]{:S(2)}) collective-permute-start(bf16[1280,2]{0,1:T(2,128)(2,1)S(1)} %copy.20), channel_id=1, source_target_pairs={{16,0},{32,16},{48,32},{64,48},{80,64},{96,80},{112,96},{128,112},... | collective-permute-start | bytes 15368 | tf_op jit(solution)/shard_map/ppermute | solution.py:19
  9.4 52.3 %collective-permute-start.3 = (bf16[384,2048]{1,0:T(8,128)(2,1)}, bf16[384,2048]{1,0:T(8,128)(2,1)S(1)}, u32[]{:S(2)}, u32[]{:S(2)}) collective-permute-start(bf16[384,2048]{1,0:T(8,128)(2,1)} %get-tuple-element.24), channel_id=1, source_target_pairs={{0,1},{1,2},{2,3},{3,4},{4,5},{5,6},{6,7},{7,8},{8,9},{9,10},{10,1... | collective-permute-start | bytes 4718600 | tf_op jit(solution)/shard_map/ppermute | solution.py:304
  13.2 53.7 %collective-permute-start.5 = (bf16[384,2048]{1,0:T(8,128)(2,1)}, bf16[384,2048]{1,0:T(8,128)(2,1)S(1)}, u32[]{:S(2)}, u32[]{:S(2)}) collective-permute-start(bf16[384,2048]{1,0:T(8,128)(2,1)} %get-tuple-element.23), channel_id=1, source_target_pairs={{1,0},{2,1},{3,2},{4,3},{5,4},{6,5},{7,6},{8,7},{9,8},{10,9},{11,1... | collective-permute-start | bytes 4718600 | tf_op jit(solution)/shard_map/ppermute | solution.py:305
  18.8 41.3 %collective-permute-start.6 = (bf16[4,128,128]{2,1,0:T(8,128)(2,1)}, bf16[4,128,128]{2,1,0:T(8,128)(2,1)}, u32[]{:S(2)}, u32[]{:S(2)}) collective-permute-start(bf16[4,128,128]{2,1,0:T(8,128)(2,1)} %param.13), channel_id=1, source_target_pairs={{16,31},{32,46},{48,61},{64,76},{80,91},{96,106},{112,121},{128,13... | collective-permute-start | bytes 393224 | tf_op jit(solution)/shard_map/ppermute | solution.py:316
  20.2 39.1 %copy-start.2 = (f32[1,2048]{1,0:T(1,128)}, f32[1,2048]{1,0:T(1,128)S(1)}, u32[]{:S(2)}) copy-start(f32[1,2048]{1,0:T(1,128)S(1)} %get-tuple-element.28) | copy-start | bytes 24580
  20.2 39.1 %copy-start.4 = (f32[1,2048]{1,0:T(1,128)}, f32[1,2048]{1,0:T(1,128)S(1)}, u32[]{:S(2)}) copy-start(f32[1,2048]{1,0:T(1,128)S(1)} %get-tuple-element.29) | copy-start | bytes 24580
  20.2 39.1 %copy-start.6 = (f32[1,2048]{1,0:T(1,128)}, f32[1,2048]{1,0:T(1,128)S(1)}, u32[]{:S(2)}) copy-start(f32[1,2048]{1,0:T(1,128)S(1)} %get-tuple-element.30) | copy-start | bytes 24580
  20.2 39.1 %copy-start.8 = (f32[1,2048]{1,0:T(1,128)}, f32[1,2048]{1,0:T(1,128)S(1)}, u32[]{:S(2)}) copy-start(f32[1,2048]{1,0:T(1,128)S(1)} %get-tuple-element.31) | copy-start | bytes 24580
  25.4 33.9 %collective-permute-start.2 = (bf16[384,4]{0,1:T(4,128)(2,1)S(1)}, bf16[384,4]{0,1:T(4,128)(2,1)S(1)}, u32[]{:S(2)}, u32[]{:S(2)}) collective-permute-start(bf16[384,4]{0,1:T(4,128)(2,1)S(1)} %get-tuple-element.33), channel_id=1, source_target_pairs={{0,1},{1,2},{2,3},{3,4},{4,5},{5,6},{6,7},{7,8},{8,9},{9,10},{10,1... | collective-permute-start | bytes 9224 | tf_op jit(solution)/shard_map/ppermute | solution.py:322
  27.3 32.3 %collective-permute-start.4 = (bf16[384,4]{0,1:T(4,128)(2,1)S(1)}, bf16[384,4]{0,1:T(4,128)(2,1)S(1)}, u32[]{:S(2)}, u32[]{:S(2)}) collective-permute-start(bf16[384,4]{0,1:T(4,128)(2,1)S(1)} %get-tuple-element.32), channel_id=1, source_target_pairs={{1,0},{2,1},{3,2},{4,3},{5,4},{6,5},{7,6},{8,7},{9,8},{10,9},{11,1... | collective-permute-start | bytes 9224 | tf_op jit(solution)/shard_map/ppermute | solution.py:323
  60.0 6.8 %copy-start.3 = (f32[1,2048]{1,0:T(1,128)S(1)}, f32[1,2048]{1,0:T(1,128)}, u32[]{:S(2)}) copy-start(f32[1,2048]{1,0:T(1,128)} %copy-done.2) | copy-start | bytes 24580
  60.1 6.8 %copy-start.5 = (f32[1,2048]{1,0:T(1,128)S(1)}, f32[1,2048]{1,0:T(1,128)}, u32[]{:S(2)}) copy-start(f32[1,2048]{1,0:T(1,128)} %copy-done.4) | copy-start | bytes 24580
  60.1 6.8 %copy-start.7 = (f32[1,2048]{1,0:T(1,128)S(1)}, f32[1,2048]{1,0:T(1,128)}, u32[]{:S(2)}) copy-start(f32[1,2048]{1,0:T(1,128)} %copy-done.6) | copy-start | bytes 24580
  60.1 6.8 %copy-start.9 = (f32[1,2048]{1,0:T(1,128)S(1)}, f32[1,2048]{1,0:T(1,128)}, u32[]{:S(2)}) copy-start(f32[1,2048]{1,0:T(1,128)} %copy-done.8) | copy-start | bytes 24580
  61.7 9.7 %copy-start.10 = (f32[1280]{0:T(1024)S(1)}, f32[1280]{0:T(1024)}, u32[]{:S(2)}) copy-start(f32[1280]{0:T(1024)} %get-tuple-element.17) | copy-start | bytes 15364
  108.6 33.0 %copy-start.14 = (pred[48]{0:T(512)(128)(4,1)S(1)}, pred[48]{0:T(512)(128)(4,1)}, u32[]{:S(2)}) copy-start(pred[48]{0:T(512)(128)(4,1)} %get-tuple-element.38) | copy-start | bytes 148
  108.6 1.9 %copy-start.1 = (f32[2,4,2,48,8,128]{5,4,3,2,1,0:T(8,128)S(1)}, f32[2,4,2,48,8,128]{5,4,3,2,1,0:T(8,128)}, u32[]{:S(2)}) copy-start(f32[2,4,2,48,8,128]{5,4,3,2,1,0:T(8,128)} %get-tuple-element.7.g_ref) | copy-start | bytes 9437188
  110.5 33.7 %copy-start.13 = (pred[48]{0:T(512)(128)(4,1)S(1)}, pred[48]{0:T(512)(128)(4,1)}, u32[]{:S(2)}) copy-start(pred[48]{0:T(512)(128)(4,1)} %get-tuple-element.11) | copy-start | bytes 148
  110.5 33.8 %copy-start.15 = (pred[48]{0:T(512)(128)(4,1)S(1)}, pred[48]{0:T(512)(128)(4,1)}, u32[]{:S(2)}) copy-start(pred[48]{0:T(512)(128)(4,1)} %get-tuple-element.21) | copy-start | bytes 148
  110.5 33.8 %copy-start.16 = (pred[48]{0:T(512)(128)(4,1)S(1)}, pred[48]{0:T(512)(128)(4,1)}, u32[]{:S(2)}) copy-start(pred[48]{0:T(512)(128)(4,1)} %iota_compare_fusion) | copy-start | bytes 148
